TPU v7x, 128 devices: a whole 4x4x4 slice. The times are simulated.
128 devices in a mesh: depth: 16 (over z_hi, y, core), lat: 8 (over x, z_lo).
Axes of the slice: x: 4, y: 4, z: 4 (z_hi: 2, z_lo: 2; z = z_hi * 2 + z_lo), core: 2. Of those that a mesh axis runs over, the one named last changes fastest.
Arguments:
- rhs_field: float32 [2, 32, 8, 8192], P(None, 'depth', None, 'lat'), may hold values from -4 to 4
- src_cell: int32 [8], replicated, may hold values from 0 to 8191
- src_layer: int32 [8], replicated, may hold values from 0 to 31
- factor: float32 [32, 64, 3, 2, 128, 128], P('depth', 'lat'), as said below
- couple: float32 [2, 2, 32, 8192], P(None, None, 'depth', 'lat')
Outputs:
- waves: float32 [2, 32, 8, 8192], P(None, 'depth', None, 'lat')
- field: float32 [2, 32, 8, 8192], P(None, 'depth', None, 'lat')
Inputs may be any that keep to these rules, and one draw needn't show every extreme that they name: The centre block of every factor is a complex diagonal of modulus 0.92 plus independent entries; the others are independent entries.
All inputs are finite; a program needn't handle non-finite values.
Results may differ from a plain program's by a relative error of at most 0.0003.
Values sent between devices are 32-bit elements; how exact they have to be, the bound alone decides.
No kernel may reach another device: no remote copies, remote signals or barrier semaphores. Data moves between devices by JAX's collectives and lax.ppermute only.
A program may use at most 128 MiB of HBM per device.

v0:
```python
import jax
import jax.numpy as jnp
from jax import lax
from jax.sharding import PartitionSpec as P


def extended(block, sides, width):
    for axis, dim in sides:
        count = lax.axis_size(axis)
        forward = [(i, i + 1) for i in range(count - 1)]
        backward = [(target, source) for source, target in forward]
        low = lax.ppermute(
            lax.slice_in_dim(block, block.shape[dim] - width, None, axis=dim), axis, forward
        )
        high = lax.ppermute(lax.slice_in_dim(block, 0, width, axis=dim), axis, backward)
        block = jnp.concatenate([low, block, high], axis=dim)
    return block


def from_behind(value, axis, steps):
    count = lax.axis_size(axis)
    leading, last = (max(0, -steps), min(count, count - steps))
    return lax.ppermute(value, axis, [(source, source + steps) for source in range(leading, last)])


def complex_scale(coef, vector):
    real_part = coef[0][None, :] * vector[0] - coef[1][None, :] * vector[1]
    imag_part = coef[0][None, :] * vector[1] + coef[1][None, :] * vector[0]
    return jnp.stack([real_part, imag_part])


def block_product(padded, blocks, strip_cells):
    tile_cells = blocks.shape[-1]
    tile_count = strip_cells // tile_cells
    shot_count = padded.shape[1]
    shifted = jnp.stack(
        [
            padded[:, :, offset * tile_cells : offset * tile_cells + strip_cells].reshape(
                2, shot_count, tile_count, tile_cells
            )
            for offset in range(3)
        ],
        axis=3,
    )
    form = "stjp,tjpq->stq"
    high = lax.Precision.HIGHEST
    real_out = jnp.einsum(form, shifted[0], blocks[:, :, 0], precision=high) - jnp.einsum(
        form, shifted[1], blocks[:, :, 1], precision=high
    )
    imag_out = jnp.einsum(form, shifted[0], blocks[:, :, 1], precision=high) + jnp.einsum(
        form, shifted[1], blocks[:, :, 0], precision=high
    )
    return jnp.stack([real_out, imag_out]).reshape(2, shot_count, strip_cells)


def apply_blocks(vector, blocks):
    tile_cells = blocks.shape[-1]
    padded = extended(vector, (("lat", 2),), tile_cells)
    return block_product(padded, blocks, vector.shape[-1])


def descend(batch_forcing, incoming, factor, couple_down, applier):
    carried = incoming
    wave_list = []
    for layer_num in range(batch_forcing.shape[1]):
        source = batch_forcing[:, layer_num] + complex_scale(couple_down[:, layer_num], carried)
        carried = applier(source, factor[layer_num])
        wave_list.append(carried)
    return (jnp.stack(wave_list, axis=1), carried)


def ascend(batch_waves, incoming, factor, couple_up, applier):
    carried = incoming
    layer_total = batch_waves.shape[1]
    field_list = [None] * layer_total
    for layer_num in reversed(range(layer_total)):
        carried = batch_waves[:, layer_num] + applier(
            complex_scale(couple_up[:, layer_num], carried), factor[layer_num]
        )
        field_list[layer_num] = carried
    return (jnp.stack(field_list, axis=1), carried)


def shards(rhs_field, src_cell, src_layer, factor, couple):
    layer_total = rhs_field.shape[1]
    shot_count = rhs_field.shape[2]
    strip_cells = rhs_field.shape[3]
    depth_pos = lax.axis_index("depth")
    lat_pos = lax.axis_index("lat")
    depth_count = lax.axis_size("depth")
    layer_ids = depth_pos * layer_total + jnp.arange(layer_total, dtype=jnp.int32)
    cell_ids = lat_pos * strip_cells + jnp.arange(strip_cells, dtype=jnp.int32)
    hit = (src_layer[None, :, None] == layer_ids[:, None, None]) & (
        src_cell[None, :, None] == cell_ids[None, None, :]
    )
    real_part = rhs_field[0] + 4.0 * hit.astype(jnp.float32)
    forcing = jnp.stack([real_part, rhs_field[1]])
    down_use = couple[0]
    up_use = couple[1]
    batch_count = 1
    batch_rows = shot_count // batch_count
    start_state = jnp.zeros((2, batch_rows, strip_cells), jnp.float32)
    segment_total = depth_count + batch_count - 1

    def down_segment(segment_num, carry):
        incoming, result = carry
        batch_num = segment_num - depth_pos
        active_flag = (batch_num >= 0) & (batch_num < batch_count)
        offset_rows = jnp.clip(batch_num, 0, batch_count - 1) * batch_rows
        wave_part, deepest = descend(forcing, incoming, factor, down_use, apply_blocks)
        updated = lax.dynamic_update_slice_in_dim(result, wave_part, offset_rows, 2)
        result = jnp.where(active_flag, updated, result)
        outgoing = from_behind(deepest, "depth", 1)
        return (outgoing, result)

    _, waves = lax.fori_loop(0, segment_total, down_segment, (start_state, jnp.zeros_like(forcing)))

    def up_segment(segment_num, carry):
        incoming, result = carry
        batch_num = segment_num - (depth_count - 1 - depth_pos)
        active_flag = (batch_num >= 0) & (batch_num < batch_count)
        offset_rows = jnp.clip(batch_num, 0, batch_count - 1) * batch_rows
        field_part, shallowest = ascend(waves, incoming, factor, up_use, apply_blocks)
        updated = lax.dynamic_update_slice_in_dim(result, field_part, offset_rows, 2)
        result = jnp.where(active_flag, updated, result)
        outgoing = from_behind(shallowest, "depth", -1)
        return (outgoing, result)

    _, field = lax.fori_loop(0, segment_total, up_segment, (start_state, jnp.zeros_like(forcing)))
    return (waves, field)


def solution(mesh):
    placed = (
        P(None, "depth", None, "lat"),
        P(),
        P(),
        P("depth", "lat", None, None, None, None),
        P(None, None, "depth", "lat"),
    )
    return jax.shard_map(
        shards,
        mesh=mesh,
        in_specs=placed,
        out_specs=(P(None, "depth", None, "lat"), P(None, "depth", None, "lat")),
        check_vma=False,
    )
```

profile of v0, /device:TPU:25, one launch (start us, length us, event | category | flops | bytes accessed | tf_op | source)
XLA Modules:
  0.0 1230.0 jit_solution(9344150849959360287)
XLA Ops:
  10.7 629.2 %while.34 = (s32[]{:T(128)}, f32[2,8,1024]{2,1,0:T(8,128)S(1)}, f32[2,2,8,1024]{3,2,1,0:T(8,128)S(1)}, f32[2,2,8,1024]{3,2,0,1:T(8,128)S(1)}, f32[2,2,1024]{2,1,...) while((s32[]{:T(128)}, f32[2,8,1024]{2,1,0:T(8,128)S(1)}, ...), condition=%wide.region_1.2_spmd.clone, body=%wide.region_0.1_spmd.clone.sunk | while | flops 302743552 | bytes 48751040 | solution.py:116
  39.4 7.4 collective-permute-start.4
  76.9 10.5 collective-permute-start.4
  116.5 10.2 collective-permute-start.4
  156.5 10.5 collective-permute-start.4
  195.7 10.4 collective-permute-start.4
  235.6 10.5 collective-permute-start.4
  275.3 10.5 collective-permute-start.4
  314.4 10.5 collective-permute-start.4
  353.6 10.5 collective-permute-start.4
  392.8 10.5 collective-permute-start.4
  432.0 10.5 collective-permute-start.4
  471.2 10.5 collective-permute-start.4
  510.5 10.5 collective-permute-start.4
  549.7 10.5 collective-permute-start.4
  589.0 10.5 collective-permute-start.4
  628.2 10.5 collective-permute-start.4
  640.6 588.7 %while.35 = (s32[]{:T(128)}, f32[2,8,1024]{2,1,0:T(8,128)}, f32[2,2,8,1024]{3,2,1,0:T(8,128)S(1)}, f32[2,2,8,1024]{3,2,1,0:T(8,128)S(1)}, f32[2,2,1024]{2,1,0:T(...) while((s32[]{:T(128)}, f32[2,8,1024]{2,1,0:T(8,128)}, ...), condition=%wide.region_3.4_spmd.clone, body=%wide.region_2.3_spmd.clone.sunk | while | flops 302784512 | bytes 29606224 | solution.py:129
  669.1 10.5 collective-permute-done.9
  708.2 7.3 collective-permute-done.9
  745.1 7.3 collective-permute-done.9
  781.8 7.3 collective-permute-done.9
  818.4 7.3 collective-permute-done.9
  855.1 7.3 collective-permute-done.9
  891.8 7.3 collective-permute-done.9
  928.5 7.3 collective-permute-done.9
  965.2 7.3 collective-permute-done.9
  1001.9 7.3 collective-permute-done.9
  1038.6 7.3 collective-permute-done.9
  1075.3 7.3 collective-permute-done.9
  1185.3 7.3 collective-permute-done.9
  1222.0 7.3 collective-permute-done.9
  (1189 shorter events, 951.7 us)
Async XLA Ops:
  11.4 10.6 collective-permute-start
  48.8 10.7 collective-permute-start
  76.9 11.8 collective-permute-start.4
  89.3 9.5 collective-permute-start
  116.5 11.5 collective-permute-start.4
  128.6 10.5 collective-permute-start
  156.5 11.8 collective-permute-start.4
  168.9 9.4 collective-permute-start
  195.7 11.8 collective-permute-start.4
  208.1 10.2 collective-permute-start
  235.6 11.8 collective-permute-start.4
  248.1 9.8 collective-permute-start
  275.3 11.8 collective-permute-start.4
  287.7 9.4 collective-permute-start
  314.4 11.8 collective-permute-start.4
  326.9 9.4 collective-permute-start
  353.6 11.8 collective-permute-start.4
  366.1 9.4 collective-permute-start
  392.8 11.8 collective-permute-start.4
  405.3 9.4 collective-permute-start
  432.0 11.8 collective-permute-start.4
  444.5 9.4 collective-permute-start
  471.2 11.8 collective-permute-start.4
  483.7 9.4 collective-permute-start
  510.5 11.8 collective-permute-start.4
  522.9 9.4 collective-permute-start
  549.7 11.8 collective-permute-start.4
  562.2 9.4 collective-permute-start
  589.0 11.8 collective-permute-start.4
  601.5 9.4 collective-permute-start
  628.2 11.8 collective-permute-start.4
  667.1 12.5 %collective-permute-start.9 = (f32[2,8,1024]{2,1,0:T(8,128)S(1)}, f32[2,8,1024]{2,1,0:T(8,128)}, u32[]{:S(2)}, u32[]{:S(2)}) collective-permute-start(f32[2,8,1024]{2,1,0:T(8,128)S(1)} %maximum_add_fusion.20), channel_id=1, source_target_pairs={{8,0},{16,8},{24,16},{32,24},{40,32},{48,40},{56,48},{64,56},{72,6... | collective-permute-start | bytes 196616 | tf_op jit(solution)/shard_map/while/body/eval_jaxpr/ppermute | solution.py:23
  (195 other events, 1246.4 us)
where the time goes:
time: 1240 us; the launch traced here: 1230 us
  starting transfers between devices  514 us (41%)
  matrix products  256 us (21%)
  waiting for transfers between devices  240 us (19%)
  local copies, waits for them, and re-layouts  167 us (13%)
  other arithmetic  43.9 us (4%)
    ppermute x64, starting transfers between devices, extended(): lax.ppermute(lax.slice_in_dim(block, block.shape[dim] - width, None, axis...  237 us
    ppermute x32, starting transfers between devices, from_behind(): lax.ppermute(value, axis, [(source, source + steps) for source in range(l...  195 us
    ppermute x32, waiting for transfers between devices, from_behind(): lax.ppermute(value, axis, [(source, source + steps) for source in range(l...  140 us
    ppermute x64, waiting for transfers between devices, extended(): lax.ppermute(lax.slice_in_dim(block, 0, width, axis=dim), axis, backward)  100 us
    ppermute x64, starting transfers between devices, extended(): lax.ppermute(lax.slice_in_dim(block, 0, width, axis=dim), axis, backward)  82.3 us
    dot_general x64, matrix products, block_product(): jnp.einsum(form, shifted[1], blocks[:, :, 0], precision=high)  64.4 us
    dot_general x64, matrix products, block_product(): jnp.einsum(form, shifted[0], blocks[:, :, 0], precision=high)  64.2 us
    dot_general x64, matrix products, block_product(): jnp.einsum(form, shifted[0], blocks[:, :, 1], precision=high)  63.8 us
  transfers between devices with their start and end apart: 160, of which 64 were waited for; matrix products, arithmetic and copies ran while one was open for 11% of the time, Pallas kernels for 0%

commit v1 on v0

v1 whole, which is shorter than its diff:
```python
import functools

import jax
import jax.numpy as jnp
from jax import lax
from jax.experimental import pallas as pl
from jax.experimental.pallas import tpu as pltpu
from jax.sharding import PartitionSpec as P

TILE = 128
GROUP = 4
OWN = 4
HALO = 3
SLOTS = OWN + 2 * HALO
WINDOW = (OWN + 2 * (HALO + 1)) * TILE
SPAN = SLOTS * TILE
HALF = OWN * TILE
VMEM_LIMIT = 10 << 20

VMEM_SPEC = pl.BlockSpec(memory_space=pltpu.VMEM)
SMEM_SPEC = pl.BlockSpec(memory_space=pltpu.SMEM)
ANY_SPEC = pl.BlockSpec(memory_space=pl.ANY)
PARAMS = pltpu.CompilerParams(vmem_limit_bytes=VMEM_LIMIT)
AXES = ("depth", "lat")


def split_store(buffer, slot_ref):
    for offset in range(3):
        for part in range(2):
            block = buffer[offset, part]
            high = block.astype(jnp.bfloat16)
            low = (block - high.astype(jnp.float32)).astype(jnp.bfloat16)
            rows = slice(offset * TILE, (offset + 1) * TILE)
            slot_ref[rows, part * TILE : (part + 1) * TILE] = high
            slot_ref[rows, (2 + part) * TILE : (3 + part) * TILE] = low


def pipelined(units, source_of, slot_of, buffers, sems):
    def copy(unit, place):
        return pltpu.make_async_copy(source_of(unit), buffers.at[place], sems.at[place])

    copy(0, 0).start()

    def body(unit, _):
        place = lax.rem(unit, 2)

        @pl.when(unit + 1 < units)
        def _():
            copy(unit + 1, 1 - place).start()

        copy(unit, place).wait()
        split_store(buffers.at[place], slot_of(unit))
        return 0

    lax.fori_loop(0, units, body, 0)


def chip_body(ids, source, *refs, mine):
    packed, buffers, sems = refs[-3:]
    core = ids[1]
    first = 2 * core if mine else 2 * (1 - core)
    count = OWN + HALO

    def source_of(unit):
        return source.at[unit // count, lax.rem(unit, count) + core]

    def slot_of(unit):
        return packed.at[first + unit // count, lax.rem(unit, count) + HALO * (1 - core)]

    pipelined(2 * count, source_of, slot_of, buffers, sems)


def halo_body(ids, *refs, places):
    sources = refs[:4]
    packed, buffers, sems = refs[-3:]
    core = ids[1]
    for side in range(2):

        @pl.when(core == side)
        def _():
            units = []
            for near, entries in ((sources[side], places[0]), (sources[2 + side], places[1])):
                for index, (layer, reach) in enumerate(entries[side]):
                    units.append((near.at[index], packed.at[layer, reach]))

            def copy(number):
                place = number % 2
                return pltpu.make_async_copy(units[number][0], buffers.at[place], sems.at[place])

            copy(0).start()
            for number in range(len(units)):
                if number + 1 < len(units):
                    copy(number + 1).start()
                copy(number).wait()
                split_store(buffers.at[number % 2], units[number][1])


PACKED = (GROUP, SLOTS, 3 * TILE, 4 * TILE)
PACK_SCRATCH = [pltpu.VMEM((2, 3, 2, TILE, TILE), jnp.float32), pltpu.SemaphoreType.DMA((2,))]


def pack_chip(ids, source, packed, mine):
    extra = () if packed is None else (packed,)
    return pl.pallas_call(
        functools.partial(chip_body, mine=mine),
        in_specs=[SMEM_SPEC, ANY_SPEC] + [VMEM_SPEC] * len(extra),
        out_specs=VMEM_SPEC,
        out_shape=jax.ShapeDtypeStruct(PACKED, jnp.bfloat16),
        scratch_shapes=PACK_SCRATCH,
        input_output_aliases={2: 0} if extra else {},
        compiler_params=PARAMS,
        name="pack_mine" if mine else "pack_partner",
    )(ids, source, *extra)


def pack_halo(ids, sources, packed, places, name):
    return pl.pallas_call(
        functools.partial(halo_body, places=places),
        in_specs=[SMEM_SPEC] + [ANY_SPEC] * 4 + [VMEM_SPEC],
        out_specs=VMEM_SPEC,
        out_shape=jax.ShapeDtypeStruct(PACKED, jnp.bfloat16),
        scratch_shapes=PACK_SCRATCH,
        input_output_aliases={5: 0},
        compiler_params=PARAMS,
        name=name,
    )(ids, *sources, packed)


def store_parts(parts_ref, where, value):
    high = value.astype(jnp.bfloat16)
    parts_ref[0:16, where] = high
    parts_ref[16:32, where] = (value - high.astype(jnp.float32)).astype(jnp.bfloat16)


def scaled(coef_real, coef_imag, value):
    real, imag = value[0:8], value[8:16]
    return jnp.concatenate(
        [coef_real * real - coef_imag * imag, coef_real * imag + coef_imag * real], axis=0
    )


def tile_product(parts_ref, packed, layer, spot):
    product = jnp.dot(
        parts_ref[:, spot * TILE : (spot + 3) * TILE],
        packed[layer, spot],
        preferred_element_type=jnp.float32,
    )
    rows = product[0:16] + product[16:32]
    both = rows[:, 0 : 2 * TILE] + rows[:, 2 * TILE : 4 * TILE]
    real, imag = both[0:8], both[8:16]
    return jnp.concatenate(
        [real[:, 0:TILE] - imag[:, TILE:], real[:, TILE:] + imag[:, 0:TILE]], axis=0
    )


def lanes(start, stop):
    return slice(start * TILE, stop * TILE)


def down_body(ids, low, mid, high, window, packed, _, out, waves, parts, *, turn):
    @pl.when(ids[0] == turn)
    def _():
        for layer in range(GROUP):
            reach = HALO - layer
            if layer == 0:
                pieces = [(lanes(0, 4), low[...]), (lanes(4, 8), mid[...]), (lanes(8, 12), high[...])]
            else:
                begin, end = HALO - reach - 1, HALO + OWN + reach + 1
                pieces = [(lanes(begin + 1, end + 1), waves[layer - 1, :, lanes(begin, end)])]
            for where, value in pieces:
                forcing = window[layer, 0:16, where]
                coef_real = window[layer, 16:17, where]
                coef_imag = window[layer, 17:18, where]
                store_parts(parts, where, forcing + scaled(coef_real, coef_imag, value))
            for spot in range(HALO - reach, HALO + OWN + reach):
                waves[layer, :, lanes(spot, spot + 1)] = tile_product(parts, packed, layer, spot)
        out[...] = waves[GROUP - 1, :, lanes(HALO, HALO + OWN)]


def up_body(ids, low, mid, high, window, packed, waves, left, right, _, out, field, parts, span, *, turn):
    @pl.when(ids[0] == turn)
    def _():
        for layer in reversed(range(GROUP)):
            reach = layer
            if layer == GROUP - 1:
                pieces = [(lanes(0, 4), low[...]), (lanes(4, 8), mid[...]), (lanes(8, 12), high[...])]
            else:
                begin, end = HALO - reach - 1, HALO + OWN + reach + 1
                pieces = [(lanes(begin + 1, end + 1), span[:, lanes(begin, end)])]
            for where, value in pieces:
                coef_real = window[layer, 18:19, where]
                coef_imag = window[layer, 19:20, where]
                store_parts(parts, where, scaled(coef_real, coef_imag, value))
            for spot in range(HALO - reach, HALO + OWN + reach):
                if layer >= 2 and spot < HALO:
                    wave = left[layer - 2, :, lanes(spot + 1, spot + 2)]
                elif layer >= 2 and spot >= HALO + OWN:
                    wave = right[layer - 2, :, lanes(spot - HALO - OWN, spot - HALO - OWN + 1)]
                else:
                    wave = waves[layer, :, lanes(spot, spot + 1)]
                span[:, lanes(spot, spot + 1)] = wave + tile_product(parts, packed, layer, spot)
            field[layer] = span[:, lanes(HALO, HALO + OWN)]
        out[...] = span[:, lanes(HALO, HALO + OWN)]


PARTS = pltpu.VMEM((32, WINDOW), jnp.bfloat16)


def down_step(ids, received, window, packed, waves, turn):
    return pl.pallas_call(
        functools.partial(down_body, turn=turn),
        in_specs=[SMEM_SPEC] + [VMEM_SPEC] * 6,
        out_specs=(VMEM_SPEC, VMEM_SPEC),
        out_shape=(
            jax.ShapeDtypeStruct((16, HALF), jnp.float32),
            jax.ShapeDtypeStruct((GROUP, 16, SPAN), jnp.float32),
        ),
        scratch_shapes=[PARTS],
        input_output_aliases={6: 1},
        compiler_params=PARAMS,
        name=f"down_{turn}",
    )(ids, *received, window, packed, waves)


def up_step(ids, received, window, packed, waves, left, right, field, turn):
    return pl.pallas_call(
        functools.partial(up_body, turn=turn),
        in_specs=[SMEM_SPEC] + [VMEM_SPEC] * 9,
        out_specs=(VMEM_SPEC, VMEM_SPEC),
        out_shape=(
            jax.ShapeDtypeStruct((16, HALF), jnp.float32),
            jax.ShapeDtypeStruct((GROUP, 16, HALF), jnp.float32),
        ),
        scratch_shapes=[PARTS, pltpu.VMEM((16, SPAN), jnp.float32)],
        input_output_aliases={9: 1},
        compiler_params=PARAMS,
        name=f"up_{turn}",
    )(ids, *received, window, packed, waves, left, right, field)


def shards(rhs_field, src_cell, src_layer, factor, couple):
    layer_total, shot_count, strip_cells = rhs_field.shape[1:]
    depth_count, lat_count = lax.axis_size("depth"), lax.axis_size("lat")
    depth_pos, lat_pos = lax.axis_index("depth"), lax.axis_index("lat")
    core = lax.rem(depth_pos, 2)
    first_core = core == 0
    chip_rows = depth_count // 2
    halves = 2 * lat_count
    ids = jnp.stack([depth_pos // 2, core]).astype(jnp.int32)

    def device(row, half):
        return (2 * row + half % 2) * lat_count + half // 2

    def at(depth, lat):
        return depth * lat_count + lat

    def hop(value, rows, step, shift):
        pairs = [
            (device(row, half), device(row + step, half + shift))
            for row in rows
            if 0 <= row + step < chip_rows
            for half in range(halves)
            if 0 <= half + shift < halves
        ]
        return lax.ppermute(value, AXES, pairs)

    partner = [(at(d, l), at(d ^ 1, l)) for d in range(depth_count) for l in range(lat_count)]

    def outward(value, sender, right):
        target, shift = (0, 1) if right else (1, -1)
        pairs = [
            (at(2 * row + sender, l), at(2 * row + target, l + shift))
            for row in range(chip_rows)
            for l in range(lat_count)
            if 0 <= l + shift < lat_count
        ]
        return lax.ppermute(value, AXES, pairs)

    other = lax.ppermute(factor, AXES, partner)
    tiles = factor.shape[1]
    two_right = jnp.concatenate([factor[0, tiles - 3 :], factor[1, tiles - 2 :]])
    two_left = jnp.concatenate([factor[0, :3], factor[1, :2]])
    near_down = (
        outward(two_right, 0, True),
        outward(two_left, 0, False),
        outward(factor[0, tiles - 1 :], 1, True),
        outward(factor[0, :1], 1, False),
    )
    four_right = jnp.concatenate([factor[1, tiles - 3 :], factor[0, tiles - 2 : tiles - 1]])
    four_left = jnp.concatenate([factor[1, :3], factor[0, 1:2]])

    layer_ids = depth_pos * layer_total + jnp.arange(layer_total, dtype=jnp.int32)
    cell_ids = lat_pos * strip_cells + jnp.arange(strip_cells, dtype=jnp.int32)
    hit = (src_layer[None, :, None] == layer_ids[:, None, None]) & (
        src_cell[None, :, None] == cell_ids[None, None, :]
    )
    real_part = rhs_field[0] + 4.0 * hit.astype(jnp.float32)
    rows = jnp.concatenate(
        [real_part, rhs_field[1]] + [couple[way, part][:, None] for way in range(2) for part in range(2)],
        axis=1,
    )
    rows_other = lax.ppermute(rows, AXES, partner)
    chip = jnp.concatenate(
        [jnp.where(first_core, rows, rows_other), jnp.where(first_core, rows_other, rows)]
    )
    edge = jnp.where(first_core, chip[..., HALF:], chip[..., :HALF])
    straight = [(at(2 * r, l), at(2 * r, l + 1)) for r in range(chip_rows) for l in range(lat_count - 1)] + [
        (at(2 * r + 1, l), at(2 * r + 1, l - 1)) for r in range(chip_rows) for l in range(1, lat_count)
    ]
    beside = lax.ppermute(edge, AXES, straight)
    window = jnp.where(
        first_core,
        jnp.concatenate([beside, chip], axis=-1),
        jnp.concatenate([chip, beside], axis=-1),
    )

    packed = pack_chip(ids, factor, None, True)
    packed = pack_chip(ids, other, packed, False)
    down_places = (
        (((0, 0), (0, 1), (0, 2), (1, 1), (1, 2)), ((0, 7), (0, 8), (0, 9), (1, 7), (1, 8))),
        (((2, 2),), ((2, 7),)),
    )
    packed = pack_halo(ids, near_down, packed, down_places, "halo_down")

    zero_half = jnp.zeros((2 * shot_count, HALF), jnp.float32)
    waves = jnp.zeros((GROUP, 2 * shot_count, SPAN), jnp.float32)
    field = jnp.zeros((GROUP, 2 * shot_count, HALF), jnp.float32)

    received = (zero_half,) * 3
    for turn in range(chip_rows):
        out, waves = down_step(ids, received, window, packed, waves, turn)
        if turn + 1 < chip_rows:
            group = range(turn % 3, chip_rows, 3)
            received = (hop(out, group, 1, 1), hop(out, group, 1, 0), hop(out, group, 1, -1))

    near_up = (outward(four_right, 1, True), outward(four_left, 1, False))
    up_places = (
        (((3, 0), (3, 1), (3, 2), (2, 1)), ((3, 7), (3, 8), (3, 9), (2, 8))),
        ((), ()),
    )
    packed = pack_halo(ids, near_up + near_up, packed, up_places, "halo_up")

    deep = waves[2:, :, HALO * TILE : (HALO + OWN) * TILE]
    everyone = range(chip_rows)
    left, right = hop(deep, everyone, 0, 1), hop(deep, everyone, 0, -1)
    received = (zero_half,) * 3
    for turn in reversed(range(chip_rows)):
        out, field = up_step(ids, received, window, packed, waves, left, right, field, turn)
        if turn:
            group = range(turn % 3, chip_rows, 3)
            received = (hop(out, group, -1, 1), hop(out, group, -1, 0), hop(out, group, -1, -1))

    own_waves = waves[:, :, HALO * TILE : (HALO + OWN) * TILE]
    both = jnp.stack([own_waves, field])
    keep = jnp.where(first_core, both[:, :2], both[:, 2:])
    give = jnp.where(first_core, both[:, 2:], both[:, :2])
    taken = lax.ppermute(give, AXES, partner)
    whole = jnp.concatenate(
        [jnp.where(first_core, keep, taken), jnp.where(first_core, taken, keep)], axis=-1
    )
    whole = whole.reshape(2, layer_total, 2, shot_count, strip_cells).transpose(0, 2, 1, 3, 4)
    return (whole[0], whole[1])


def solution(mesh):
    placed = (
        P(None, "depth", None, "lat"),
        P(),
        P(),
        P("depth", "lat", None, None, None, None),
        P(None, None, "depth", "lat"),
    )
    return jax.shard_map(
        shards,
        mesh=mesh,
        in_specs=placed,
        out_specs=(P(None, "depth", None, "lat"), P(None, "depth", None, "lat")),
        check_vma=False,
    )
```

time: 1240 us -> 277 us (0.22)
  the two profiles are of different devices: /device:TPU:25 before, /device:TPU:1 now
where the time goes in v1:
time: 277 us; the launch traced here: 276 us
  starting transfers between devices  130 us (47%)
  waiting for transfers between devices  95 us (34%)
  Pallas kernels  32.3 us (12%)
  local copies, waits for them, and re-layouts  10.4 us (4%)
  other arithmetic  7.04 us (3%)
    ppermute x44, waiting for transfers between devices, hop(): return lax.ppermute(value, AXES, pairs)  80.6 us
    ppermute x44, starting transfers between devices, hop(): return lax.ppermute(value, AXES, pairs)  79.5 us
    ppermute x6, starting transfers between devices, outward(): return lax.ppermute(value, AXES, pairs)  43.3 us
    pallas_call x2, Pallas kernels, pack_chip(): pl.pallas_call(functools.partial(chip_body, mine=mine), in_specs=[SMEM_SP...  12.8 us
    ppermute x6, waiting for transfers between devices, outward(): return lax.ppermute(value, AXES, pairs)  7.32 us
    pallas_call x8, Pallas kernels, up_step(): pl.pallas_call(functools.partial(up_body, turn=turn), in_specs=[SMEM_SPEC...  7.08 us
    pallas_call x8, Pallas kernels, down_step(): pl.pallas_call(functools.partial(down_body, turn=turn), in_specs=[SMEM_SP...  7.02 us
    ppermute x1, waiting for transfers between devices, shards(): beside = lax.ppermute(edge, AXES, straight)  5.67 us
  transfers between devices with their start and end apart: 54, of which 15 were waited for; matrix products, arithmetic and copies ran while one was open for 5% of the time, Pallas kernels for 9%

profile of v1, /device:TPU:1, one launch (start us, length us, event | category | flops | bytes accessed | tf_op | source)
XLA Modules:
  0.0 276.2 jit_solution(14548663115755075884)
XLA Ops:
  0.6 1.5 collective-permute-start.6
  2.1 1.5 slice_bitcast_fusion.4
  3.6 2.8 %slice_bitcast_fusion.2 = (f32[3,3,2,128,128]{4,3,2,1,0:T(8,128)S(1)}, f32[3,3,2,128,128]{4,3,2,1,0:T(8,128)S(1)}, f32[3,3,2,128,128]{4,3,2,1,0:T(8,128)S(1)}, f32[3,3,2,128,128]{4,3,2,1,0:T(8,128)S(1)}) fusion(f32[2,8,3,2,128,128]{5,4,3,2,1,0:T(8,128)} %source.1), kind=kLoop, calls=%fused_computation.6 | loop fusion | bytes 9437184 | tf_op jit(solution)/shard_map/squeeze | solution.py:282
  6.4 1.5 pad_maximum_fusion
  7.9 2.0 collective-permute-start.2
  9.9 1.5 pad_maximum_fusion.1
  13.1 4.1 %collective-permute-start = (f32[2,20,1024]{2,1,0:T(8,128)S(1)}, f32[2,20,1024]{2,1,0:T(8,128)}, u32[]{:S(2)}, u32[]{:S(2)}) collective-permute-start(f32[2,20,1024]{2,1,0:T(8,128)S(1)} %concatenate.27), channel_id=1, source_target_pairs={{0,8},{1,9},{2,10},{3,11},{4,12},{5,13},{6,14},{7,15},{8,0},{9,1},... | collective-permute-start | bytes 491528 | tf_op jit(solution)/shard_map/ppermute | solution.py:302
  17.2 2.4 slice_bitcast_fusion.8
  19.6 1.9 collective-permute-start.4
  26.5 5.7 %collective-permute-done.1 = f32[4,20,512]{2,1,0:T(8,128)S(1)} collective-permute-done((f32[4,20,512]{2,1,0:T(8,128)S(1)}, f32[4,20,512]{2,1,0:T(8,128)S(1)}, u32[]{:S(2)}, u32[]{:S(2)}) %collective-permute-start.1) | collective-permute-done | bytes 163872 | tf_op jit(solution)/shard_map/ppermute | solution.py:310
  32.2 35.5 %collective-permute-start.28 = (f32[4,3,2,128,128]{4,3,2,1,0:T(8,128)}, f32[4,3,2,128,128]{4,3,2,1,0:T(8,128)S(1)}, u32[]{:S(2)}, u32[]{:S(2)}) collective-permute-start(f32[4,3,2,128,128]{4,3,2,1,0:T(8,128)} %pad_maximum_fusion.2), channel_id=1, source_target_pairs={{8,1},{9,2},{10,3},{11,4},{12,5},{13,6},{14,7},{24,17},{25,18},{26... | collective-permute-start | bytes 4718600 | tf_op jit(solution)/shard_map/ppermute | solution.py:277
  70.5 2.8 %copy-done = f32[2,8,3,2,128,128]{5,4,3,2,1,0:T(8,128)S(1)} copy-done((f32[2,8,3,2,128,128]{5,4,3,2,1,0:T(8,128)S(1)}, f32[2,8,3,2,128,128]{5,4,3,2,1,0:T(8,128)}, u32[]{:S(2)}) %copy-start) | copy-done | bytes 6291480
  73.3 4.4 %pack_mine.1.refs_0_ = bf16[4,10,384,512]{3,2,1,0:T(8,128)(2,1)S(1)} custom-call(s32[2]{0:T(128)S(1)} %pad_add_fusion.ids, f32[2,8,3,2,128,128]{5,4,3,2,1,0:T(8,128)S(1)} %copy-done), custom_call_target="tpu_custom_call" | custom-call | tf_op jit(solution)/shard_map/pack_mine/pallas_call | solution.py:104
  77.8 8.3 %pack_partner.1.refs_4_ = bf16[4,10,384,512]{3,2,1,0:T(8,128)(2,1)S(1)} custom-call(s32[2]{0:T(128)S(1)} %pad_add_fusion.ids, f32[2,8,3,2,128,128]{5,4,3,2,1,0:T(8,128)} %collective-permute-done.6.source, bf16[4,10,384,512]{3,2,1,0:T(8,128)(2,1)S(1)} %pack_mine.1.refs_0_), custom_call_target="tpu_custom_call", output_to_operand_aliasing={{}: (2, {})} | custom-call | tf_op jit(solution)/shard_map/pack_partner/pallas_call | solution.py:104
  86.2 7.3 %collective-permute-done.5.refs_3_ = f32[1,3,2,128,128]{4,3,2,1,0:T(8,128)} collective-permute-done((f32[1,3,2,128,128]{4,3,2,1,0:T(8,128)}, f32[1,3,2,128,128]{4,3,2,1,0:T(8,128)}, u32[]{:S(2)}, u32[]{:S(2)}) %collective-permute-start.5) | collective-permute-done | bytes 393248 | tf_op jit(solution)/shard_map/ppermute | solution.py:277
  93.5 3.8 %halo_down.1.packed.refs_4_ = bf16[4,10,384,512]{3,2,1,0:T(8,128)(2,1)S(1)} custom-call(s32[2]{0:T(128)S(1)} %pad_add_fusion.ids, f32[5,3,2,128,128]{4,3,2,1,0:T(8,128)} %collective-permute-done.2.refs_0_, f32[5,3,2,128,128]{4,3,2,1,0:T(8,128)} %collective-permute-done.3.refs_1_, ...), custom_call_target="tpu_custom_call", output_to_operand_aliasing={{}: (5, {})} | custom-call | tf_op jit(solution)/shard_map/halo_down/pallas_call | solution.py:117
  97.4 2.4 down_0.1
  101.0 1.4 collective-permute-start.8
  110.5 10.4 %collective-permute-start.16 = (f32[16,512]{1,0:T(8,128)S(1)}, f32[16,512]{1,0:T(8,128)S(1)}, u32[]{:S(2)}, u32[]{:S(2)}) collective-permute-start(f32[16,512]{1,0:T(8,128)S(1)} %get-tuple-element.38), channel_id=1, source_target_pairs={{0,24},{8,17},{1,25},{9,18},{2,26},{10,19},{3,27},{11,20},{4,28},{... | collective-permute-start | bytes 98312 | tf_op jit(solution)/shard_map/ppermute | solution.py:265
  130.4 26.7 %collective-permute-start.25 = (f32[16,512]{1,0:T(8,128)S(1)}, f32[16,512]{1,0:T(8,128)S(1)}, u32[]{:S(2)}, u32[]{:S(2)}) collective-permute-start(f32[16,512]{1,0:T(8,128)S(1)} %get-tuple-element.44), channel_id=1, source_target_pairs={{0,24},{8,17},{1,25},{9,18},{2,26},{10,19},{3,27},{11,20},{4,28},{... | collective-permute-start | bytes 98312 | tf_op jit(solution)/shard_map/ppermute | solution.py:265
  161.9 3.8 %collective-permute-start.30 = (f32[2,16,512]{2,1,0:T(8,128)S(1)}, f32[2,16,512]{2,1,0:T(8,128)S(1)}, u32[]{:S(2)}, u32[]{:S(2)}) collective-permute-start(f32[2,16,512]{2,1,0:T(8,128)S(1)} %slice.93), channel_id=1, source_target_pairs={{0,8},{8,1},{1,9},{9,2},{2,10},{10,3},{3,11},{11,4},{4,12},{12,5},... | collective-permute-start | bytes 196616 | tf_op jit(solution)/shard_map/ppermute | solution.py:265
  165.7 1.9 collective-permute-start.31
  167.7 1.6 halo_up.1.packed
  169.3 2.4 collective-permute-done.31.right
  177.5 13.3 %collective-permute-done.33.mid = f32[16,512]{1,0:T(8,128)S(1)} collective-permute-done((f32[16,512]{1,0:T(8,128)S(1)}, f32[16,512]{1,0:T(8,128)S(1)}, u32[]{:S(2)}, u32[]{:S(2)}) %collective-permute-start.33) | collective-permute-done | bytes 32800 | tf_op jit(solution)/shard_map/ppermute | solution.py:265
  190.8 4.7 %collective-permute-done.34.high = f32[16,512]{1,0:T(8,128)S(1)} collective-permute-done((f32[16,512]{1,0:T(8,128)S(1)}, f32[16,512]{1,0:T(8,128)S(1)}, u32[]{:S(2)}, u32[]{:S(2)}) %collective-permute-start.34) | collective-permute-done | bytes 32800 | tf_op jit(solution)/shard_map/ppermute | solution.py:265
  205.4 24.3 %collective-permute-done.41.low = f32[16,512]{1,0:T(8,128)S(1)} collective-permute-done((f32[16,512]{1,0:T(8,128)S(1)}, f32[16,512]{1,0:T(8,128)S(1)}, u32[]{:S(2)}, u32[]{:S(2)}) %collective-permute-start.41) | collective-permute-done | bytes 32800 | tf_op jit(solution)/shard_map/ppermute | solution.py:265
  230.1 2.4 collective-permute-done.43.high
  242.2 26.1 %collective-permute-done.50.low = f32[16,512]{1,0:T(8,128)S(1)} collective-permute-done((f32[16,512]{1,0:T(8,128)S(1)}, f32[16,512]{1,0:T(8,128)S(1)}, u32[]{:S(2)}, u32[]{:S(2)}) %collective-permute-start.50) | collective-permute-done | bytes 32800 | tf_op jit(solution)/shard_map/ppermute | solution.py:265
  268.3 2.6 collective-permute-done.52.high
  270.9 3.0 %up_0.1 = (f32[16,512]{1,0:T(8,128)}, f32[4,16,512]{2,1,0:T(8,128)S(1)}) custom-call(s32[2]{0:T(128)S(1)} %pad_add_fusion.ids, f32[16,512]{1,0:T(8,128)S(1)} %collective-permute-done.50.low, f32[16,512]{1,0:T(8,128)S(1)} %collective-permute-done.51.mid, f32[16,512]{1,0:T(8,128)S(1)} %collective-permute-done.52.high, ...), custom_call_target="tpu_custom_call", output_to_operand_aliasing={{1}: (9, {})} | custom-call | tf_op jit(solution)/shard_map/up_0/pallas_call | solution.py:226
  274.1 1.3 collective-permute-done.53
  (152 shorter events, 59.1 us)
Async XLA Ops:
  0.6 68.4 %collective-permute-start.6 = (f32[2,8,3,2,128,128]{5,4,3,2,1,0:T(8,128)}, f32[2,8,3,2,128,128]{5,4,3,2,1,0:T(8,128)}, u32[]{:S(2)}, u32[]{:S(2)}) collective-permute-start(f32[2,8,3,2,128,128]{5,4,3,2,1,0:T(8,128)} %source.1), channel_id=1, source_target_pairs={{0,8},{1,9},{2,10},{3,11},{4,12},{5,13},{6,14},{7,15},{8,0},{9,1},... | collective-permute-start | bytes 18874376 | tf_op jit(solution)/shard_map/ppermute | solution.py:279
  7.9 85.6 %collective-permute-start.2 = (f32[5,3,2,128,128]{4,3,2,1,0:T(8,128)}, f32[5,3,2,128,128]{4,3,2,1,0:T(8,128)}, u32[]{:S(2)}, u32[]{:S(2)}) collective-permute-start(f32[5,3,2,128,128]{4,3,2,1,0:T(8,128)} %pad_maximum_fusion), channel_id=1, source_target_pairs={{0,1},{1,2},{2,3},{3,4},{4,5},{5,6},{6,7},{16,17},{17,18},{18,19},... | collective-permute-start | bytes 5898248 | tf_op jit(solution)/shard_map/ppermute | solution.py:277
  11.4 82.1 %collective-permute-start.3 = (f32[5,3,2,128,128]{4,3,2,1,0:T(8,128)}, f32[5,3,2,128,128]{4,3,2,1,0:T(8,128)}, u32[]{:S(2)}, u32[]{:S(2)}) collective-permute-start(f32[5,3,2,128,128]{4,3,2,1,0:T(8,128)} %pad_maximum_fusion.1), channel_id=1, source_target_pairs={{1,8},{2,9},{3,10},{4,11},{5,12},{6,13},{7,14},{17,24},{18,25},{19... | collective-permute-start | bytes 5898248 | tf_op jit(solution)/shard_map/ppermute | solution.py:277
  13.1 8.4 %collective-permute-start = (f32[2,20,1024]{2,1,0:T(8,128)S(1)}, f32[2,20,1024]{2,1,0:T(8,128)}, u32[]{:S(2)}, u32[]{:S(2)}) collective-permute-start(f32[2,20,1024]{2,1,0:T(8,128)S(1)} %concatenate.27), channel_id=1, source_target_pairs={{0,8},{1,9},{2,10},{3,11},{4,12},{5,13},{6,14},{7,15},{8,0},{9,1},... | collective-permute-start | bytes 491528 | tf_op jit(solution)/shard_map/ppermute | solution.py:302
  19.6 48.2 %collective-permute-start.4 = (f32[1,3,2,128,128]{4,3,2,1,0:T(8,128)}, f32[1,3,2,128,128]{4,3,2,1,0:T(8,128)S(1)}, u32[]{:S(2)}, u32[]{:S(2)}) collective-permute-start(f32[1,3,2,128,128]{4,3,2,1,0:T(8,128)} %get-tuple-element.64), channel_id=1, source_target_pairs={{8,1},{9,2},{10,3},{11,4},{12,5},{13,6},{14,7},{24,17},{25,18},{26... | collective-permute-start | bytes 1179656 | tf_op jit(solution)/shard_map/ppermute | solution.py:277
  22.7 9.5 %collective-permute-start.1 = (f32[4,20,512]{2,1,0:T(8,128)S(1)}, f32[4,20,512]{2,1,0:T(8,128)S(1)}, u32[]{:S(2)}, u32[]{:S(2)}) collective-permute-start(f32[4,20,512]{2,1,0:T(8,128)S(1)} %fusion.1), channel_id=1, source_target_pairs={{0,1},{1,2},{2,3},{3,4},{4,5},{5,6},{6,7},{16,17},{17,18},{18,19},... | collective-permute-start | bytes 491528 | tf_op jit(solution)/shard_map/ppermute | solution.py:310
  32.2 135.4 %collective-permute-start.28 = (f32[4,3,2,128,128]{4,3,2,1,0:T(8,128)}, f32[4,3,2,128,128]{4,3,2,1,0:T(8,128)S(1)}, u32[]{:S(2)}, u32[]{:S(2)}) collective-permute-start(f32[4,3,2,128,128]{4,3,2,1,0:T(8,128)} %pad_maximum_fusion.2), channel_id=1, source_target_pairs={{8,1},{9,2},{10,3},{11,4},{12,5},{13,6},{14,7},{24,17},{25,18},{26... | collective-permute-start | bytes 4718600 | tf_op jit(solution)/shard_map/ppermute | solution.py:277
  67.8 99.9 %collective-permute-start.29 = (f32[4,3,2,128,128]{4,3,2,1,0:T(8,128)}, f32[4,3,2,128,128]{4,3,2,1,0:T(8,128)S(1)}, u32[]{:S(2)}, u32[]{:S(2)}) collective-permute-start(f32[4,3,2,128,128]{4,3,2,1,0:T(8,128)} %pad_maximum_fusion.3), channel_id=1, source_target_pairs={{9,8},{10,9},{11,10},{12,11},{13,12},{14,13},{15,14},{25,24},{26,2... | collective-permute-start | bytes 4718600 | tf_op jit(solution)/shard_map/ppermute | solution.py:277
  69.1 24.4 %collective-permute-start.5 = (f32[1,3,2,128,128]{4,3,2,1,0:T(8,128)}, f32[1,3,2,128,128]{4,3,2,1,0:T(8,128)}, u32[]{:S(2)}, u32[]{:S(2)}) collective-permute-start(f32[1,3,2,128,128]{4,3,2,1,0:T(8,128)} %get-tuple-element.62), channel_id=1, source_target_pairs={{9,8},{10,9},{11,10},{12,11},{13,12},{14,13},{15,14},{25,24},{26,2... | collective-permute-start | bytes 1179656 | tf_op jit(solution)/shard_map/ppermute | solution.py:277
  99.7 4.0 %collective-permute-start.7 = (f32[16,512]{1,0:T(8,128)S(1)}, f32[16,512]{1,0:T(8,128)S(1)}, u32[]{:S(2)}, u32[]{:S(2)}) collective-permute-start(f32[16,512]{1,0:T(8,128)S(1)} %get-tuple-element.32), channel_id=1, source_target_pairs={{0,24},{8,17},{1,25},{9,18},{2,26},{10,19},{3,27},{11,20},{4,28},{... | collective-permute-start | bytes 98312 | tf_op jit(solution)/shard_map/ppermute | solution.py:265
  101.0 2.7 collective-permute-start.8
  102.4 2.3 collective-permute-start.9
  110.5 13.0 %collective-permute-start.16 = (f32[16,512]{1,0:T(8,128)S(1)}, f32[16,512]{1,0:T(8,128)S(1)}, u32[]{:S(2)}, u32[]{:S(2)}) collective-permute-start(f32[16,512]{1,0:T(8,128)S(1)} %get-tuple-element.38), channel_id=1, source_target_pairs={{0,24},{8,17},{1,25},{9,18},{2,26},{10,19},{3,27},{11,20},{4,28},{... | collective-permute-start | bytes 98312 | tf_op jit(solution)/shard_map/ppermute | solution.py:265
  120.9 2.6 collective-permute-start.17
  122.2 2.3 collective-permute-start.18
  125.2 2.0 collective-permute-start.19
  127.8 2.0 collective-permute-start.22
  130.4 29.3 %collective-permute-start.25 = (f32[16,512]{1,0:T(8,128)S(1)}, f32[16,512]{1,0:T(8,128)S(1)}, u32[]{:S(2)}, u32[]{:S(2)}) collective-permute-start(f32[16,512]{1,0:T(8,128)S(1)} %get-tuple-element.44), channel_id=1, source_target_pairs={{0,24},{8,17},{1,25},{9,18},{2,26},{10,19},{3,27},{11,20},{4,28},{... | collective-permute-start | bytes 98312 | tf_op jit(solution)/shard_map/ppermute | solution.py:265
  157.2 2.6 collective-permute-start.26
  158.5 2.3 collective-permute-start.27
  161.9 7.3 %collective-permute-start.30 = (f32[2,16,512]{2,1,0:T(8,128)S(1)}, f32[2,16,512]{2,1,0:T(8,128)S(1)}, u32[]{:S(2)}, u32[]{:S(2)}) collective-permute-start(f32[2,16,512]{2,1,0:T(8,128)S(1)} %slice.93), channel_id=1, source_target_pairs={{0,8},{8,1},{1,9},{9,2},{2,10},{10,3},{3,11},{11,4},{4,12},{12,5},... | collective-permute-start | bytes 196616 | tf_op jit(solution)/shard_map/ppermute | solution.py:265
  165.7 5.9 %collective-permute-start.31 = (f32[2,16,512]{2,1,0:T(8,128)S(1)}, f32[2,16,512]{2,1,0:T(8,128)S(1)}, u32[]{:S(2)}, u32[]{:S(2)}) collective-permute-start(f32[2,16,512]{2,1,0:T(8,128)S(1)} %slice.93), channel_id=1, source_target_pairs={{8,0},{1,8},{9,1},{2,9},{10,2},{3,10},{11,3},{4,11},{12,4},{5,12},... | collective-permute-start | bytes 196616 | tf_op jit(solution)/shard_map/ppermute | solution.py:265
  172.2 5.2 %collective-permute-start.32 = (f32[16,512]{1,0:T(8,128)S(1)}, f32[16,512]{1,0:T(8,128)S(1)}, u32[]{:S(2)}, u32[]{:S(2)}) collective-permute-start(f32[16,512]{1,0:T(8,128)S(1)} %get-tuple-element.47), channel_id=1, source_target_pairs={{16,8},{24,1},{17,9},{25,2},{18,10},{26,3},{19,11},{27,4},{20,12},... | collective-permute-start | bytes 98312 | tf_op jit(solution)/shard_map/ppermute | solution.py:265
  173.5 17.2 %collective-permute-start.33 = (f32[16,512]{1,0:T(8,128)S(1)}, f32[16,512]{1,0:T(8,128)S(1)}, u32[]{:S(2)}, u32[]{:S(2)}) collective-permute-start(f32[16,512]{1,0:T(8,128)S(1)} %get-tuple-element.47), channel_id=1, source_target_pairs={{16,0},{24,8},{17,1},{25,9},{18,2},{26,10},{19,3},{27,11},{20,4},{... | collective-permute-start | bytes 98312 | tf_op jit(solution)/shard_map/ppermute | solution.py:265
  174.8 20.7 %collective-permute-start.34 = (f32[16,512]{1,0:T(8,128)S(1)}, f32[16,512]{1,0:T(8,128)S(1)}, u32[]{:S(2)}, u32[]{:S(2)}) collective-permute-start(f32[16,512]{1,0:T(8,128)S(1)} %get-tuple-element.47), channel_id=1, source_target_pairs={{24,0},{17,8},{25,1},{18,9},{26,2},{19,10},{27,3},{20,11},{28,4},{... | collective-permute-start | bytes 98312 | tf_op jit(solution)/shard_map/ppermute | solution.py:265
  201.5 28.2 %collective-permute-start.41 = (f32[16,512]{1,0:T(8,128)S(1)}, f32[16,512]{1,0:T(8,128)S(1)}, u32[]{:S(2)}, u32[]{:S(2)}) collective-permute-start(f32[16,512]{1,0:T(8,128)S(1)} %get-tuple-element.53), channel_id=1, source_target_pairs={{16,8},{24,1},{17,9},{25,2},{18,10},{26,3},{19,11},{27,4},{20,12},... | collective-permute-start | bytes 98312 | tf_op jit(solution)/shard_map/ppermute | solution.py:265
  202.8 27.3 %collective-permute-start.42 = (f32[16,512]{1,0:T(8,128)S(1)}, f32[16,512]{1,0:T(8,128)S(1)}, u32[]{:S(2)}, u32[]{:S(2)}) collective-permute-start(f32[16,512]{1,0:T(8,128)S(1)} %get-tuple-element.53), channel_id=1, source_target_pairs={{16,0},{24,8},{17,1},{25,9},{18,2},{26,10},{19,3},{27,11},{20,4},{... | collective-permute-start | bytes 98312 | tf_op jit(solution)/shard_map/ppermute | solution.py:265
  204.1 28.4 %collective-permute-start.43 = (f32[16,512]{1,0:T(8,128)S(1)}, f32[16,512]{1,0:T(8,128)S(1)}, u32[]{:S(2)}, u32[]{:S(2)}) collective-permute-start(f32[16,512]{1,0:T(8,128)S(1)} %get-tuple-element.53), channel_id=1, source_target_pairs={{24,0},{17,8},{25,1},{18,9},{26,2},{19,10},{27,3},{20,11},{28,4},{... | collective-permute-start | bytes 98312 | tf_op jit(solution)/shard_map/ppermute | solution.py:265
  235.7 2.0 collective-permute-start.47
  238.3 30.0 %collective-permute-start.50 = (f32[16,512]{1,0:T(8,128)S(1)}, f32[16,512]{1,0:T(8,128)S(1)}, u32[]{:S(2)}, u32[]{:S(2)}) collective-permute-start(f32[16,512]{1,0:T(8,128)S(1)} %get-tuple-element.59), channel_id=1, source_target_pairs={{16,8},{24,1},{17,9},{25,2},{18,10},{26,3},{19,11},{27,4},{20,12},... | collective-permute-start | bytes 98312 | tf_op jit(solution)/shard_map/ppermute | solution.py:265
  239.6 28.7 %collective-permute-start.51 = (f32[16,512]{1,0:T(8,128)S(1)}, f32[16,512]{1,0:T(8,128)S(1)}, u32[]{:S(2)}, u32[]{:S(2)}) collective-permute-start(f32[16,512]{1,0:T(8,128)S(1)} %get-tuple-element.59), channel_id=1, source_target_pairs={{16,0},{24,8},{17,1},{25,9},{18,2},{26,10},{19,3},{27,11},{20,4},{... | collective-permute-start | bytes 98312 | tf_op jit(solution)/shard_map/ppermute | solution.py:265
  240.9 30.1 %collective-permute-start.52 = (f32[16,512]{1,0:T(8,128)S(1)}, f32[16,512]{1,0:T(8,128)S(1)}, u32[]{:S(2)}, u32[]{:S(2)}) collective-permute-start(f32[16,512]{1,0:T(8,128)S(1)} %get-tuple-element.59), channel_id=1, source_target_pairs={{24,0},{17,8},{25,1},{18,9},{26,2},{19,10},{27,3},{20,11},{28,4},{... | collective-permute-start | bytes 98312 | tf_op jit(solution)/shard_map/ppermute | solution.py:265
  (35 other events, 107.4 us)

commit v2 on v1

--- a/solution.py
+++ b/solution.py
@@ -35,20 +35,25 @@
             slot_ref[rows, (2 + part) * TILE : (3 + part) * TILE] = low
 
 
-def pipelined(units, source_of, slot_of, buffers, sems):
-    def copy(unit, place):
-        return pltpu.make_async_copy(source_of(unit), buffers.at[place], sems.at[place])
-
-    copy(0, 0).start()
+BUFFERS = 4
+
+
+def pipelined(units, start, sample, slot_of, buffers, sems):
+    for ahead in range(BUFFERS - 1):
+
+        @pl.when(ahead < units)
+        def _():
+            start(ahead, buffers.at[ahead], sems.at[ahead])
 
     def body(unit, _):
-        place = lax.rem(unit, 2)
-
-        @pl.when(unit + 1 < units)
-        def _():
-            copy(unit + 1, 1 - place).start()
-
-        copy(unit, place).wait()
+        place = lax.rem(unit, BUFFERS)
+        later = lax.rem(unit + BUFFERS - 1, BUFFERS)
+
+        @pl.when(unit + BUFFERS - 1 < units)
+        def _():
+            start(unit + BUFFERS - 1, buffers.at[later], sems.at[later])
+
+        pltpu.make_async_copy(sample, buffers.at[place], sems.at[place]).wait()
         split_store(buffers.at[place], slot_of(unit))
         return 0
 
@@ -61,42 +66,55 @@
     first = 2 * core if mine else 2 * (1 - core)
     count = OWN + HALO
 
-    def source_of(unit):
-        return source.at[unit // count, lax.rem(unit, count) + core]
+    def start(unit, buffer, sem):
+        block = source.at[unit // count, lax.rem(unit, count) + core]
+        pltpu.make_async_copy(block, buffer, sem).start()
 
     def slot_of(unit):
         return packed.at[first + unit // count, lax.rem(unit, count) + HALO * (1 - core)]
 
-    pipelined(2 * count, source_of, slot_of, buffers, sems)
-
-
-def halo_body(ids, *refs, places):
-    sources = refs[:4]
+    pipelined(2 * count, start, source.at[0, 0], slot_of, buffers, sems)
+
+
+def pick(number, values):
+    result = jnp.int32(values[0])
+    for index, value in enumerate(values[1:], 1):
+        result = jnp.where(number == index, value, result)
+    return result
+
+
+def halo_body(ids, straight, cross, *refs, rows, slots):
     packed, buffers, sems = refs[-3:]
-    core = ids[1]
-    for side in range(2):
-
-        @pl.when(core == side)
-        def _():
-            units = []
-            for near, entries in ((sources[side], places[0]), (sources[2 + side], places[1])):
-                for index, (layer, reach) in enumerate(entries[side]):
-                    units.append((near.at[index], packed.at[layer, reach]))
-
-            def copy(number):
-                place = number % 2
-                return pltpu.make_async_copy(units[number][0], buffers.at[place], sems.at[place])
-
-            copy(0).start()
-            for number in range(len(units)):
-                if number + 1 < len(units):
-                    copy(number + 1).start()
-                copy(number).wait()
-                split_store(buffers.at[number % 2], units[number][1])
+    row, core = ids[0], ids[1]
+    units = len(slots[0])
+    first = units // 2
+
+    def start(unit, buffer, sem):
+        @pl.when(unit < first)
+        def _():
+            pltpu.make_async_copy(straight.at[unit], buffer, sem).start()
+
+        @pl.when(unit >= first)
+        def _():
+            pltpu.make_async_copy(cross.at[unit - first], buffer, sem).start()
+
+    def slot_of(unit):
+        number = unit + units * core
+        return packed.at[
+            pick(number, [layer for side in slots for layer, _ in side]),
+            pick(number, [slot for side in slots for _, slot in side]),
+        ]
+
+    @pl.when((row >= rows[0]) & (row < rows[1]))
+    def _():
+        pipelined(units, start, straight.at[0], slot_of, buffers, sems)
 
 
 PACKED = (GROUP, SLOTS, 3 * TILE, 4 * TILE)
-PACK_SCRATCH = [pltpu.VMEM((2, 3, 2, TILE, TILE), jnp.float32), pltpu.SemaphoreType.DMA((2,))]
+PACK_SCRATCH = [
+    pltpu.VMEM((BUFFERS, 3, 2, TILE, TILE), jnp.float32),
+    pltpu.SemaphoreType.DMA((BUFFERS,)),
+]
 
 
 def pack_chip(ids, source, packed, mine):
@@ -110,20 +128,116 @@
         input_output_aliases={2: 0} if extra else {},
         compiler_params=PARAMS,
         name="pack_mine" if mine else "pack_partner",
-    )(ids, source, *extra)
-
-
-def pack_halo(ids, sources, packed, places, name):
-    return pl.pallas_call(
-        functools.partial(halo_body, places=places),
-        in_specs=[SMEM_SPEC] + [ANY_SPEC] * 4 + [VMEM_SPEC],
+    )(ids, pltpu.with_memory_space_constraint(source, pltpu.HBM) if mine else source, *extra)
+
+
+def pack_halo(ids, sources, packed, rows, slots, name):
+    return pl.pallas_call(
+        functools.partial(halo_body, rows=rows, slots=slots),
+        in_specs=[SMEM_SPEC, ANY_SPEC, ANY_SPEC, VMEM_SPEC],
         out_specs=VMEM_SPEC,
         out_shape=jax.ShapeDtypeStruct(PACKED, jnp.bfloat16),
         scratch_shapes=PACK_SCRATCH,
-        input_output_aliases={5: 0},
+        input_output_aliases={3: 0},
         compiler_params=PARAMS,
         name=name,
     )(ids, *sources, packed)
+
+
+def cut_body(ids, mine, other, straight, cross, sems, *, parts):
+    row = ids[0]
+    for begin_row, end_row, runs in parts:
+        for side in range(2):
+
+            @pl.when((row >= begin_row) & (row < end_row) & (ids[1] == side))
+            def _():
+                copies = []
+                for out, entries in zip((straight, cross), runs[side]):
+                    place = 0
+                    for layer, begin, end in entries:
+                        source = mine if layer // 2 == side else other
+                        target = out.at[place : place + end - begin]
+                        copies.append(
+                            pltpu.make_async_copy(
+                                source.at[layer % 2, begin:end], target, sems.at[len(copies)]
+                            )
+                        )
+                        place += end - begin
+                for copy in copies:
+                    copy.start()
+                for copy in copies:
+                    copy.wait()
+
+
+def cut(ids, mine, other, parts, name):
+    count = sum(end - begin for _, begin, end in parts[0][2][0][0])
+    return pl.pallas_call(
+        functools.partial(cut_body, parts=parts),
+        in_specs=[SMEM_SPEC, ANY_SPEC, ANY_SPEC],
+        out_specs=[ANY_SPEC] * 2,
+        out_shape=[pltpu.VMEM((count, 3, 2, TILE, TILE), jnp.float32)] * 2,
+        scratch_shapes=[pltpu.SemaphoreType.DMA((6,))],
+        compiler_params=PARAMS,
+        name=name,
+    )(ids, pltpu.with_memory_space_constraint(mine, pltpu.HBM), other)
+
+
+ROWS = 20
+
+
+def rows_body(ids, cells, layers, rhs, couple, rows):
+    strip = rhs.shape[-1]
+    shot = lax.broadcasted_iota(jnp.int32, (8, strip), 0)
+    position = lax.broadcasted_iota(jnp.int32, (8, strip), 1) + ids[2] * strip
+    target = jnp.full((8, strip), -1, jnp.int32)
+    depth = jnp.full((8, strip), -1, jnp.int32)
+    for index in range(8):
+        target = jnp.where(shot == index, cells[index], target)
+        depth = jnp.where(shot == index, layers[index], depth)
+    here = target == position
+    for layer in range(2):
+        hit = here & (depth == ids[3] * 2 + layer)
+        rows[layer, 0:8] = rhs[0, layer] + jnp.where(hit, 4.0, 0.0)
+        rows[layer, 8:16] = rhs[1, layer]
+        for way in range(2):
+            for part in range(2):
+                spot = 16 + 2 * way + part
+                rows[layer, spot : spot + 1] = couple[way, part, layer : layer + 1]
+
+
+def edge_body(ids, rows, other, edge):
+    for side in range(2):
+
+        @pl.when(ids[1] == side)
+        def _():
+            mine, partner = slice(2 * side, 2 * side + 2), slice(2 - 2 * side, 4 - 2 * side)
+            where = slice(HALF, 2 * HALF) if side == 0 else slice(0, HALF)
+            edge[mine] = rows[:, :, where]
+            edge[partner] = other[:, :, where]
+
+
+def window_body(ids, rows, other, beside, window):
+    for side in range(2):
+
+        @pl.when(ids[1] == side)
+        def _():
+            mine, partner = slice(2 * side, 2 * side + 2), slice(2 - 2 * side, 4 - 2 * side)
+            chip = slice(HALF, WINDOW) if side == 0 else slice(0, 2 * HALF)
+            rest = slice(0, HALF) if side == 0 else slice(2 * HALF, WINDOW)
+            window[mine, :, chip] = rows[...]
+            window[partner, :, chip] = other[...]
+            window[:, :, rest] = beside[...]
+
+
+def small_call(body, smem, arrays, shape, name):
+    return pl.pallas_call(
+        body,
+        in_specs=[SMEM_SPEC] * len(smem) + [VMEM_SPEC] * len(arrays),
+        out_specs=VMEM_SPEC,
+        out_shape=jax.ShapeDtypeStruct(shape, jnp.float32),
+        compiler_params=PARAMS,
+        name=name,
+    )(*smem, *arrays)
 
 
 def store_parts(parts_ref, where, value):
@@ -175,6 +289,39 @@
             for spot in range(HALO - reach, HALO + OWN + reach):
                 waves[layer, :, lanes(spot, spot + 1)] = tile_product(parts, packed, layer, spot)
         out[...] = waves[GROUP - 1, :, lanes(HALO, HALO + OWN)]
+
+
+def pair_body(ids, low, mid, high, window, packed, _, *refs, turn, first):
+    outs, waves, parts = refs[:-2], refs[-2], refs[-1]
+
+    @pl.when(ids[0] == turn)
+    def _():
+        for layer in (first, first + 1):
+            if layer == 0:
+                pieces = [
+                    (lanes(2, 4), low[:, lanes(2, 4)]),
+                    (lanes(4, 8), mid[...]),
+                    (lanes(8, 10), high[:, lanes(0, 2)]),
+                ]
+            elif layer == 2:
+                waves[1, :, lanes(1, 3)] = low[...]
+                waves[1, :, lanes(7, 9)] = high[...]
+                pieces = [(lanes(2, 10), waves[1, :, lanes(1, 9)])]
+            else:
+                pieces = [(lanes(3, 9), waves[layer - 1, :, lanes(2, 8)])]
+            for where, value in pieces:
+                forcing = window[layer, 0:16, where]
+                coef_real = window[layer, 16:17, where]
+                coef_imag = window[layer, 17:18, where]
+                store_parts(parts, where, forcing + scaled(coef_real, coef_imag, value))
+            reach = first + 1 - layer
+            for spot in range(HALO - reach, HALO + OWN + reach):
+                waves[layer, :, lanes(spot, spot + 1)] = tile_product(parts, packed, layer, spot)
+        if first:
+            outs[0][...] = waves[3, :, lanes(HALO, HALO + OWN)]
+        else:
+            outs[0][...] = waves[1, :, lanes(HALO, HALO + 2)]
+            outs[1][...] = waves[1, :, lanes(HALO + 2, HALO + OWN)]
 
 
 def up_body(ids, low, mid, high, window, packed, waves, left, right, _, out, field, parts, span, *, turn):
@@ -222,6 +369,21 @@
     )(ids, *received, window, packed, waves)
 
 
+def pair_step(ids, low, mid, high, window, packed, waves, turn, first):
+    widths = (HALF,) if first else (2 * TILE, 2 * TILE)
+    return pl.pallas_call(
+        functools.partial(pair_body, turn=turn, first=first),
+        in_specs=[SMEM_SPEC] + [VMEM_SPEC] * 6,
+        out_specs=(VMEM_SPEC,) * (len(widths) + 1),
+        out_shape=tuple(jax.ShapeDtypeStruct((16, width), jnp.float32) for width in widths)
+        + (jax.ShapeDtypeStruct((GROUP, 16, SPAN), jnp.float32),),
+        scratch_shapes=[PARTS],
+        input_output_aliases={6: len(widths)},
+        compiler_params=PARAMS,
+        name=f"pair_{turn}_{first}",
+    )(ids, low, mid, high, window, packed, waves)
+
+
 def up_step(ids, received, window, packed, waves, left, right, field, turn):
     return pl.pallas_call(
         functools.partial(up_body, turn=turn),
@@ -238,6 +400,82 @@
     )(ids, *received, window, packed, waves, left, right, field)
 
 
+def give_body(ids, waves, field, give):
+    own = slice(HALO * TILE, (HALO + OWN) * TILE)
+    for side in range(2):
+
+        @pl.when(ids[1] == side)
+        def _():
+            partner = slice(2 - 2 * side, 4 - 2 * side)
+            give[0] = waves[partner, :, own]
+            give[1] = field[partner]
+
+
+def join_body(ids, waves, field, taken, out_waves, out_field):
+    for side in range(2):
+
+        @pl.when(ids[1] == side)
+        def _():
+            mine = slice(HALF * side, HALF * (side + 1))
+            partner = slice(HALF * (1 - side), HALF * (2 - side))
+            for layer in range(2):
+                for part in range(2):
+                    rows = slice(8 * part, 8 * (part + 1))
+                    own = slice(HALO * TILE, (HALO + OWN) * TILE)
+                    out_waves[part, layer, :, mine] = waves[2 * side + layer, rows, own]
+                    out_field[part, layer, :, mine] = field[2 * side + layer, rows]
+                    out_waves[part, layer, :, partner] = taken[0, layer, rows]
+                    out_field[part, layer, :, partner] = taken[1, layer, rows]
+
+
+def join(ids, waves, field, taken, shape):
+    return pl.pallas_call(
+        join_body,
+        in_specs=[SMEM_SPEC] + [VMEM_SPEC] * 3,
+        out_specs=(VMEM_SPEC,) * 2,
+        out_shape=(jax.ShapeDtypeStruct(shape, jnp.float32),) * 2,
+        compiler_params=PARAMS,
+        name="join",
+    )(ids, waves, field, taken)
+
+
+PAIR_ROWS = 2
+LATE_ROWS = 5
+FIRST_RUNS = (
+    (((0, 7, 8),), ((0, 0, 1),)),
+    (((2, 0, 1),), ((2, 7, 8),)),
+)
+FIRST_SLOTS = (((0, 2), (2, 2)), ((2, 7), (0, 7)))
+DOWN_RUNS = (
+    (((0, 5, 8),), ((0, 0, 3),)),
+    (((1, 0, 2), (2, 0, 1)), ((1, 6, 8), (2, 7, 8))),
+)
+DOWN_SLOTS = (
+    ((0, 0), (0, 1), (0, 2), (1, 1), (1, 2), (2, 2)),
+    ((1, 7), (1, 8), (2, 7), (0, 7), (0, 8), (0, 9)),
+)
+EARLY_RUNS = (
+    (((3, 7, 8), (2, 6, 7)), ((3, 0, 1), (2, 1, 2))),
+    (((3, 1, 3),), ((3, 5, 7),)),
+)
+EARLY_SLOTS = (
+    ((3, 2), (2, 1), (3, 0), (3, 1)),
+    ((3, 8), (3, 9), (3, 7), (2, 8)),
+)
+EXTRA_RUNS = (
+    (((1, 7, 8), (2, 6, 7)), ((1, 0, 1), (2, 1, 2))),
+    (((3, 1, 3),), ((3, 5, 7),)),
+)
+EXTRA_SLOTS = (
+    ((1, 2), (2, 1), (3, 0), (3, 1)),
+    ((3, 8), (3, 9), (1, 7), (2, 8)),
+)
+
+
+def gated(value, *others):
+    return lax.optimization_barrier((value, *others))[0]
+
+
 def shards(rhs_field, src_cell, src_layer, factor, couple):
     layer_total, shot_count, strip_cells = rhs_field.shape[1:]
     depth_count, lat_count = lax.axis_size("depth"), lax.axis_size("lat")
@@ -246,7 +484,8 @@
     first_core = core == 0
     chip_rows = depth_count // 2
     halves = 2 * lat_count
-    ids = jnp.stack([depth_pos // 2, core]).astype(jnp.int32)
+    everyone = range(chip_rows)
+    ids = jnp.stack([depth_pos // 2, core, lat_pos, depth_pos]).astype(jnp.int32)
 
     def device(row, half):
         return (2 * row + half % 2) * lat_count + half // 2
@@ -266,100 +505,99 @@
 
     partner = [(at(d, l), at(d ^ 1, l)) for d in range(depth_count) for l in range(lat_count)]
 
-    def outward(value, sender, right):
-        target, shift = (0, 1) if right else (1, -1)
-        pairs = [
-            (at(2 * row + sender, l), at(2 * row + target, l + shift))
-            for row in range(chip_rows)
-            for l in range(lat_count)
-            if 0 <= l + shift < lat_count
-        ]
-        return lax.ppermute(value, AXES, pairs)
-
-    other = lax.ppermute(factor, AXES, partner)
-    tiles = factor.shape[1]
-    two_right = jnp.concatenate([factor[0, tiles - 3 :], factor[1, tiles - 2 :]])
-    two_left = jnp.concatenate([factor[0, :3], factor[1, :2]])
-    near_down = (
-        outward(two_right, 0, True),
-        outward(two_left, 0, False),
-        outward(factor[0, tiles - 1 :], 1, True),
-        outward(factor[0, :1], 1, False),
-    )
-    four_right = jnp.concatenate([factor[1, tiles - 3 :], factor[0, tiles - 2 : tiles - 1]])
-    four_left = jnp.concatenate([factor[1, :3], factor[0, 1:2]])
-
-    layer_ids = depth_pos * layer_total + jnp.arange(layer_total, dtype=jnp.int32)
-    cell_ids = lat_pos * strip_cells + jnp.arange(strip_cells, dtype=jnp.int32)
-    hit = (src_layer[None, :, None] == layer_ids[:, None, None]) & (
-        src_cell[None, :, None] == cell_ids[None, None, :]
-    )
-    real_part = rhs_field[0] + 4.0 * hit.astype(jnp.float32)
-    rows = jnp.concatenate(
-        [real_part, rhs_field[1]] + [couple[way, part][:, None] for way in range(2) for part in range(2)],
-        axis=1,
+    def beside_pairs(rows, same):
+        pairs = []
+        for row in rows:
+            for side in range(2):
+                shift = 1 if (side == 0) == same else -1
+                target = side if same else 1 - side
+                pairs += [
+                    (at(2 * row + side, l), at(2 * row + target, l + shift))
+                    for l in range(lat_count)
+                    if 0 <= l + shift < lat_count
+                ]
+        return pairs
+
+    def send_halo(ids, other, parts, name):
+        straight, cross = cut(ids, factor, other, parts, name)
+        rows = [row for begin, end, _ in parts for row in range(begin, end)]
+        return straight, (
+            lax.ppermute(straight, AXES, beside_pairs(rows, True)),
+            lax.ppermute(cross, AXES, beside_pairs(rows, False)),
+        )
+
+    first_cut, first_halo = send_halo(ids, factor, ((0, PAIR_ROWS, FIRST_RUNS),), "cut_first")
+    other = lax.ppermute(gated(factor, first_cut), AXES, partner)
+
+    rows = small_call(
+        rows_body, (ids, src_cell, src_layer), (rhs_field, couple), (layer_total, ROWS, strip_cells), "rows"
     )
     rows_other = lax.ppermute(rows, AXES, partner)
-    chip = jnp.concatenate(
-        [jnp.where(first_core, rows, rows_other), jnp.where(first_core, rows_other, rows)]
-    )
-    edge = jnp.where(first_core, chip[..., HALF:], chip[..., :HALF])
-    straight = [(at(2 * r, l), at(2 * r, l + 1)) for r in range(chip_rows) for l in range(lat_count - 1)] + [
-        (at(2 * r + 1, l), at(2 * r + 1, l - 1)) for r in range(chip_rows) for l in range(1, lat_count)
-    ]
-    beside = lax.ppermute(edge, AXES, straight)
-    window = jnp.where(
-        first_core,
-        jnp.concatenate([beside, chip], axis=-1),
-        jnp.concatenate([chip, beside], axis=-1),
-    )
-
-    packed = pack_chip(ids, factor, None, True)
+    edge = small_call(edge_body, (ids,), (rows, rows_other), (GROUP, ROWS, HALF), "edge")
+    packed = pack_chip(gated(ids, rows), factor, None, True)
+    other, packed = lax.optimization_barrier((other, packed, edge))[:2]
+    beside = lax.ppermute(edge, AXES, beside_pairs(everyone, True))
+    window = small_call(
+        window_body, (ids,), (rows, rows_other, beside), (GROUP, ROWS, WINDOW), "window"
+    )
+    down_parts = ((PAIR_ROWS, chip_rows, DOWN_RUNS),)
+    early_parts = ((LATE_ROWS, chip_rows, EARLY_RUNS), (0, PAIR_ROWS, EXTRA_RUNS))
+    late_parts = ((0, LATE_ROWS, EARLY_RUNS),)
+    _, halo = send_halo(gated(ids, beside), other, down_parts, "cut_down")
     packed = pack_chip(ids, other, packed, False)
-    down_places = (
-        (((0, 0), (0, 1), (0, 2), (1, 1), (1, 2)), ((0, 7), (0, 8), (0, 9), (1, 7), (1, 8))),
-        (((2, 2),), ((2, 7),)),
-    )
-    packed = pack_halo(ids, near_down, packed, down_places, "halo_down")
+    packed = pack_halo(
+        gated(ids, window), first_halo, packed, (0, PAIR_ROWS), FIRST_SLOTS, "halo_first"
+    )
 
     zero_half = jnp.zeros((2 * shot_count, HALF), jnp.float32)
     waves = jnp.zeros((GROUP, 2 * shot_count, SPAN), jnp.float32)
     field = jnp.zeros((GROUP, 2 * shot_count, HALF), jnp.float32)
 
     received = (zero_half,) * 3
-    for turn in range(chip_rows):
-        out, waves = down_step(ids, received, window, packed, waves, turn)
+    for turn in everyone:
+        if turn < PAIR_ROWS:
+            left_edge, right_edge, waves = pair_step(
+                ids, *received, window, packed, waves, turn, 0
+            )
+            pairs = range(PAIR_ROWS)
+            low, high = hop(right_edge, pairs, 0, 1), hop(left_edge, pairs, 0, -1)
+            out, waves = pair_step(ids, low, left_edge, high, window, packed, waves, turn, 2)
+            if turn + 1 == PAIR_ROWS:
+                down_rows = (PAIR_ROWS, chip_rows)
+                packed = pack_halo(gated(ids, out), halo, packed, down_rows, DOWN_SLOTS, "halo_down")
+                _, halo = send_halo(gated(ids, out, *halo), other, early_parts, "cut_early")
+                out, packed = lax.optimization_barrier((out, packed))
+        else:
+            out, waves = down_step(ids, received, window, packed, waves, turn)
+            if turn + 1 == LATE_ROWS:
+                late_ids = gated(ids, out)
+                early_rows, first_rows = (LATE_ROWS, chip_rows), (0, PAIR_ROWS)
+                packed = pack_halo(late_ids, halo, packed, early_rows, EARLY_SLOTS, "halo_early")
+                packed = pack_halo(late_ids, halo, packed, first_rows, EXTRA_SLOTS, "halo_extra")
+                out, packed = lax.optimization_barrier((out, packed))
+            if turn == LATE_ROWS:
+                _, halo = send_halo(gated(ids, out), other, late_parts, "cut_late")
         if turn + 1 < chip_rows:
             group = range(turn % 3, chip_rows, 3)
             received = (hop(out, group, 1, 1), hop(out, group, 1, 0), hop(out, group, 1, -1))
 
-    near_up = (outward(four_right, 1, True), outward(four_left, 1, False))
-    up_places = (
-        (((3, 0), (3, 1), (3, 2), (2, 1)), ((3, 7), (3, 8), (3, 9), (2, 8))),
-        ((), ()),
-    )
-    packed = pack_halo(ids, near_up + near_up, packed, up_places, "halo_up")
-
     deep = waves[2:, :, HALO * TILE : (HALO + OWN) * TILE]
-    everyone = range(chip_rows)
     left, right = hop(deep, everyone, 0, 1), hop(deep, everyone, 0, -1)
     received = (zero_half,) * 3
-    for turn in reversed(range(chip_rows)):
+    for turn in reversed(everyone):
         out, field = up_step(ids, received, window, packed, waves, left, right, field, turn)
+        if turn == LATE_ROWS:
+            packed = pack_halo(gated(ids, out), halo, packed, (0, LATE_ROWS), EARLY_SLOTS, "halo_late")
+            out, packed = lax.optimization_barrier((out, packed))
         if turn:
             group = range(turn % 3, chip_rows, 3)
             received = (hop(out, group, -1, 1), hop(out, group, -1, 0), hop(out, group, -1, -1))
 
-    own_waves = waves[:, :, HALO * TILE : (HALO + OWN) * TILE]
-    both = jnp.stack([own_waves, field])
-    keep = jnp.where(first_core, both[:, :2], both[:, 2:])
-    give = jnp.where(first_core, both[:, 2:], both[:, :2])
+    shape = (2, layer_total, 2 * shot_count, HALF)
+    waves = gated(waves, field)
+    give = small_call(give_body, (ids,), (waves, field), shape, "give")
     taken = lax.ppermute(give, AXES, partner)
-    whole = jnp.concatenate(
-        [jnp.where(first_core, keep, taken), jnp.where(first_core, taken, keep)], axis=-1
-    )
-    whole = whole.reshape(2, layer_total, 2, shot_count, strip_cells).transpose(0, 2, 1, 3, 4)
-    return (whole[0], whole[1])
+    return join(ids, waves, field, taken, rhs_field.shape)
 
 
 def solution(mesh):

time: 277 us -> 241 us (0.87)
  starting transfers between devices: 130 us -> 100 us
  Pallas kernels: 32.3 us -> 39.8 us
  local copies, waits for them, and re-layouts: 10.4 us -> 3.01 us
  other arithmetic: 7.04 us -> 0.08 us
    ppermute x8 -> x10, starting transfers between devices: 46.1 us -> 26 us  [the longest x4 18.6 us: send_halo(): lax.ppermute(cross, AXES, beside_pairs(rows, False))]
    pallas_call x2 -> x18, Pallas kernels: 5.42 us -> 19.1 us  [the longest x4 6.31 us: cut(): pl.pallas_call(functools.partial(cut_body, parts=parts), in_specs=[SMEM_S...]
    ppermute x44 -> x48, waiting for transfers between devices: 80.6 us -> 67.3 us  [hop(): return lax.ppermute(value, AXES, pairs)]
    squeeze x5 -> x0, local copies, waits for them, and re-layouts: 7.42 us -> none  [the longest x2 4.29 us: shards(): two_left = jnp.concatenate([factor[0, :3], factor[1, :2]])]
    ppermute x8 -> x10, waiting for transfers between devices: 13 us -> 20.3 us  [the longest x4 20.1 us: send_halo(): lax.ppermute(cross, AXES, beside_pairs(rows, False))]
    ppermute x1, waiting for transfers between devices: 0.01 us -> 6.42 us  [shards(): rows_other = lax.ppermute(rows, AXES, partner)]
    ppermute x44 -> x48, starting transfers between devices: 79.5 us -> 73.8 us  [hop(): return lax.ppermute(value, AXES, pairs)]
    concatenate x4 -> x0, other arithmetic: 5.46 us -> none  [the longest x1 1.47 us: shards(): two_right = jnp.concatenate([factor[0, tiles - 3:], factor[1, tiles - 2:]])]
  transfers between devices with their start and end apart: 54 -> 60, of which waited for: 15 -> 19; matrix products, arithmetic and copies ran while one was open for 5% -> 0% of each run, Pallas kernels for 9% -> 9%
where the time goes in v2:
time: 241 us; the launch traced here: 240 us
  starting transfers between devices  100 us (41%)
  waiting for transfers between devices  95.3 us (40%)
  Pallas kernels  39.8 us (17%)
  local copies, waits for them, and re-layouts  3.01 us (1%)
    ppermute x48, starting transfers between devices, hop(): return lax.ppermute(value, AXES, pairs)  73.8 us
    ppermute x48, waiting for transfers between devices, hop(): return lax.ppermute(value, AXES, pairs)  67.3 us
    ppermute x4, waiting for transfers between devices, send_halo(): lax.ppermute(cross, AXES, beside_pairs(rows, False))  20.1 us
    ppermute x4, starting transfers between devices, send_halo(): lax.ppermute(cross, AXES, beside_pairs(rows, False))  18.6 us
    pallas_call x2, Pallas kernels, pack_chip(): pl.pallas_call(functools.partial(chip_body, mine=mine), in_specs=[SMEM_SP...  9.58 us
    pallas_call x8, Pallas kernels, up_step(): pl.pallas_call(functools.partial(up_body, turn=turn), in_specs=[SMEM_SPEC...  7.08 us
    ppermute x1, waiting for transfers between devices, shards(): rows_other = lax.ppermute(rows, AXES, partner)  6.42 us
    pallas_call x4, Pallas kernels, cut(): pl.pallas_call(functools.partial(cut_body, parts=parts), in_specs=[SMEM_S...  6.31 us
  transfers between devices with their start and end apart: 60, of which 19 were waited for; matrix products, arithmetic and copies ran while one was open for 0% of the time, Pallas kernels for 9%

profile of v2, /device:TPU:1, one launch (start us, length us, event | category | flops | bytes accessed | tf_op | source)
XLA Modules:
  0.0 239.9 jit_solution(8616557886840945997)
XLA Ops:
  0.7 1.7 cut_first.1
  7.6 6.4 %collective-permute-done.other = f32[2,20,1024]{2,1,0:T(8,128)S(1)} collective-permute-done((f32[2,20,1024]{2,1,0:T(8,128)S(1)}, f32[2,20,1024]{2,1,0:T(8,128)S(1)}, u32[]{:S(2)}, u32[]{:S(2)}) %collective-permute-start) | collective-permute-done | bytes 163872 | tf_op jit(solution)/shard_map/ppermute | solution.py:535
  15.9 5.2 %pack_mine.1.refs_0_ = bf16[4,10,384,512]{3,2,1,0:T(8,128)(2,1)S(1)} custom-call(s32[4]{0:T(128)S(1)} %pad_add_fusion.ids, f32[2,8,3,2,128,128]{5,4,3,2,1,0:T(8,128)} %mine.7), custom_call_target="tpu_custom_call" | custom-call | tf_op jit(solution)/shard_map/pack_mine/pallas_call | solution.py:122
  24.7 8.0 %collective-permute-start.3 = (f32[1,3,2,128,128]{4,3,2,1,0:T(8,128)S(1)}, f32[1,3,2,128,128]{4,3,2,1,0:T(8,128)S(1)}, u32[]{:S(2)}, u32[]{:S(2)}) collective-permute-start(f32[1,3,2,128,128]{4,3,2,1,0:T(8,128)S(1)} %get-tuple-element.66), channel_id=1, source_target_pairs={{1,8},{2,9},{3,10},{4,11},{5,12},{6,13},{7,14},{8,1},{9,2},{10,3},... | collective-permute-start | bytes 1179656 | tf_op jit(solution)/shard_map/ppermute | solution.py:526
  33.3 4.4 %pack_partner.1.refs_0_ = bf16[4,10,384,512]{3,2,1,0:T(8,128)(2,1)S(1)} custom-call(s32[4]{0:T(128)S(1)} %pad_add_fusion.ids, f32[2,8,3,2,128,128]{5,4,3,2,1,0:T(8,128)S(1)} %collective-permute-done.4.source.other, bf16[4,10,384,512]{3,2,1,0:T(8,128)(2,1)S(1)} %pack_mine.1.refs_0_), custom_call_target="tpu_custom_call", output_to_operand_aliasing={{}: (2, {})} | custom-call | tf_op jit(solution)/shard_map/pack_partner/pallas_call | solution.py:122
  37.7 8.4 %collective-permute-done.3.cross = f32[1,3,2,128,128]{4,3,2,1,0:T(8,128)S(1)} collective-permute-done((f32[1,3,2,128,128]{4,3,2,1,0:T(8,128)S(1)}, f32[1,3,2,128,128]{4,3,2,1,0:T(8,128)S(1)}, u32[]{:S(2)}, u32[]{:S(2)}) %collective-permute-start.3) | collective-permute-done | bytes 393248 | tf_op jit(solution)/shard_map/ppermute | solution.py:526
  48.5 4.3 %collective-permute-start.5 = (f32[16,256]{1,0:T(8,128)S(1)}, f32[16,256]{1,0:T(8,128)S(1)}, u32[]{:S(2)}, u32[]{:S(2)}) collective-permute-start(f32[16,256]{1,0:T(8,128)S(1)} %get-tuple-element.71), channel_id=1, source_target_pairs={{0,8},{8,1},{1,9},{9,2},{2,10},{10,3},{3,11},{11,4},{4,12},{12,5},... | collective-permute-start | bytes 49160 | tf_op jit(solution)/shard_map/ppermute | solution.py:504
  52.8 1.9 collective-permute-start.6
  54.8 3.1 %collective-permute-done.6.high = f32[16,256]{1,0:T(8,128)S(1)} collective-permute-done((f32[16,256]{1,0:T(8,128)S(1)}, f32[16,256]{1,0:T(8,128)S(1)}, u32[]{:S(2)}, u32[]{:S(2)}) %collective-permute-start.6) | collective-permute-done | bytes 16416 | tf_op jit(solution)/shard_map/ppermute | solution.py:504
  65.1 3.9 %collective-permute-start.10 = (f32[16,256]{1,0:T(8,128)S(1)}, f32[16,256]{1,0:T(8,128)S(1)}, u32[]{:S(2)}, u32[]{:S(2)}) collective-permute-start(f32[16,256]{1,0:T(8,128)S(1)} %get-tuple-element.76), channel_id=1, source_target_pairs={{0,8},{8,1},{1,9},{9,2},{2,10},{10,3},{3,11},{11,4},{4,12},{12,5},... | collective-permute-start | bytes 49160 | tf_op jit(solution)/shard_map/ppermute | solution.py:504
  69.0 1.9 collective-permute-start.11
  71.0 3.1 %collective-permute-done.11.high = f32[16,256]{1,0:T(8,128)S(1)} collective-permute-done((f32[16,256]{1,0:T(8,128)S(1)}, f32[16,256]{1,0:T(8,128)S(1)}, u32[]{:S(2)}, u32[]{:S(2)}) %collective-permute-start.11) | collective-permute-done | bytes 16416 | tf_op jit(solution)/shard_map/ppermute | solution.py:504
  74.7 2.0 cut_early.1
  78.0 5.5 %collective-permute-start.24 = (f32[2,3,2,128,128]{4,3,2,1,0:T(8,128)S(1)}, f32[2,3,2,128,128]{4,3,2,1,0:T(8,128)S(1)}, u32[]{:S(2)}, u32[]{:S(2)}) collective-permute-start(f32[2,3,2,128,128]{4,3,2,1,0:T(8,128)S(1)} %get-tuple-element.95), channel_id=1, source_target_pairs={{81,88},{82,89},{83,90},{84,91},{85,92},{86,93},{87,94},{88,81},{8... | collective-permute-start | bytes 2359304 | tf_op jit(solution)/shard_map/ppermute | solution.py:526
  89.3 9.5 %collective-permute-start.20 = (f32[16,512]{1,0:T(8,128)S(1)}, f32[16,512]{1,0:T(8,128)S(1)}, u32[]{:S(2)}, u32[]{:S(2)}) collective-permute-start(f32[16,512]{1,0:T(8,128)S(1)} %get-tuple-element.89), channel_id=1, source_target_pairs={{0,24},{8,17},{1,25},{9,18},{2,26},{10,19},{3,27},{11,20},{4,28},{... | collective-permute-start | bytes 98312 | tf_op jit(solution)/shard_map/ppermute | solution.py:504
  103.0 11.7 %collective-permute-done.24.cross = f32[2,3,2,128,128]{4,3,2,1,0:T(8,128)S(1)} collective-permute-done((f32[2,3,2,128,128]{4,3,2,1,0:T(8,128)S(1)}, f32[2,3,2,128,128]{4,3,2,1,0:T(8,128)S(1)}, u32[]{:S(2)}, u32[]{:S(2)}) %collective-permute-start.24) | collective-permute-done | bytes 786464 | tf_op jit(solution)/shard_map/ppermute | solution.py:526
  115.2 1.7 halo_extra.1.packed.refs_0_
  119.7 2.0 cut_late.1
  123.0 4.4 %collective-permute-start.43 = (f32[2,3,2,128,128]{4,3,2,1,0:T(8,128)S(1)}, f32[2,3,2,128,128]{4,3,2,1,0:T(8,128)S(1)}, u32[]{:S(2)}, u32[]{:S(2)}) collective-permute-start(f32[2,3,2,128,128]{4,3,2,1,0:T(8,128)S(1)} %get-tuple-element.112), channel_id=1, source_target_pairs={{1,8},{2,9},{3,10},{4,11},{5,12},{6,13},{7,14},{8,1},{9,2},{10,3},... | collective-permute-start | bytes 2359304 | tf_op jit(solution)/shard_map/ppermute | solution.py:526
  130.0 7.5 %collective-permute-start.31 = (f32[16,512]{1,0:T(8,128)S(1)}, f32[16,512]{1,0:T(8,128)S(1)}, u32[]{:S(2)}, u32[]{:S(2)}) collective-permute-start(f32[16,512]{1,0:T(8,128)S(1)} %get-tuple-element.101), channel_id=1, source_target_pairs={{0,24},{8,17},{1,25},{9,18},{2,26},{10,19},{3,27},{11,20},{4,28},{... | collective-permute-start | bytes 98312 | tf_op jit(solution)/shard_map/ppermute | solution.py:504
  137.5 1.6 collective-permute-start.32
  142.5 5.4 %collective-permute-start.34 = (f32[2,16,512]{2,1,0:T(8,128)S(1)}, f32[2,16,512]{2,1,0:T(8,128)S(1)}, u32[]{:S(2)}, u32[]{:S(2)}) collective-permute-start(f32[2,16,512]{2,1,0:T(8,128)S(1)} %slice.3), channel_id=1, source_target_pairs={{0,8},{8,1},{1,9},{9,2},{2,10},{10,3},{3,11},{11,4},{4,12},{12,5},... | collective-permute-start | bytes 196616 | tf_op jit(solution)/shard_map/ppermute | solution.py:504
  148.0 1.9 collective-permute-start.35
  149.9 13.0 %collective-permute-done.34.left = f32[2,16,512]{2,1,0:T(8,128)S(1)} collective-permute-done((f32[2,16,512]{2,1,0:T(8,128)S(1)}, f32[2,16,512]{2,1,0:T(8,128)S(1)}, u32[]{:S(2)}, u32[]{:S(2)}) %collective-permute-start.34) | collective-permute-done | bytes 65568 | tf_op jit(solution)/shard_map/ppermute | solution.py:504
  168.7 4.3 %collective-permute-done.37.mid = f32[16,512]{1,0:T(8,128)S(1)} collective-permute-done((f32[16,512]{1,0:T(8,128)S(1)}, f32[16,512]{1,0:T(8,128)S(1)}, u32[]{:S(2)}, u32[]{:S(2)}) %collective-permute-start.37) | collective-permute-done | bytes 32800 | tf_op jit(solution)/shard_map/ppermute | solution.py:504
  173.0 3.4 %collective-permute-done.38.high = f32[16,512]{1,0:T(8,128)S(1)} collective-permute-done((f32[16,512]{1,0:T(8,128)S(1)}, f32[16,512]{1,0:T(8,128)S(1)}, u32[]{:S(2)}, u32[]{:S(2)}) %collective-permute-start.38) | collective-permute-done | bytes 32800 | tf_op jit(solution)/shard_map/ppermute | solution.py:504
  179.6 1.7 halo_late.1.packed
  188.0 15.5 %collective-permute-done.47.low = f32[16,512]{1,0:T(8,128)S(1)} collective-permute-done((f32[16,512]{1,0:T(8,128)S(1)}, f32[16,512]{1,0:T(8,128)S(1)}, u32[]{:S(2)}, u32[]{:S(2)}) %collective-permute-start.47) | collective-permute-done | bytes 32800 | tf_op jit(solution)/shard_map/ppermute | solution.py:504
  204.1 3.4 %collective-permute-done.49.high = f32[16,512]{1,0:T(8,128)S(1)} collective-permute-done((f32[16,512]{1,0:T(8,128)S(1)}, f32[16,512]{1,0:T(8,128)S(1)}, u32[]{:S(2)}, u32[]{:S(2)}) %collective-permute-start.49) | collective-permute-done | bytes 32800 | tf_op jit(solution)/shard_map/ppermute | solution.py:504
  217.2 13.6 %collective-permute-done.56.low = f32[16,512]{1,0:T(8,128)S(1)} collective-permute-done((f32[16,512]{1,0:T(8,128)S(1)}, f32[16,512]{1,0:T(8,128)S(1)}, u32[]{:S(2)}, u32[]{:S(2)}) %collective-permute-start.56) | collective-permute-done | bytes 32800 | tf_op jit(solution)/shard_map/ppermute | solution.py:504
  230.9 2.7 %collective-permute-done.58.high = f32[16,512]{1,0:T(8,128)S(1)} collective-permute-done((f32[16,512]{1,0:T(8,128)S(1)}, f32[16,512]{1,0:T(8,128)S(1)}, u32[]{:S(2)}, u32[]{:S(2)}) %collective-permute-start.58) | collective-permute-done | bytes 32800 | tf_op jit(solution)/shard_map/ppermute | solution.py:504
  233.6 3.0 %up_0.1 = (f32[16,512]{1,0:T(8,128)}, f32[4,16,512]{2,1,0:T(8,128)S(1)}) custom-call(s32[4]{0:T(128)S(1)} %pad_add_fusion.ids, f32[16,512]{1,0:T(8,128)S(1)} %collective-permute-done.56.low, f32[16,512]{1,0:T(8,128)S(1)} %collective-permute-done.57.mid, f32[16,512]{1,0:T(8,128)S(1)} %collective-permute-done.58.high, ...), custom_call_target="tpu_custom_call", output_to_operand_aliasing={{1}: (9, {})} | custom-call | tf_op jit(solution)/shard_map/up_0/pallas_call | solution.py:388
  (135 shorter events, 72.0 us)
Async XLA Ops:
  2.4 18.8 %collective-permute-start.4 = (f32[2,8,3,2,128,128]{5,4,3,2,1,0:T(8,128)}, f32[2,8,3,2,128,128]{5,4,3,2,1,0:T(8,128)S(1)}, u32[]{:S(2)}, u32[]{:S(2)}) collective-permute-start(f32[2,8,3,2,128,128]{5,4,3,2,1,0:T(8,128)} %mine.7), channel_id=1, source_target_pairs={{0,8},{1,9},{2,10},{3,11},{4,12},{5,13},{6,14},{7,15},{8,0},{9,1},... | collective-permute-start | bytes 18874376 | tf_op jit(solution)/shard_map/ppermute | solution.py:530
  7.5 6.5 %collective-permute-start = (f32[2,20,1024]{2,1,0:T(8,128)S(1)}, f32[2,20,1024]{2,1,0:T(8,128)S(1)}, u32[]{:S(2)}, u32[]{:S(2)}) collective-permute-start(f32[2,20,1024]{2,1,0:T(8,128)S(1)} %rows.1), channel_id=1, source_target_pairs={{0,8},{1,9},{2,10},{3,11},{4,12},{5,13},{6,14},{7,15},{8,0},{9,1},... | collective-permute-start | bytes 491528 | tf_op jit(solution)/shard_map/ppermute | solution.py:535
  14.6 6.7 %collective-permute-start.1 = (f32[4,20,512]{2,1,0:T(8,128)S(1)}, f32[4,20,512]{2,1,0:T(8,128)S(1)}, u32[]{:S(2)}, u32[]{:S(2)}) collective-permute-start(f32[4,20,512]{2,1,0:T(8,128)S(1)} %edge.1), channel_id=1, source_target_pairs={{0,1},{1,2},{2,3},{3,4},{4,5},{5,6},{6,7},{9,8},{10,9},{11,10},{12... | collective-permute-start | bytes 491528 | tf_op jit(solution)/shard_map/ppermute | solution.py:539
  21.9 52.8 %collective-permute-start.12 = (f32[3,3,2,128,128]{4,3,2,1,0:T(8,128)S(1)}, f32[3,3,2,128,128]{4,3,2,1,0:T(8,128)S(1)}, u32[]{:S(2)}, u32[]{:S(2)}) collective-permute-start(f32[3,3,2,128,128]{4,3,2,1,0:T(8,128)S(1)} %get-tuple-element.82), channel_id=1, source_target_pairs={{32,33},{33,34},{34,35},{35,36},{36,37},{37,38},{38,39},{41,40},{4... | collective-permute-start | bytes 3538952 | tf_op jit(solution)/shard_map/ppermute | solution.py:525
  22.6 52.0 %collective-permute-start.13 = (f32[3,3,2,128,128]{4,3,2,1,0:T(8,128)S(1)}, f32[3,3,2,128,128]{4,3,2,1,0:T(8,128)S(1)}, u32[]{:S(2)}, u32[]{:S(2)}) collective-permute-start(f32[3,3,2,128,128]{4,3,2,1,0:T(8,128)S(1)} %get-tuple-element.83), channel_id=1, source_target_pairs={{33,40},{34,41},{35,42},{36,43},{37,44},{38,45},{39,46},{40,33},{4... | collective-permute-start | bytes 3538952 | tf_op jit(solution)/shard_map/ppermute | solution.py:526
  23.4 14.3 %collective-permute-start.2 = (f32[1,3,2,128,128]{4,3,2,1,0:T(8,128)S(1)}, f32[1,3,2,128,128]{4,3,2,1,0:T(8,128)S(1)}, u32[]{:S(2)}, u32[]{:S(2)}) collective-permute-start(f32[1,3,2,128,128]{4,3,2,1,0:T(8,128)S(1)} %get-tuple-element.65), channel_id=1, source_target_pairs={{0,1},{1,2},{2,3},{3,4},{4,5},{5,6},{6,7},{9,8},{10,9},{11,10},{12... | collective-permute-start | bytes 1179656 | tf_op jit(solution)/shard_map/ppermute | solution.py:525
  24.7 21.4 %collective-permute-start.3 = (f32[1,3,2,128,128]{4,3,2,1,0:T(8,128)S(1)}, f32[1,3,2,128,128]{4,3,2,1,0:T(8,128)S(1)}, u32[]{:S(2)}, u32[]{:S(2)}) collective-permute-start(f32[1,3,2,128,128]{4,3,2,1,0:T(8,128)S(1)} %get-tuple-element.66), channel_id=1, source_target_pairs={{1,8},{2,9},{3,10},{4,11},{5,12},{6,13},{7,14},{8,1},{9,2},{10,3},... | collective-permute-start | bytes 1179656 | tf_op jit(solution)/shard_map/ppermute | solution.py:526
  48.5 6.2 %collective-permute-start.5 = (f32[16,256]{1,0:T(8,128)S(1)}, f32[16,256]{1,0:T(8,128)S(1)}, u32[]{:S(2)}, u32[]{:S(2)}) collective-permute-start(f32[16,256]{1,0:T(8,128)S(1)} %get-tuple-element.71), channel_id=1, source_target_pairs={{0,8},{8,1},{1,9},{9,2},{2,10},{10,3},{3,11},{11,4},{4,12},{12,5},... | collective-permute-start | bytes 49160 | tf_op jit(solution)/shard_map/ppermute | solution.py:504
  52.8 5.1 %collective-permute-start.6 = (f32[16,256]{1,0:T(8,128)S(1)}, f32[16,256]{1,0:T(8,128)S(1)}, u32[]{:S(2)}, u32[]{:S(2)}) collective-permute-start(f32[16,256]{1,0:T(8,128)S(1)} %get-tuple-element.72.mid), channel_id=1, source_target_pairs={{8,0},{1,8},{9,1},{2,9},{10,2},{3,10},{11,3},{4,11},{12,4},{5,12},... | collective-permute-start | bytes 49160 | tf_op jit(solution)/shard_map/ppermute | solution.py:504
  59.1 4.4 %collective-permute-start.7 = (f32[16,512]{1,0:T(8,128)S(1)}, f32[16,512]{1,0:T(8,128)S(1)}, u32[]{:S(2)}, u32[]{:S(2)}) collective-permute-start(f32[16,512]{1,0:T(8,128)S(1)} %get-tuple-element.74), channel_id=1, source_target_pairs={{0,24},{8,17},{1,25},{9,18},{2,26},{10,19},{3,27},{11,20},{4,28},{... | collective-permute-start | bytes 98312 | tf_op jit(solution)/shard_map/ppermute | solution.py:504
  60.7 2.9 %collective-permute-start.8 = (f32[16,512]{1,0:T(8,128)S(1)}, f32[16,512]{1,0:T(8,128)S(1)}, u32[]{:S(2)}, u32[]{:S(2)}) collective-permute-start(f32[16,512]{1,0:T(8,128)S(1)} %get-tuple-element.74), channel_id=1, source_target_pairs={{0,16},{8,24},{1,17},{9,25},{2,18},{10,26},{3,19},{11,27},{4,20},{... | collective-permute-start | bytes 98312 | tf_op jit(solution)/shard_map/ppermute | solution.py:504
  65.1 5.9 %collective-permute-start.10 = (f32[16,256]{1,0:T(8,128)S(1)}, f32[16,256]{1,0:T(8,128)S(1)}, u32[]{:S(2)}, u32[]{:S(2)}) collective-permute-start(f32[16,256]{1,0:T(8,128)S(1)} %get-tuple-element.76), channel_id=1, source_target_pairs={{0,8},{8,1},{1,9},{9,2},{2,10},{10,3},{3,11},{11,4},{4,12},{12,5},... | collective-permute-start | bytes 49160 | tf_op jit(solution)/shard_map/ppermute | solution.py:504
  69.0 5.1 %collective-permute-start.11 = (f32[16,256]{1,0:T(8,128)S(1)}, f32[16,256]{1,0:T(8,128)S(1)}, u32[]{:S(2)}, u32[]{:S(2)}) collective-permute-start(f32[16,256]{1,0:T(8,128)S(1)} %get-tuple-element.77.mid), channel_id=1, source_target_pairs={{8,0},{1,8},{9,1},{2,9},{10,2},{3,10},{11,3},{4,11},{12,4},{5,12},... | collective-permute-start | bytes 49160 | tf_op jit(solution)/shard_map/ppermute | solution.py:504
  76.7 26.3 %collective-permute-start.23 = (f32[2,3,2,128,128]{4,3,2,1,0:T(8,128)S(1)}, f32[2,3,2,128,128]{4,3,2,1,0:T(8,128)S(1)}, u32[]{:S(2)}, u32[]{:S(2)}) collective-permute-start(f32[2,3,2,128,128]{4,3,2,1,0:T(8,128)S(1)} %get-tuple-element.94), channel_id=1, source_target_pairs={{80,81},{81,82},{82,83},{83,84},{84,85},{85,86},{86,87},{89,88},{9... | collective-permute-start | bytes 2359304 | tf_op jit(solution)/shard_map/ppermute | solution.py:525
  78.0 36.6 %collective-permute-start.24 = (f32[2,3,2,128,128]{4,3,2,1,0:T(8,128)S(1)}, f32[2,3,2,128,128]{4,3,2,1,0:T(8,128)S(1)}, u32[]{:S(2)}, u32[]{:S(2)}) collective-permute-start(f32[2,3,2,128,128]{4,3,2,1,0:T(8,128)S(1)} %get-tuple-element.95), channel_id=1, source_target_pairs={{81,88},{82,89},{83,90},{84,91},{85,92},{86,93},{87,94},{88,81},{8... | collective-permute-start | bytes 2359304 | tf_op jit(solution)/shard_map/ppermute | solution.py:526
  89.3 12.1 %collective-permute-start.20 = (f32[16,512]{1,0:T(8,128)S(1)}, f32[16,512]{1,0:T(8,128)S(1)}, u32[]{:S(2)}, u32[]{:S(2)}) collective-permute-start(f32[16,512]{1,0:T(8,128)S(1)} %get-tuple-element.89), channel_id=1, source_target_pairs={{0,24},{8,17},{1,25},{9,18},{2,26},{10,19},{3,27},{11,20},{4,28},{... | collective-permute-start | bytes 98312 | tf_op jit(solution)/shard_map/ppermute | solution.py:504
  98.8 2.6 %collective-permute-start.21 = (f32[16,512]{1,0:T(8,128)S(1)}, f32[16,512]{1,0:T(8,128)S(1)}, u32[]{:S(2)}, u32[]{:S(2)}) collective-permute-start(f32[16,512]{1,0:T(8,128)S(1)} %get-tuple-element.89), channel_id=1, source_target_pairs={{0,16},{8,24},{1,17},{9,25},{2,18},{10,26},{3,19},{11,27},{4,20},{... | collective-permute-start | bytes 98312 | tf_op jit(solution)/shard_map/ppermute | solution.py:504
  121.7 57.9 %collective-permute-start.42 = (f32[2,3,2,128,128]{4,3,2,1,0:T(8,128)S(1)}, f32[2,3,2,128,128]{4,3,2,1,0:T(8,128)S(1)}, u32[]{:S(2)}, u32[]{:S(2)}) collective-permute-start(f32[2,3,2,128,128]{4,3,2,1,0:T(8,128)S(1)} %get-tuple-element.111), channel_id=1, source_target_pairs={{0,1},{1,2},{2,3},{3,4},{4,5},{5,6},{6,7},{9,8},{10,9},{11,10},{12... | collective-permute-start | bytes 2359304 | tf_op jit(solution)/shard_map/ppermute | solution.py:525
  123.0 56.7 %collective-permute-start.43 = (f32[2,3,2,128,128]{4,3,2,1,0:T(8,128)S(1)}, f32[2,3,2,128,128]{4,3,2,1,0:T(8,128)S(1)}, u32[]{:S(2)}, u32[]{:S(2)}) collective-permute-start(f32[2,3,2,128,128]{4,3,2,1,0:T(8,128)S(1)} %get-tuple-element.112), channel_id=1, source_target_pairs={{1,8},{2,9},{3,10},{4,11},{5,12},{6,13},{7,14},{8,1},{9,2},{10,3},... | collective-permute-start | bytes 2359304 | tf_op jit(solution)/shard_map/ppermute | solution.py:526
  130.0 10.4 %collective-permute-start.31 = (f32[16,512]{1,0:T(8,128)S(1)}, f32[16,512]{1,0:T(8,128)S(1)}, u32[]{:S(2)}, u32[]{:S(2)}) collective-permute-start(f32[16,512]{1,0:T(8,128)S(1)} %get-tuple-element.101), channel_id=1, source_target_pairs={{0,24},{8,17},{1,25},{9,18},{2,26},{10,19},{3,27},{11,20},{4,28},{... | collective-permute-start | bytes 98312 | tf_op jit(solution)/shard_map/ppermute | solution.py:504
  137.5 2.9 %collective-permute-start.32 = (f32[16,512]{1,0:T(8,128)S(1)}, f32[16,512]{1,0:T(8,128)S(1)}, u32[]{:S(2)}, u32[]{:S(2)}) collective-permute-start(f32[16,512]{1,0:T(8,128)S(1)} %get-tuple-element.101), channel_id=1, source_target_pairs={{0,16},{8,24},{1,17},{9,25},{2,18},{10,26},{3,19},{11,27},{4,20},{... | collective-permute-start | bytes 98312 | tf_op jit(solution)/shard_map/ppermute | solution.py:504
  142.5 20.4 %collective-permute-start.34 = (f32[2,16,512]{2,1,0:T(8,128)S(1)}, f32[2,16,512]{2,1,0:T(8,128)S(1)}, u32[]{:S(2)}, u32[]{:S(2)}) collective-permute-start(f32[2,16,512]{2,1,0:T(8,128)S(1)} %slice.3), channel_id=1, source_target_pairs={{0,8},{8,1},{1,9},{9,2},{2,10},{10,3},{3,11},{11,4},{4,12},{12,5},... | collective-permute-start | bytes 196616 | tf_op jit(solution)/shard_map/ppermute | solution.py:504
  148.0 15.0 %collective-permute-start.35 = (f32[2,16,512]{2,1,0:T(8,128)S(1)}, f32[2,16,512]{2,1,0:T(8,128)S(1)}, u32[]{:S(2)}, u32[]{:S(2)}) collective-permute-start(f32[2,16,512]{2,1,0:T(8,128)S(1)} %slice.3), channel_id=1, source_target_pairs={{8,0},{1,8},{9,1},{2,9},{10,2},{3,10},{11,3},{4,11},{12,4},{5,12},... | collective-permute-start | bytes 196616 | tf_op jit(solution)/shard_map/ppermute | solution.py:504
  163.5 5.2 %collective-permute-start.36 = (f32[16,512]{1,0:T(8,128)S(1)}, f32[16,512]{1,0:T(8,128)S(1)}, u32[]{:S(2)}, u32[]{:S(2)}) collective-permute-start(f32[16,512]{1,0:T(8,128)S(1)} %get-tuple-element.104), channel_id=1, source_target_pairs={{16,8},{24,1},{17,9},{25,2},{18,10},{26,3},{19,11},{27,4},{20,12},... | collective-permute-start | bytes 98312 | tf_op jit(solution)/shard_map/ppermute | solution.py:504
  164.8 8.2 %collective-permute-start.37 = (f32[16,512]{1,0:T(8,128)S(1)}, f32[16,512]{1,0:T(8,128)S(1)}, u32[]{:S(2)}, u32[]{:S(2)}) collective-permute-start(f32[16,512]{1,0:T(8,128)S(1)} %get-tuple-element.104), channel_id=1, source_target_pairs={{16,0},{24,8},{17,1},{25,9},{18,2},{26,10},{19,3},{27,11},{20,4},{... | collective-permute-start | bytes 98312 | tf_op jit(solution)/shard_map/ppermute | solution.py:504
  166.1 10.3 %collective-permute-start.38 = (f32[16,512]{1,0:T(8,128)S(1)}, f32[16,512]{1,0:T(8,128)S(1)}, u32[]{:S(2)}, u32[]{:S(2)}) collective-permute-start(f32[16,512]{1,0:T(8,128)S(1)} %get-tuple-element.104), channel_id=1, source_target_pairs={{24,0},{17,8},{25,1},{18,9},{26,2},{19,10},{27,3},{20,11},{28,4},{... | collective-permute-start | bytes 98312 | tf_op jit(solution)/shard_map/ppermute | solution.py:504
  184.1 19.4 %collective-permute-start.47 = (f32[16,512]{1,0:T(8,128)S(1)}, f32[16,512]{1,0:T(8,128)S(1)}, u32[]{:S(2)}, u32[]{:S(2)}) collective-permute-start(f32[16,512]{1,0:T(8,128)S(1)} %get-tuple-element.116), channel_id=1, source_target_pairs={{16,8},{24,1},{17,9},{25,2},{18,10},{26,3},{19,11},{27,4},{20,12},... | collective-permute-start | bytes 98312 | tf_op jit(solution)/shard_map/ppermute | solution.py:504
  185.4 18.7 %collective-permute-start.48 = (f32[16,512]{1,0:T(8,128)S(1)}, f32[16,512]{1,0:T(8,128)S(1)}, u32[]{:S(2)}, u32[]{:S(2)}) collective-permute-start(f32[16,512]{1,0:T(8,128)S(1)} %get-tuple-element.116), channel_id=1, source_target_pairs={{16,0},{24,8},{17,1},{25,9},{18,2},{26,10},{19,3},{27,11},{20,4},{... | collective-permute-start | bytes 98312 | tf_op jit(solution)/shard_map/ppermute | solution.py:504
  186.7 20.8 %collective-permute-start.49 = (f32[16,512]{1,0:T(8,128)S(1)}, f32[16,512]{1,0:T(8,128)S(1)}, u32[]{:S(2)}, u32[]{:S(2)}) collective-permute-start(f32[16,512]{1,0:T(8,128)S(1)} %get-tuple-element.116), channel_id=1, source_target_pairs={{24,0},{17,8},{25,1},{18,9},{26,2},{19,10},{27,3},{20,11},{28,4},{... | collective-permute-start | bytes 98312 | tf_op jit(solution)/shard_map/ppermute | solution.py:504
  213.3 17.5 %collective-permute-start.56 = (f32[16,512]{1,0:T(8,128)S(1)}, f32[16,512]{1,0:T(8,128)S(1)}, u32[]{:S(2)}, u32[]{:S(2)}) collective-permute-start(f32[16,512]{1,0:T(8,128)S(1)} %get-tuple-element.122), channel_id=1, source_target_pairs={{16,8},{24,1},{17,9},{25,2},{18,10},{26,3},{19,11},{27,4},{20,12},... | collective-permute-start | bytes 98312 | tf_op jit(solution)/shard_map/ppermute | solution.py:504
  214.6 16.3 %collective-permute-start.57 = (f32[16,512]{1,0:T(8,128)S(1)}, f32[16,512]{1,0:T(8,128)S(1)}, u32[]{:S(2)}, u32[]{:S(2)}) collective-permute-start(f32[16,512]{1,0:T(8,128)S(1)} %get-tuple-element.122), channel_id=1, source_target_pairs={{16,0},{24,8},{17,1},{25,9},{18,2},{26,10},{19,3},{27,11},{20,4},{... | collective-permute-start | bytes 98312 | tf_op jit(solution)/shard_map/ppermute | solution.py:504
  215.9 17.7 %collective-permute-start.58 = (f32[16,512]{1,0:T(8,128)S(1)}, f32[16,512]{1,0:T(8,128)S(1)}, u32[]{:S(2)}, u32[]{:S(2)}) collective-permute-start(f32[16,512]{1,0:T(8,128)S(1)} %get-tuple-element.122), channel_id=1, source_target_pairs={{24,0},{17,8},{25,1},{18,9},{26,2},{19,10},{27,3},{20,11},{28,4},{... | collective-permute-start | bytes 98312 | tf_op jit(solution)/shard_map/ppermute | solution.py:504
  (32 other events, 43.8 us)

commit v3 on v2

--- a/solution.py
+++ b/solution.py
@@ -21,6 +21,7 @@
 SMEM_SPEC = pl.BlockSpec(memory_space=pltpu.SMEM)
 ANY_SPEC = pl.BlockSpec(memory_space=pl.ANY)
 PARAMS = pltpu.CompilerParams(vmem_limit_bytes=VMEM_LIMIT)
+BRIEF = pl.CostEstimate(flops=1, transcendentals=0, bytes_accessed=1)
 AXES = ("depth", "lat")
 
 
@@ -83,20 +84,23 @@
     return result
 
 
-def halo_body(ids, straight, cross, *refs, rows, slots):
+def halo_body(ids, straight, cross, *refs, rows, slots, split):
     packed, buffers, sems = refs[-3:]
     row, core = ids[0], ids[1]
     units = len(slots[0])
     first = units // 2
 
     def start(unit, buffer, sem):
-        @pl.when(unit < first)
-        def _():
-            pltpu.make_async_copy(straight.at[unit], buffer, sem).start()
-
-        @pl.when(unit >= first)
-        def _():
-            pltpu.make_async_copy(cross.at[unit - first], buffer, sem).start()
+        by_straight = unit < first if split else core == 0
+        place = lax.rem(unit, first) if split else unit
+
+        @pl.when(by_straight)
+        def _():
+            pltpu.make_async_copy(straight.at[place], buffer, sem).start()
+
+        @pl.when(jnp.logical_not(by_straight))
+        def _():
+            pltpu.make_async_copy(cross.at[place], buffer, sem).start()
 
     def slot_of(unit):
         number = unit + units * core
@@ -127,19 +131,21 @@
         scratch_shapes=PACK_SCRATCH,
         input_output_aliases={2: 0} if extra else {},
         compiler_params=PARAMS,
+        cost_estimate=BRIEF,
         name="pack_mine" if mine else "pack_partner",
     )(ids, pltpu.with_memory_space_constraint(source, pltpu.HBM) if mine else source, *extra)
 
 
-def pack_halo(ids, sources, packed, rows, slots, name):
-    return pl.pallas_call(
-        functools.partial(halo_body, rows=rows, slots=slots),
+def pack_halo(ids, sources, packed, rows, slots, name, split=True):
+    return pl.pallas_call(
+        functools.partial(halo_body, rows=rows, slots=slots, split=split),
         in_specs=[SMEM_SPEC, ANY_SPEC, ANY_SPEC, VMEM_SPEC],
         out_specs=VMEM_SPEC,
         out_shape=jax.ShapeDtypeStruct(PACKED, jnp.bfloat16),
         scratch_shapes=PACK_SCRATCH,
         input_output_aliases={3: 0},
         compiler_params=PARAMS,
+        cost_estimate=BRIEF,
         name=name,
     )(ids, *sources, packed)
 
@@ -178,6 +184,7 @@
         out_shape=[pltpu.VMEM((count, 3, 2, TILE, TILE), jnp.float32)] * 2,
         scratch_shapes=[pltpu.SemaphoreType.DMA((6,))],
         compiler_params=PARAMS,
+        cost_estimate=BRIEF,
         name=name,
     )(ids, pltpu.with_memory_space_constraint(mine, pltpu.HBM), other)
 
@@ -236,6 +243,7 @@
         out_specs=VMEM_SPEC,
         out_shape=jax.ShapeDtypeStruct(shape, jnp.float32),
         compiler_params=PARAMS,
+        cost_estimate=BRIEF,
         name=name,
     )(*smem, *arrays)
 
@@ -365,6 +373,7 @@
         scratch_shapes=[PARTS],
         input_output_aliases={6: 1},
         compiler_params=PARAMS,
+        cost_estimate=BRIEF,
         name=f"down_{turn}",
     )(ids, *received, window, packed, waves)
 
@@ -380,6 +389,7 @@
         scratch_shapes=[PARTS],
         input_output_aliases={6: len(widths)},
         compiler_params=PARAMS,
+        cost_estimate=BRIEF,
         name=f"pair_{turn}_{first}",
     )(ids, low, mid, high, window, packed, waves)
 
@@ -396,6 +406,7 @@
         scratch_shapes=[PARTS, pltpu.VMEM((16, SPAN), jnp.float32)],
         input_output_aliases={9: 1},
         compiler_params=PARAMS,
+        cost_estimate=BRIEF,
         name=f"up_{turn}",
     )(ids, *received, window, packed, waves, left, right, field)
 
@@ -435,6 +446,7 @@
         out_specs=(VMEM_SPEC,) * 2,
         out_shape=(jax.ShapeDtypeStruct(shape, jnp.float32),) * 2,
         compiler_params=PARAMS,
+        cost_estimate=BRIEF,
         name="join",
     )(ids, waves, field, taken)
 
@@ -447,12 +459,12 @@
 )
 FIRST_SLOTS = (((0, 2), (2, 2)), ((2, 7), (0, 7)))
 DOWN_RUNS = (
-    (((0, 5, 8),), ((0, 0, 3),)),
-    (((1, 0, 2), (2, 0, 1)), ((1, 6, 8), (2, 7, 8))),
+    (((0, 5, 7), (1, 6, 8)), ((0, 1, 3), (1, 0, 2))),
+    ((), ()),
 )
 DOWN_SLOTS = (
-    ((0, 0), (0, 1), (0, 2), (1, 1), (1, 2), (2, 2)),
-    ((1, 7), (1, 8), (2, 7), (0, 7), (0, 8), (0, 9)),
+    ((0, 0), (0, 1), (1, 1), (1, 2)),
+    ((0, 8), (0, 9), (1, 7), (1, 8)),
 )
 EARLY_RUNS = (
     (((3, 7, 8), (2, 6, 7)), ((3, 0, 1), (2, 1, 2))),
@@ -462,14 +474,8 @@
     ((3, 2), (2, 1), (3, 0), (3, 1)),
     ((3, 8), (3, 9), (3, 7), (2, 8)),
 )
-EXTRA_RUNS = (
-    (((1, 7, 8), (2, 6, 7)), ((1, 0, 1), (2, 1, 2))),
-    (((3, 1, 3),), ((3, 5, 7),)),
-)
-EXTRA_SLOTS = (
-    ((1, 2), (2, 1), (3, 0), (3, 1)),
-    ((3, 8), (3, 9), (1, 7), (2, 8)),
-)
+LAST_RUNS = ((((1, 7, 8),), ((1, 0, 1),)), ((), ()))
+LAST_SLOTS = (((1, 2),), ((1, 7),))
 
 
 def gated(value, *others):
@@ -505,10 +511,10 @@
 
     partner = [(at(d, l), at(d ^ 1, l)) for d in range(depth_count) for l in range(lat_count)]
 
-    def beside_pairs(rows, same):
+    def beside_pairs(rows, same, sides=(0, 1)):
         pairs = []
         for row in rows:
-            for side in range(2):
+            for side in sides:
                 shift = 1 if (side == 0) == same else -1
                 target = side if same else 1 - side
                 pairs += [
@@ -518,35 +524,42 @@
                 ]
         return pairs
 
-    def send_halo(ids, other, parts, name):
+    def send_halo(ids, other, parts, name, sides=(0, 1), after=()):
         straight, cross = cut(ids, factor, other, parts, name)
+        straight, cross = lax.optimization_barrier((straight, cross, *after))[:2]
         rows = [row for begin, end, _ in parts for row in range(begin, end)]
         return straight, (
-            lax.ppermute(straight, AXES, beside_pairs(rows, True)),
-            lax.ppermute(cross, AXES, beside_pairs(rows, False)),
+            lax.ppermute(straight, AXES, beside_pairs(rows, True, sides)),
+            lax.ppermute(cross, AXES, beside_pairs(rows, False, sides)),
         )
 
-    first_cut, first_halo = send_halo(ids, factor, ((0, PAIR_ROWS, FIRST_RUNS),), "cut_first")
+    first_cut, first_halo = send_halo(ids, factor, ((0, chip_rows, FIRST_RUNS),), "cut_first")
+    down_parts = ((PAIR_ROWS, chip_rows, DOWN_RUNS),)
+    early_parts = ((LATE_ROWS, chip_rows, EARLY_RUNS),)
+    late_parts = ((0, LATE_ROWS, EARLY_RUNS),)
+    last_parts = ((0, PAIR_ROWS, LAST_RUNS),)
     other = lax.ppermute(gated(factor, first_cut), AXES, partner)
 
     rows = small_call(
-        rows_body, (ids, src_cell, src_layer), (rhs_field, couple), (layer_total, ROWS, strip_cells), "rows"
+        rows_body,
+        (gated(ids, first_cut), src_cell, src_layer),
+        (rhs_field, couple),
+        (layer_total, ROWS, strip_cells),
+        "rows",
     )
     rows_other = lax.ppermute(rows, AXES, partner)
-    edge = small_call(edge_body, (ids,), (rows, rows_other), (GROUP, ROWS, HALF), "edge")
     packed = pack_chip(gated(ids, rows), factor, None, True)
-    other, packed = lax.optimization_barrier((other, packed, edge))[:2]
+    edge = small_call(
+        edge_body, (gated(ids, packed),), (rows, rows_other), (GROUP, ROWS, HALF), "edge"
+    )
+    packed = pack_chip(ids, other, packed, False)
     beside = lax.ppermute(edge, AXES, beside_pairs(everyone, True))
     window = small_call(
-        window_body, (ids,), (rows, rows_other, beside), (GROUP, ROWS, WINDOW), "window"
-    )
-    down_parts = ((PAIR_ROWS, chip_rows, DOWN_RUNS),)
-    early_parts = ((LATE_ROWS, chip_rows, EARLY_RUNS), (0, PAIR_ROWS, EXTRA_RUNS))
-    late_parts = ((0, LATE_ROWS, EARLY_RUNS),)
-    _, halo = send_halo(gated(ids, beside), other, down_parts, "cut_down")
-    packed = pack_chip(ids, other, packed, False)
+        window_body, (gated(ids, packed, *first_halo),), (rows, rows_other, beside), (GROUP, ROWS, WINDOW), "window"
+    )
+    _, halo = send_halo(gated(ids, rows), factor, down_parts, "cut_down", (0,), (window, *first_halo))
     packed = pack_halo(
-        gated(ids, window), first_halo, packed, (0, PAIR_ROWS), FIRST_SLOTS, "halo_first"
+        gated(ids, window), first_halo, packed, (0, chip_rows), FIRST_SLOTS, "halo_first"
     )
 
     zero_half = jnp.zeros((2 * shot_count, HALF), jnp.float32)
@@ -564,19 +577,18 @@
             out, waves = pair_step(ids, low, left_edge, high, window, packed, waves, turn, 2)
             if turn + 1 == PAIR_ROWS:
                 down_rows = (PAIR_ROWS, chip_rows)
-                packed = pack_halo(gated(ids, out), halo, packed, down_rows, DOWN_SLOTS, "halo_down")
-                _, halo = send_halo(gated(ids, out, *halo), other, early_parts, "cut_early")
+                packed = pack_halo(
+                    gated(ids, out), halo, packed, down_rows, DOWN_SLOTS, "halo_down", False
+                )
+                _, early_halo = send_halo(gated(ids, out, *halo), other, early_parts, "cut_early")
                 out, packed = lax.optimization_barrier((out, packed))
         else:
             out, waves = down_step(ids, received, window, packed, waves, turn)
-            if turn + 1 == LATE_ROWS:
-                late_ids = gated(ids, out)
-                early_rows, first_rows = (LATE_ROWS, chip_rows), (0, PAIR_ROWS)
-                packed = pack_halo(late_ids, halo, packed, early_rows, EARLY_SLOTS, "halo_early")
-                packed = pack_halo(late_ids, halo, packed, first_rows, EXTRA_SLOTS, "halo_extra")
+            if turn == LATE_ROWS:
+                late_ids, last_rows = gated(ids, out), (LATE_ROWS + 1, chip_rows)
+                packed = pack_halo(late_ids, early_halo, packed, last_rows, EARLY_SLOTS, "halo_last")
                 out, packed = lax.optimization_barrier((out, packed))
-            if turn == LATE_ROWS:
-                _, halo = send_halo(gated(ids, out), other, late_parts, "cut_late")
+                _, late_halo = send_halo(gated(ids, out), other, late_parts, "cut_late")
         if turn + 1 < chip_rows:
             group = range(turn % 3, chip_rows, 3)
             received = (hop(out, group, 1, 1), hop(out, group, 1, 0), hop(out, group, 1, -1))
@@ -586,8 +598,21 @@
     received = (zero_half,) * 3
     for turn in reversed(everyone):
         out, field = up_step(ids, received, window, packed, waves, left, right, field, turn)
+        if turn == LATE_ROWS + 1:
+            row = (LATE_ROWS, LATE_ROWS + 1)
+            packed = pack_halo(gated(ids, out), early_halo, packed, row, EARLY_SLOTS, "halo_early")
+            out, packed = lax.optimization_barrier((out, packed))
         if turn == LATE_ROWS:
-            packed = pack_halo(gated(ids, out), halo, packed, (0, LATE_ROWS), EARLY_SLOTS, "halo_late")
+            late_rows = (0, LATE_ROWS)
+            packed = pack_halo(gated(ids, out), late_halo, packed, late_rows, EARLY_SLOTS, "halo_late")
+            out, packed = lax.optimization_barrier((out, packed))
+        if turn == LATE_ROWS - 1:
+            _, last_halo = send_halo(gated(ids, out), factor, last_parts, "cut_last", (0,))
+        if turn == PAIR_ROWS:
+            last_rows = (0, PAIR_ROWS)
+            packed = pack_halo(
+                gated(ids, out), last_halo, packed, last_rows, LAST_SLOTS, "halo_extra", False
+            )
             out, packed = lax.optimization_barrier((out, packed))
         if turn:
             group = range(turn % 3, chip_rows, 3)

time: 241 us -> 225 us (0.934)
  waiting for transfers between devices: 95.3 us -> 72.3 us
  starting transfers between devices: 100 us -> 108 us
    ppermute x8 -> x10, waiting for transfers between devices: 20.1 us -> 1.82 us  [the longest x5 1.81 us: send_halo(): lax.ppermute(cross, AXES, beside_pairs(rows, False, sides))]
    ppermute x48, starting transfers between devices: 73.8 us -> 87.6 us  [hop(): return lax.ppermute(value, AXES, pairs)]
    ppermute x1, waiting for transfers between devices: 6.42 us -> 0.01 us  [shards(): rows_other = lax.ppermute(rows, AXES, partner)]
    ppermute x8 -> x10, starting transfers between devices: 23.2 us -> 17.6 us  [the longest x5 12.9 us: send_halo(): lax.ppermute(cross, AXES, beside_pairs(rows, False, sides))]
    pallas_call x4 -> x5, Pallas kernels: 6.31 us -> 5.53 us  [cut(): pl.pallas_call(functools.partial(cut_body, parts=parts), in_specs=[SMEM_S...]
    pallas_call x5 -> x6, Pallas kernels: 5.58 us -> 5.37 us  [pack_halo(): pl.pallas_call(functools.partial(halo_body, rows=rows, slots=slots, split...]
  transfers between devices with their start and end apart: 60 -> 62, of which waited for: 19 -> 16; matrix products, arithmetic and copies ran while one was open for 0% -> 0% of each run, Pallas kernels for 9% -> 11%
where the time goes in v3:
time: 225 us; the launch traced here: 224 us
  starting transfers between devices  108 us (48%)
  waiting for transfers between devices  72.3 us (32%)
  Pallas kernels  38.8 us (17%)
  local copies, waits for them, and re-layouts  3.01 us (1%)
    ppermute x48, starting transfers between devices, hop(): return lax.ppermute(value, AXES, pairs)  87.6 us
    ppermute x48, waiting for transfers between devices, hop(): return lax.ppermute(value, AXES, pairs)  69.1 us
    ppermute x5, starting transfers between devices, send_halo(): lax.ppermute(cross, AXES, beside_pairs(rows, False, sides))  12.9 us
    pallas_call x2, Pallas kernels, pack_chip(): pl.pallas_call(functools.partial(chip_body, mine=mine), in_specs=[SMEM_SP...  9.58 us
    pallas_call x8, Pallas kernels, up_step(): pl.pallas_call(functools.partial(up_body, turn=turn), in_specs=[SMEM_SPEC...  7.08 us
    pallas_call x5, Pallas kernels, cut(): pl.pallas_call(functools.partial(cut_body, parts=parts), in_specs=[SMEM_S...  5.53 us
    pallas_call x6, Pallas kernels, pack_halo(): pl.pallas_call(functools.partial(halo_body, rows=rows, slots=slots, split...  5.37 us
    ppermute x5, starting transfers between devices, send_halo(): lax.ppermute(straight, AXES, beside_pairs(rows, True, sides))  4.73 us
  transfers between devices with their start and end apart: 62, of which 16 were waited for; matrix products, arithmetic and copies ran while one was open for 0% of the time, Pallas kernels for 11%

profile of v3, /device:TPU:1, one launch (start us, length us, event | category | flops | bytes accessed | tf_op | source)
XLA Modules:
  0.0 224.1 jit_solution(5543297596986267217)
XLA Ops:
  0.7 1.7 cut_first.1
  2.4 1.5 collective-permute-start
  5.2 5.2 %collective-permute-start.2 = (f32[1,3,2,128,128]{4,3,2,1,0:T(8,128)S(1)}, f32[1,3,2,128,128]{4,3,2,1,0:T(8,128)S(1)}, u32[]{:S(2)}, u32[]{:S(2)}) collective-permute-start(f32[1,3,2,128,128]{4,3,2,1,0:T(8,128)S(1)} %get-tuple-element.79), channel_id=1, source_target_pairs={{1,8},{2,9},{3,10},{4,11},{5,12},{6,13},{7,14},{8,1},{9,2},{10,3},... | collective-permute-start | bytes 1179656 | tf_op jit(solution)/shard_map/ppermute | solution.py:533
  14.1 5.2 %pack_mine.1.refs_0_ = bf16[4,10,384,512]{3,2,1,0:T(8,128)(2,1)S(1)} custom-call(s32[4]{0:T(128)S(1)} %pad_add_fusion.ids, f32[2,8,3,2,128,128]{5,4,3,2,1,0:T(8,128)} %other.5), custom_call_target="tpu_custom_call" | custom-call | flops 1 | bytes 1 | tf_op jit(solution)/shard_map/pack_mine/pallas_call | solution.py:126
  21.8 4.4 %pack_partner.1.refs_0_ = bf16[4,10,384,512]{3,2,1,0:T(8,128)(2,1)S(1)} custom-call(s32[4]{0:T(128)S(1)} %pad_add_fusion.ids, f32[2,8,3,2,128,128]{5,4,3,2,1,0:T(8,128)S(1)} %collective-permute-done.source.other, bf16[4,10,384,512]{3,2,1,0:T(8,128)(2,1)S(1)} %pack_mine.1.refs_0_), custom_call_target="tpu_custom_call", output_to_operand_aliasing={{}: (2, {})} | custom-call | flops 1 | bytes 1 | tf_op jit(solution)/shard_map/pack_partner/pallas_call | solution.py:126
  26.2 1.8 collective-permute-done.2.cross
  32.6 6.0 %collective-permute-start.5 = (f32[16,256]{1,0:T(8,128)S(1)}, f32[16,256]{1,0:T(8,128)S(1)}, u32[]{:S(2)}, u32[]{:S(2)}) collective-permute-start(f32[16,256]{1,0:T(8,128)S(1)} %get-tuple-element.83), channel_id=1, source_target_pairs={{0,8},{8,1},{1,9},{9,2},{2,10},{10,3},{3,11},{11,4},{4,12},{12,5},... | collective-permute-start | bytes 49160 | tf_op jit(solution)/shard_map/ppermute | solution.py:510
  38.6 1.9 collective-permute-start.6
  40.5 3.1 %collective-permute-done.6.high = f32[16,256]{1,0:T(8,128)S(1)} collective-permute-done((f32[16,256]{1,0:T(8,128)S(1)}, f32[16,256]{1,0:T(8,128)S(1)}, u32[]{:S(2)}, u32[]{:S(2)}) %collective-permute-start.6) | collective-permute-done | bytes 16416 | tf_op jit(solution)/shard_map/ppermute | solution.py:510
  44.9 1.5 collective-permute-start.7
  46.4 1.6 collective-permute-start.8
  50.8 3.9 %collective-permute-start.10 = (f32[16,256]{1,0:T(8,128)S(1)}, f32[16,256]{1,0:T(8,128)S(1)}, u32[]{:S(2)}, u32[]{:S(2)}) collective-permute-start(f32[16,256]{1,0:T(8,128)S(1)} %get-tuple-element.88), channel_id=1, source_target_pairs={{0,8},{8,1},{1,9},{9,2},{2,10},{10,3},{3,11},{11,4},{4,12},{12,5},... | collective-permute-start | bytes 49160 | tf_op jit(solution)/shard_map/ppermute | solution.py:510
  54.8 1.9 collective-permute-start.11
  56.7 3.1 %collective-permute-done.11.high = f32[16,256]{1,0:T(8,128)S(1)} collective-permute-done((f32[16,256]{1,0:T(8,128)S(1)}, f32[16,256]{1,0:T(8,128)S(1)}, u32[]{:S(2)}, u32[]{:S(2)}) %collective-permute-start.11) | collective-permute-done | bytes 16416 | tf_op jit(solution)/shard_map/ppermute | solution.py:510
  68.3 21.0 %collective-permute-start.20 = (f32[16,512]{1,0:T(8,128)S(1)}, f32[16,512]{1,0:T(8,128)S(1)}, u32[]{:S(2)}, u32[]{:S(2)}) collective-permute-start(f32[16,512]{1,0:T(8,128)S(1)} %get-tuple-element.102), channel_id=1, source_target_pairs={{0,24},{8,17},{1,25},{9,18},{2,26},{10,19},{3,27},{11,20},{4,28},{... | collective-permute-start | bytes 98312 | tf_op jit(solution)/shard_map/ppermute | solution.py:510
  96.9 2.0 cut_late.1
  100.2 4.9 %collective-permute-start.43 = (f32[2,3,2,128,128]{4,3,2,1,0:T(8,128)S(1)}, f32[2,3,2,128,128]{4,3,2,1,0:T(8,128)S(1)}, u32[]{:S(2)}, u32[]{:S(2)}) collective-permute-start(f32[2,3,2,128,128]{4,3,2,1,0:T(8,128)S(1)} %get-tuple-element.128), channel_id=1, source_target_pairs={{1,8},{2,9},{3,10},{4,11},{5,12},{6,13},{7,14},{8,1},{9,2},{10,3},... | collective-permute-start | bytes 2359304 | tf_op jit(solution)/shard_map/ppermute | solution.py:533
  107.7 9.6 %collective-permute-start.31 = (f32[16,512]{1,0:T(8,128)S(1)}, f32[16,512]{1,0:T(8,128)S(1)}, u32[]{:S(2)}, u32[]{:S(2)}) collective-permute-start(f32[16,512]{1,0:T(8,128)S(1)} %get-tuple-element.114), channel_id=1, source_target_pairs={{0,24},{8,17},{1,25},{9,18},{2,26},{10,19},{3,27},{11,20},{4,28},{... | collective-permute-start | bytes 98312 | tf_op jit(solution)/shard_map/ppermute | solution.py:510
  117.3 1.6 collective-permute-start.32
  122.3 3.9 %collective-permute-start.34 = (f32[2,16,512]{2,1,0:T(8,128)S(1)}, f32[2,16,512]{2,1,0:T(8,128)S(1)}, u32[]{:S(2)}, u32[]{:S(2)}) collective-permute-start(f32[2,16,512]{2,1,0:T(8,128)S(1)} %slice.3), channel_id=1, source_target_pairs={{0,8},{8,1},{1,9},{9,2},{2,10},{10,3},{3,11},{11,4},{4,12},{12,5},... | collective-permute-start | bytes 196616 | tf_op jit(solution)/shard_map/ppermute | solution.py:510
  126.3 1.9 collective-permute-start.35
  128.2 10.7 %collective-permute-done.34.left = f32[2,16,512]{2,1,0:T(8,128)S(1)} collective-permute-done((f32[2,16,512]{2,1,0:T(8,128)S(1)}, f32[2,16,512]{2,1,0:T(8,128)S(1)}, u32[]{:S(2)}, u32[]{:S(2)}) %collective-permute-start.34) | collective-permute-done | bytes 65568 | tf_op jit(solution)/shard_map/ppermute | solution.py:510
  143.4 1.3 collective-permute-done.36.low
  144.7 5.4 %collective-permute-done.37.mid = f32[16,512]{1,0:T(8,128)S(1)} collective-permute-done((f32[16,512]{1,0:T(8,128)S(1)}, f32[16,512]{1,0:T(8,128)S(1)}, u32[]{:S(2)}, u32[]{:S(2)}) %collective-permute-start.37) | collective-permute-done | bytes 32800 | tf_op jit(solution)/shard_map/ppermute | solution.py:510
  150.1 3.8 %collective-permute-done.38.high = f32[16,512]{1,0:T(8,128)S(1)} collective-permute-done((f32[16,512]{1,0:T(8,128)S(1)}, f32[16,512]{1,0:T(8,128)S(1)}, u32[]{:S(2)}, u32[]{:S(2)}) %collective-permute-start.38) | collective-permute-done | bytes 32800 | tf_op jit(solution)/shard_map/ppermute | solution.py:510
  157.7 1.7 halo_late.1.packed.refs_0_
  168.7 22.7 %collective-permute-done.47.low = f32[16,512]{1,0:T(8,128)S(1)} collective-permute-done((f32[16,512]{1,0:T(8,128)S(1)}, f32[16,512]{1,0:T(8,128)S(1)}, u32[]{:S(2)}, u32[]{:S(2)}) %collective-permute-start.47) | collective-permute-done | bytes 32800 | tf_op jit(solution)/shard_map/ppermute | solution.py:510
  191.3 3.7 %collective-permute-done.49.high = f32[16,512]{1,0:T(8,128)S(1)} collective-permute-done((f32[16,512]{1,0:T(8,128)S(1)}, f32[16,512]{1,0:T(8,128)S(1)}, u32[]{:S(2)}, u32[]{:S(2)}) %collective-permute-start.49) | collective-permute-done | bytes 32800 | tf_op jit(solution)/shard_map/ppermute | solution.py:510
  205.5 9.5 %collective-permute-done.58.low = f32[16,512]{1,0:T(8,128)S(1)} collective-permute-done((f32[16,512]{1,0:T(8,128)S(1)}, f32[16,512]{1,0:T(8,128)S(1)}, u32[]{:S(2)}, u32[]{:S(2)}) %collective-permute-start.58) | collective-permute-done | bytes 32800 | tf_op jit(solution)/shard_map/ppermute | solution.py:510
  215.2 2.6 %collective-permute-done.60.high = f32[16,512]{1,0:T(8,128)S(1)} collective-permute-done((f32[16,512]{1,0:T(8,128)S(1)}, f32[16,512]{1,0:T(8,128)S(1)}, u32[]{:S(2)}, u32[]{:S(2)}) %collective-permute-start.60) | collective-permute-done | bytes 32800 | tf_op jit(solution)/shard_map/ppermute | solution.py:510
  217.8 3.0 %up_0.1 = (f32[16,512]{1,0:T(8,128)}, f32[4,16,512]{2,1,0:T(8,128)S(1)}) custom-call(s32[4]{0:T(128)S(1)} %pad_add_fusion.ids, f32[16,512]{1,0:T(8,128)S(1)} %collective-permute-done.58.low, f32[16,512]{1,0:T(8,128)S(1)} %collective-permute-done.59.mid, f32[16,512]{1,0:T(8,128)S(1)} %collective-permute-done.60.high, ...), custom_call_target="tpu_custom_call", output_to_operand_aliasing={{1}: (9, {})} | custom-call | flops 1 | bytes 1 | tf_op jit(solution)/shard_map/up_0/pallas_call | solution.py:398
  221.5 1.3 collective-permute-done.61.taken
  (141 shorter events, 68.9 us)
Async XLA Ops:
  2.4 19.3 %collective-permute-start = (f32[2,8,3,2,128,128]{5,4,3,2,1,0:T(8,128)}, f32[2,8,3,2,128,128]{5,4,3,2,1,0:T(8,128)S(1)}, u32[]{:S(2)}, u32[]{:S(2)}) collective-permute-start(f32[2,8,3,2,128,128]{5,4,3,2,1,0:T(8,128)} %other.5), channel_id=1, source_target_pairs={{0,8},{1,9},{2,10},{3,11},{4,12},{5,13},{6,14},{7,15},{8,0},{9,1},... | collective-permute-start | bytes 18874376 | tf_op jit(solution)/shard_map/ppermute | solution.py:541
  3.9 22.2 %collective-permute-start.1 = (f32[1,3,2,128,128]{4,3,2,1,0:T(8,128)S(1)}, f32[1,3,2,128,128]{4,3,2,1,0:T(8,128)S(1)}, u32[]{:S(2)}, u32[]{:S(2)}) collective-permute-start(f32[1,3,2,128,128]{4,3,2,1,0:T(8,128)S(1)} %get-tuple-element.75), channel_id=1, source_target_pairs={{0,1},{1,2},{2,3},{3,4},{4,5},{5,6},{6,7},{9,8},{10,9},{11,10},{12... | collective-permute-start | bytes 1179656 | tf_op jit(solution)/shard_map/ppermute | solution.py:532
  5.2 22.8 %collective-permute-start.2 = (f32[1,3,2,128,128]{4,3,2,1,0:T(8,128)S(1)}, f32[1,3,2,128,128]{4,3,2,1,0:T(8,128)S(1)}, u32[]{:S(2)}, u32[]{:S(2)}) collective-permute-start(f32[1,3,2,128,128]{4,3,2,1,0:T(8,128)S(1)} %get-tuple-element.79), channel_id=1, source_target_pairs={{1,8},{2,9},{3,10},{4,11},{5,12},{6,13},{7,14},{8,1},{9,2},{10,3},... | collective-permute-start | bytes 1179656 | tf_op jit(solution)/shard_map/ppermute | solution.py:533
  14.0 5.3 %collective-permute-start.3 = (f32[2,20,1024]{2,1,0:T(8,128)S(1)}, f32[2,20,1024]{2,1,0:T(8,128)S(1)}, u32[]{:S(2)}, u32[]{:S(2)}) collective-permute-start(f32[2,20,1024]{2,1,0:T(8,128)S(1)} %rows.1), channel_id=1, source_target_pairs={{0,8},{1,9},{2,10},{3,11},{4,12},{5,13},{6,14},{7,15},{8,0},{9,1},... | collective-permute-start | bytes 491528 | tf_op jit(solution)/shard_map/ppermute | solution.py:550
  19.8 8.2 %collective-permute-start.4 = (f32[4,20,512]{2,1,0:T(8,128)S(1)}, f32[4,20,512]{2,1,0:T(8,128)S(1)}, u32[]{:S(2)}, u32[]{:S(2)}) collective-permute-start(f32[4,20,512]{2,1,0:T(8,128)S(1)} %edge.1), channel_id=1, source_target_pairs={{0,1},{1,2},{2,3},{3,4},{4,5},{5,6},{6,7},{9,8},{10,9},{11,10},{12... | collective-permute-start | bytes 491528 | tf_op jit(solution)/shard_map/ppermute | solution.py:556
  28.6 31.8 %collective-permute-start.12 = (f32[4,3,2,128,128]{4,3,2,1,0:T(8,128)S(1)}, f32[4,3,2,128,128]{4,3,2,1,0:T(8,128)S(1)}, u32[]{:S(2)}, u32[]{:S(2)}) collective-permute-start(f32[4,3,2,128,128]{4,3,2,1,0:T(8,128)S(1)} %get-tuple-element.95), channel_id=1, source_target_pairs={{32,33},{33,34},{34,35},{35,36},{36,37},{37,38},{38,39},{48,49},{4... | collective-permute-start | bytes 4718600 | tf_op jit(solution)/shard_map/ppermute | solution.py:532
  29.4 31.1 %collective-permute-start.13 = (f32[4,3,2,128,128]{4,3,2,1,0:T(8,128)S(1)}, f32[4,3,2,128,128]{4,3,2,1,0:T(8,128)S(1)}, u32[]{:S(2)}, u32[]{:S(2)}) collective-permute-start(f32[4,3,2,128,128]{4,3,2,1,0:T(8,128)S(1)} %get-tuple-element.96), channel_id=1, source_target_pairs={{33,40},{34,41},{35,42},{36,43},{37,44},{38,45},{39,46},{49,56},{5... | collective-permute-start | bytes 4718600 | tf_op jit(solution)/shard_map/ppermute | solution.py:533
  32.6 7.9 %collective-permute-start.5 = (f32[16,256]{1,0:T(8,128)S(1)}, f32[16,256]{1,0:T(8,128)S(1)}, u32[]{:S(2)}, u32[]{:S(2)}) collective-permute-start(f32[16,256]{1,0:T(8,128)S(1)} %get-tuple-element.83), channel_id=1, source_target_pairs={{0,8},{8,1},{1,9},{9,2},{2,10},{10,3},{3,11},{11,4},{4,12},{12,5},... | collective-permute-start | bytes 49160 | tf_op jit(solution)/shard_map/ppermute | solution.py:510
  38.6 5.1 %collective-permute-start.6 = (f32[16,256]{1,0:T(8,128)S(1)}, f32[16,256]{1,0:T(8,128)S(1)}, u32[]{:S(2)}, u32[]{:S(2)}) collective-permute-start(f32[16,256]{1,0:T(8,128)S(1)} %get-tuple-element.84.mid), channel_id=1, source_target_pairs={{8,0},{1,8},{9,1},{2,9},{10,2},{3,10},{11,3},{4,11},{12,4},{5,12},... | collective-permute-start | bytes 49160 | tf_op jit(solution)/shard_map/ppermute | solution.py:510
  44.9 4.4 %collective-permute-start.7 = (f32[16,512]{1,0:T(8,128)S(1)}, f32[16,512]{1,0:T(8,128)S(1)}, u32[]{:S(2)}, u32[]{:S(2)}) collective-permute-start(f32[16,512]{1,0:T(8,128)S(1)} %get-tuple-element.86), channel_id=1, source_target_pairs={{0,24},{8,17},{1,25},{9,18},{2,26},{10,19},{3,27},{11,20},{4,28},{... | collective-permute-start | bytes 98312 | tf_op jit(solution)/shard_map/ppermute | solution.py:510
  50.8 5.9 %collective-permute-start.10 = (f32[16,256]{1,0:T(8,128)S(1)}, f32[16,256]{1,0:T(8,128)S(1)}, u32[]{:S(2)}, u32[]{:S(2)}) collective-permute-start(f32[16,256]{1,0:T(8,128)S(1)} %get-tuple-element.88), channel_id=1, source_target_pairs={{0,8},{8,1},{1,9},{9,2},{2,10},{10,3},{3,11},{11,4},{4,12},{12,5},... | collective-permute-start | bytes 49160 | tf_op jit(solution)/shard_map/ppermute | solution.py:510
  54.8 5.1 %collective-permute-start.11 = (f32[16,256]{1,0:T(8,128)S(1)}, f32[16,256]{1,0:T(8,128)S(1)}, u32[]{:S(2)}, u32[]{:S(2)}) collective-permute-start(f32[16,256]{1,0:T(8,128)S(1)} %get-tuple-element.89.mid), channel_id=1, source_target_pairs={{8,0},{1,8},{9,1},{2,9},{10,2},{3,10},{11,3},{4,11},{12,4},{5,12},... | collective-permute-start | bytes 49160 | tf_op jit(solution)/shard_map/ppermute | solution.py:510
  61.1 35.2 %collective-permute-start.26 = (f32[2,3,2,128,128]{4,3,2,1,0:T(8,128)S(1)}, f32[2,3,2,128,128]{4,3,2,1,0:T(8,128)S(1)}, u32[]{:S(2)}, u32[]{:S(2)}) collective-permute-start(f32[2,3,2,128,128]{4,3,2,1,0:T(8,128)S(1)} %get-tuple-element.109), channel_id=1, source_target_pairs={{80,81},{81,82},{82,83},{83,84},{84,85},{85,86},{86,87},{89,88},{9... | collective-permute-start | bytes 2359304 | tf_op jit(solution)/shard_map/ppermute | solution.py:532
  61.8 34.5 %collective-permute-start.27 = (f32[2,3,2,128,128]{4,3,2,1,0:T(8,128)S(1)}, f32[2,3,2,128,128]{4,3,2,1,0:T(8,128)S(1)}, u32[]{:S(2)}, u32[]{:S(2)}) collective-permute-start(f32[2,3,2,128,128]{4,3,2,1,0:T(8,128)S(1)} %get-tuple-element.110), channel_id=1, source_target_pairs={{81,88},{82,89},{83,90},{84,91},{85,92},{86,93},{87,94},{88,81},{8... | collective-permute-start | bytes 2359304 | tf_op jit(solution)/shard_map/ppermute | solution.py:533
  68.3 23.6 %collective-permute-start.20 = (f32[16,512]{1,0:T(8,128)S(1)}, f32[16,512]{1,0:T(8,128)S(1)}, u32[]{:S(2)}, u32[]{:S(2)}) collective-permute-start(f32[16,512]{1,0:T(8,128)S(1)} %get-tuple-element.102), channel_id=1, source_target_pairs={{0,24},{8,17},{1,25},{9,18},{2,26},{10,19},{3,27},{11,20},{4,28},{... | collective-permute-start | bytes 98312 | tf_op jit(solution)/shard_map/ppermute | solution.py:510
  98.9 58.8 %collective-permute-start.42 = (f32[2,3,2,128,128]{4,3,2,1,0:T(8,128)S(1)}, f32[2,3,2,128,128]{4,3,2,1,0:T(8,128)S(1)}, u32[]{:S(2)}, u32[]{:S(2)}) collective-permute-start(f32[2,3,2,128,128]{4,3,2,1,0:T(8,128)S(1)} %get-tuple-element.127), channel_id=1, source_target_pairs={{0,1},{1,2},{2,3},{3,4},{4,5},{5,6},{6,7},{9,8},{10,9},{11,10},{12... | collective-permute-start | bytes 2359304 | tf_op jit(solution)/shard_map/ppermute | solution.py:532
  100.2 57.5 %collective-permute-start.43 = (f32[2,3,2,128,128]{4,3,2,1,0:T(8,128)S(1)}, f32[2,3,2,128,128]{4,3,2,1,0:T(8,128)S(1)}, u32[]{:S(2)}, u32[]{:S(2)}) collective-permute-start(f32[2,3,2,128,128]{4,3,2,1,0:T(8,128)S(1)} %get-tuple-element.128), channel_id=1, source_target_pairs={{1,8},{2,9},{3,10},{4,11},{5,12},{6,13},{7,14},{8,1},{9,2},{10,3},... | collective-permute-start | bytes 2359304 | tf_op jit(solution)/shard_map/ppermute | solution.py:533
  107.7 12.5 %collective-permute-start.31 = (f32[16,512]{1,0:T(8,128)S(1)}, f32[16,512]{1,0:T(8,128)S(1)}, u32[]{:S(2)}, u32[]{:S(2)}) collective-permute-start(f32[16,512]{1,0:T(8,128)S(1)} %get-tuple-element.114), channel_id=1, source_target_pairs={{0,24},{8,17},{1,25},{9,18},{2,26},{10,19},{3,27},{11,20},{4,28},{... | collective-permute-start | bytes 98312 | tf_op jit(solution)/shard_map/ppermute | solution.py:510
  117.3 2.9 %collective-permute-start.32 = (f32[16,512]{1,0:T(8,128)S(1)}, f32[16,512]{1,0:T(8,128)S(1)}, u32[]{:S(2)}, u32[]{:S(2)}) collective-permute-start(f32[16,512]{1,0:T(8,128)S(1)} %get-tuple-element.114), channel_id=1, source_target_pairs={{0,16},{8,24},{1,17},{9,25},{2,18},{10,26},{3,19},{11,27},{4,20},{... | collective-permute-start | bytes 98312 | tf_op jit(solution)/shard_map/ppermute | solution.py:510
  122.3 16.6 %collective-permute-start.34 = (f32[2,16,512]{2,1,0:T(8,128)S(1)}, f32[2,16,512]{2,1,0:T(8,128)S(1)}, u32[]{:S(2)}, u32[]{:S(2)}) collective-permute-start(f32[2,16,512]{2,1,0:T(8,128)S(1)} %slice.3), channel_id=1, source_target_pairs={{0,8},{8,1},{1,9},{9,2},{2,10},{10,3},{3,11},{11,4},{4,12},{12,5},... | collective-permute-start | bytes 196616 | tf_op jit(solution)/shard_map/ppermute | solution.py:510
  126.3 12.7 %collective-permute-start.35 = (f32[2,16,512]{2,1,0:T(8,128)S(1)}, f32[2,16,512]{2,1,0:T(8,128)S(1)}, u32[]{:S(2)}, u32[]{:S(2)}) collective-permute-start(f32[2,16,512]{2,1,0:T(8,128)S(1)} %slice.3), channel_id=1, source_target_pairs={{8,0},{1,8},{9,1},{2,9},{10,2},{3,10},{11,3},{4,11},{12,4},{5,12},... | collective-permute-start | bytes 196616 | tf_op jit(solution)/shard_map/ppermute | solution.py:510
  139.5 5.2 %collective-permute-start.36 = (f32[16,512]{1,0:T(8,128)S(1)}, f32[16,512]{1,0:T(8,128)S(1)}, u32[]{:S(2)}, u32[]{:S(2)}) collective-permute-start(f32[16,512]{1,0:T(8,128)S(1)} %get-tuple-element.117), channel_id=1, source_target_pairs={{16,8},{24,1},{17,9},{25,2},{18,10},{26,3},{19,11},{27,4},{20,12},... | collective-permute-start | bytes 98312 | tf_op jit(solution)/shard_map/ppermute | solution.py:510
  140.8 9.3 %collective-permute-start.37 = (f32[16,512]{1,0:T(8,128)S(1)}, f32[16,512]{1,0:T(8,128)S(1)}, u32[]{:S(2)}, u32[]{:S(2)}) collective-permute-start(f32[16,512]{1,0:T(8,128)S(1)} %get-tuple-element.117), channel_id=1, source_target_pairs={{16,0},{24,8},{17,1},{25,9},{18,2},{26,10},{19,3},{27,11},{20,4},{... | collective-permute-start | bytes 98312 | tf_op jit(solution)/shard_map/ppermute | solution.py:510
  142.1 11.8 %collective-permute-start.38 = (f32[16,512]{1,0:T(8,128)S(1)}, f32[16,512]{1,0:T(8,128)S(1)}, u32[]{:S(2)}, u32[]{:S(2)}) collective-permute-start(f32[16,512]{1,0:T(8,128)S(1)} %get-tuple-element.117), channel_id=1, source_target_pairs={{24,0},{17,8},{25,1},{18,9},{26,2},{19,10},{27,3},{20,11},{28,4},{... | collective-permute-start | bytes 98312 | tf_op jit(solution)/shard_map/ppermute | solution.py:510
  162.8 35.4 %collective-permute-start.53 = (f32[1,3,2,128,128]{4,3,2,1,0:T(8,128)S(1)}, f32[1,3,2,128,128]{4,3,2,1,0:T(8,128)S(1)}, u32[]{:S(2)}, u32[]{:S(2)}) collective-permute-start(f32[1,3,2,128,128]{4,3,2,1,0:T(8,128)S(1)} %get-tuple-element.139), channel_id=1, source_target_pairs={{0,1},{1,2},{2,3},{3,4},{4,5},{5,6},{6,7},{16,17},{17,18},{18,19},... | collective-permute-start | bytes 1179656 | tf_op jit(solution)/shard_map/ppermute | solution.py:532
  163.5 34.7 %collective-permute-start.54 = (f32[1,3,2,128,128]{4,3,2,1,0:T(8,128)S(1)}, f32[1,3,2,128,128]{4,3,2,1,0:T(8,128)S(1)}, u32[]{:S(2)}, u32[]{:S(2)}) collective-permute-start(f32[1,3,2,128,128]{4,3,2,1,0:T(8,128)S(1)} %get-tuple-element.140), channel_id=1, source_target_pairs={{1,8},{2,9},{3,10},{4,11},{5,12},{6,13},{7,14},{17,24},{18,25},{19... | collective-permute-start | bytes 1179656 | tf_op jit(solution)/shard_map/ppermute | solution.py:533
  164.8 26.6 %collective-permute-start.47 = (f32[16,512]{1,0:T(8,128)S(1)}, f32[16,512]{1,0:T(8,128)S(1)}, u32[]{:S(2)}, u32[]{:S(2)}) collective-permute-start(f32[16,512]{1,0:T(8,128)S(1)} %get-tuple-element.132), channel_id=1, source_target_pairs={{16,8},{24,1},{17,9},{25,2},{18,10},{26,3},{19,11},{27,4},{20,12},... | collective-permute-start | bytes 98312 | tf_op jit(solution)/shard_map/ppermute | solution.py:510
  166.1 25.3 %collective-permute-start.48 = (f32[16,512]{1,0:T(8,128)S(1)}, f32[16,512]{1,0:T(8,128)S(1)}, u32[]{:S(2)}, u32[]{:S(2)}) collective-permute-start(f32[16,512]{1,0:T(8,128)S(1)} %get-tuple-element.132), channel_id=1, source_target_pairs={{16,0},{24,8},{17,1},{25,9},{18,2},{26,10},{19,3},{27,11},{20,4},{... | collective-permute-start | bytes 98312 | tf_op jit(solution)/shard_map/ppermute | solution.py:510
  167.4 27.6 %collective-permute-start.49 = (f32[16,512]{1,0:T(8,128)S(1)}, f32[16,512]{1,0:T(8,128)S(1)}, u32[]{:S(2)}, u32[]{:S(2)}) collective-permute-start(f32[16,512]{1,0:T(8,128)S(1)} %get-tuple-element.132), channel_id=1, source_target_pairs={{24,0},{17,8},{25,1},{18,9},{26,2},{19,10},{27,3},{20,11},{28,4},{... | collective-permute-start | bytes 98312 | tf_op jit(solution)/shard_map/ppermute | solution.py:510
  201.6 13.4 %collective-permute-start.58 = (f32[16,512]{1,0:T(8,128)S(1)}, f32[16,512]{1,0:T(8,128)S(1)}, u32[]{:S(2)}, u32[]{:S(2)}) collective-permute-start(f32[16,512]{1,0:T(8,128)S(1)} %get-tuple-element.144), channel_id=1, source_target_pairs={{16,8},{24,1},{17,9},{25,2},{18,10},{26,3},{19,11},{27,4},{20,12},... | collective-permute-start | bytes 98312 | tf_op jit(solution)/shard_map/ppermute | solution.py:510
  202.9 12.3 %collective-permute-start.59 = (f32[16,512]{1,0:T(8,128)S(1)}, f32[16,512]{1,0:T(8,128)S(1)}, u32[]{:S(2)}, u32[]{:S(2)}) collective-permute-start(f32[16,512]{1,0:T(8,128)S(1)} %get-tuple-element.144), channel_id=1, source_target_pairs={{16,0},{24,8},{17,1},{25,9},{18,2},{26,10},{19,3},{27,11},{20,4},{... | collective-permute-start | bytes 98312 | tf_op jit(solution)/shard_map/ppermute | solution.py:510
  204.2 13.6 %collective-permute-start.60 = (f32[16,512]{1,0:T(8,128)S(1)}, f32[16,512]{1,0:T(8,128)S(1)}, u32[]{:S(2)}, u32[]{:S(2)}) collective-permute-start(f32[16,512]{1,0:T(8,128)S(1)} %get-tuple-element.144), channel_id=1, source_target_pairs={{24,0},{17,8},{25,1},{18,9},{26,2},{19,10},{27,3},{20,11},{28,4},{... | collective-permute-start | bytes 98312 | tf_op jit(solution)/shard_map/ppermute | solution.py:510
  (34 other events, 49.3 us)

commit v4 on v3

--- a/solution.py
+++ b/solution.py
@@ -279,23 +279,33 @@
     return slice(start * TILE, stop * TILE)
 
 
+def down_operand(parts, window, layer, where, value):
+    forcing = window[layer, 0:16, where]
+    coef_real, coef_imag = window[layer, 16:17, where], window[layer, 17:18, where]
+    store_parts(parts.at[layer % 2], where, forcing + scaled(coef_real, coef_imag, value))
+
+
+def up_operand(parts, window, layer, where, value):
+    coef_real, coef_imag = window[layer, 18:19, where], window[layer, 19:20, where]
+    store_parts(parts.at[layer % 2], where, scaled(coef_real, coef_imag, value))
+
+
+def down_layers(window, packed, waves, parts, layers):
+    for layer in layers:
+        reach = layers[-1] - layer
+        for spot in range(HALO - reach, HALO + OWN + reach):
+            value = tile_product(parts.at[layer % 2], packed, layer, spot)
+            waves[layer, :, lanes(spot, spot + 1)] = value
+            if reach:
+                down_operand(parts, window, layer + 1, lanes(spot + 1, spot + 2), value)
+
+
 def down_body(ids, low, mid, high, window, packed, _, out, waves, parts, *, turn):
     @pl.when(ids[0] == turn)
     def _():
-        for layer in range(GROUP):
-            reach = HALO - layer
-            if layer == 0:
-                pieces = [(lanes(0, 4), low[...]), (lanes(4, 8), mid[...]), (lanes(8, 12), high[...])]
-            else:
-                begin, end = HALO - reach - 1, HALO + OWN + reach + 1
-                pieces = [(lanes(begin + 1, end + 1), waves[layer - 1, :, lanes(begin, end)])]
-            for where, value in pieces:
-                forcing = window[layer, 0:16, where]
-                coef_real = window[layer, 16:17, where]
-                coef_imag = window[layer, 17:18, where]
-                store_parts(parts, where, forcing + scaled(coef_real, coef_imag, value))
-            for spot in range(HALO - reach, HALO + OWN + reach):
-                waves[layer, :, lanes(spot, spot + 1)] = tile_product(parts, packed, layer, spot)
+        for index, source in enumerate((low, mid, high)):
+            down_operand(parts, window, 0, lanes(4 * index, 4 * index + 4), source[...])
+        down_layers(window, packed, waves, parts, range(GROUP))
         out[...] = waves[GROUP - 1, :, lanes(HALO, HALO + OWN)]
 
 
@@ -304,27 +314,15 @@
 
     @pl.when(ids[0] == turn)
     def _():
-        for layer in (first, first + 1):
-            if layer == 0:
-                pieces = [
-                    (lanes(2, 4), low[:, lanes(2, 4)]),
-                    (lanes(4, 8), mid[...]),
-                    (lanes(8, 10), high[:, lanes(0, 2)]),
-                ]
-            elif layer == 2:
-                waves[1, :, lanes(1, 3)] = low[...]
-                waves[1, :, lanes(7, 9)] = high[...]
-                pieces = [(lanes(2, 10), waves[1, :, lanes(1, 9)])]
-            else:
-                pieces = [(lanes(3, 9), waves[layer - 1, :, lanes(2, 8)])]
-            for where, value in pieces:
-                forcing = window[layer, 0:16, where]
-                coef_real = window[layer, 16:17, where]
-                coef_imag = window[layer, 17:18, where]
-                store_parts(parts, where, forcing + scaled(coef_real, coef_imag, value))
-            reach = first + 1 - layer
-            for spot in range(HALO - reach, HALO + OWN + reach):
-                waves[layer, :, lanes(spot, spot + 1)] = tile_product(parts, packed, layer, spot)
+        if first:
+            waves[1, :, lanes(1, 3)] = low[...]
+            waves[1, :, lanes(7, 9)] = high[...]
+            down_operand(parts, window, first, lanes(2, 10), waves[1, :, lanes(1, 9)])
+        else:
+            down_operand(parts, window, first, lanes(2, 4), low[:, lanes(2, 4)])
+            down_operand(parts, window, first, lanes(4, 8), mid[...])
+            down_operand(parts, window, first, lanes(8, 10), high[:, lanes(0, 2)])
+        down_layers(window, packed, waves, parts, (first, first + 1))
         if first:
             outs[0][...] = waves[3, :, lanes(HALO, HALO + OWN)]
         else:
@@ -332,33 +330,28 @@
             outs[1][...] = waves[1, :, lanes(HALO + 2, HALO + OWN)]
 
 
-def up_body(ids, low, mid, high, window, packed, waves, left, right, _, out, field, parts, span, *, turn):
+def up_body(ids, low, mid, high, window, packed, waves, left, right, _, out, field, parts, *, turn):
     @pl.when(ids[0] == turn)
     def _():
+        for index, source in enumerate((low, mid, high)):
+            up_operand(parts, window, GROUP - 1, lanes(4 * index, 4 * index + 4), source[...])
         for layer in reversed(range(GROUP)):
-            reach = layer
-            if layer == GROUP - 1:
-                pieces = [(lanes(0, 4), low[...]), (lanes(4, 8), mid[...]), (lanes(8, 12), high[...])]
-            else:
-                begin, end = HALO - reach - 1, HALO + OWN + reach + 1
-                pieces = [(lanes(begin + 1, end + 1), span[:, lanes(begin, end)])]
-            for where, value in pieces:
-                coef_real = window[layer, 18:19, where]
-                coef_imag = window[layer, 19:20, where]
-                store_parts(parts, where, scaled(coef_real, coef_imag, value))
-            for spot in range(HALO - reach, HALO + OWN + reach):
+            for spot in range(HALO - layer, HALO + OWN + layer):
                 if layer >= 2 and spot < HALO:
                     wave = left[layer - 2, :, lanes(spot + 1, spot + 2)]
                 elif layer >= 2 and spot >= HALO + OWN:
                     wave = right[layer - 2, :, lanes(spot - HALO - OWN, spot - HALO - OWN + 1)]
                 else:
                     wave = waves[layer, :, lanes(spot, spot + 1)]
-                span[:, lanes(spot, spot + 1)] = wave + tile_product(parts, packed, layer, spot)
-            field[layer] = span[:, lanes(HALO, HALO + OWN)]
-        out[...] = span[:, lanes(HALO, HALO + OWN)]
-
-
-PARTS = pltpu.VMEM((32, WINDOW), jnp.bfloat16)
+                value = wave + tile_product(parts.at[layer % 2], packed, layer, spot)
+                if layer:
+                    up_operand(parts, window, layer - 1, lanes(spot + 1, spot + 2), value)
+                if HALO <= spot < HALO + OWN:
+                    field[layer, :, lanes(spot - HALO, spot - HALO + 1)] = value
+        out[...] = field[0]
+
+
+PARTS = pltpu.VMEM((2, 32, WINDOW), jnp.bfloat16)
 
 
 def down_step(ids, received, window, packed, waves, turn):
@@ -403,7 +396,7 @@
             jax.ShapeDtypeStruct((16, HALF), jnp.float32),
             jax.ShapeDtypeStruct((GROUP, 16, HALF), jnp.float32),
         ),
-        scratch_shapes=[PARTS, pltpu.VMEM((16, SPAN), jnp.float32)],
+        scratch_shapes=[PARTS],
         input_output_aliases={9: 1},
         compiler_params=PARAMS,
         cost_estimate=BRIEF,

time: 225 us -> 225 us (level)
  no operation moved by 1% of the time
where the time goes in v4:
time: 225 us; the launch traced here: 224 us
  starting transfers between devices  108 us (48%)
  waiting for transfers between devices  72.3 us (32%)
  Pallas kernels  38.8 us (17%)
  local copies, waits for them, and re-layouts  3.01 us (1%)
    ppermute x48, starting transfers between devices, hop(): return lax.ppermute(value, AXES, pairs)  87.6 us
    ppermute x48, waiting for transfers between devices, hop(): return lax.ppermute(value, AXES, pairs)  69.1 us
    ppermute x5, starting transfers between devices, send_halo(): lax.ppermute(cross, AXES, beside_pairs(rows, False, sides))  12.9 us
    pallas_call x2, Pallas kernels, pack_chip(): pl.pallas_call(functools.partial(chip_body, mine=mine), in_specs=[SMEM_SP...  9.58 us
    pallas_call x8, Pallas kernels, up_step(): pl.pallas_call(functools.partial(up_body, turn=turn), in_specs=[SMEM_SPEC...  7.08 us
    pallas_call x5, Pallas kernels, cut(): pl.pallas_call(functools.partial(cut_body, parts=parts), in_specs=[SMEM_S...  5.53 us
    pallas_call x6, Pallas kernels, pack_halo(): pl.pallas_call(functools.partial(halo_body, rows=rows, slots=slots, split...  5.37 us
    ppermute x5, starting transfers between devices, send_halo(): lax.ppermute(straight, AXES, beside_pairs(rows, True, sides))  4.73 us
  transfers between devices with their start and end apart: 62, of which 16 were waited for; matrix products, arithmetic and copies ran while one was open for 0% of the time, Pallas kernels for 11%

profile of v4, /device:TPU:1, one launch (start us, length us, event | category | flops | bytes accessed | tf_op | source)
XLA Modules:
  0.0 224.1 jit_solution(17100345951190305584)
XLA Ops:
  0.7 1.7 cut_first.1
  2.4 1.5 collective-permute-start
  5.2 5.2 %collective-permute-start.2 = (f32[1,3,2,128,128]{4,3,2,1,0:T(8,128)S(1)}, f32[1,3,2,128,128]{4,3,2,1,0:T(8,128)S(1)}, u32[]{:S(2)}, u32[]{:S(2)}) collective-permute-start(f32[1,3,2,128,128]{4,3,2,1,0:T(8,128)S(1)} %get-tuple-element.79), channel_id=1, source_target_pairs={{1,8},{2,9},{3,10},{4,11},{5,12},{6,13},{7,14},{8,1},{9,2},{10,3},... | collective-permute-start | bytes 1179656 | tf_op jit(solution)/shard_map/ppermute | solution.py:526
  14.1 5.2 %pack_mine.1.refs_0_ = bf16[4,10,384,512]{3,2,1,0:T(8,128)(2,1)S(1)} custom-call(s32[4]{0:T(128)S(1)} %pad_add_fusion.ids, f32[2,8,3,2,128,128]{5,4,3,2,1,0:T(8,128)} %other.5), custom_call_target="tpu_custom_call" | custom-call | flops 1 | bytes 1 | tf_op jit(solution)/shard_map/pack_mine/pallas_call | solution.py:126
  21.8 4.4 %pack_partner.1.refs_0_ = bf16[4,10,384,512]{3,2,1,0:T(8,128)(2,1)S(1)} custom-call(s32[4]{0:T(128)S(1)} %pad_add_fusion.ids, f32[2,8,3,2,128,128]{5,4,3,2,1,0:T(8,128)S(1)} %collective-permute-done.source.other, bf16[4,10,384,512]{3,2,1,0:T(8,128)(2,1)S(1)} %pack_mine.1.refs_0_), custom_call_target="tpu_custom_call", output_to_operand_aliasing={{}: (2, {})} | custom-call | flops 1 | bytes 1 | tf_op jit(solution)/shard_map/pack_partner/pallas_call | solution.py:126
  26.2 1.8 collective-permute-done.2.cross
  32.6 6.0 %collective-permute-start.5 = (f32[16,256]{1,0:T(8,128)S(1)}, f32[16,256]{1,0:T(8,128)S(1)}, u32[]{:S(2)}, u32[]{:S(2)}) collective-permute-start(f32[16,256]{1,0:T(8,128)S(1)} %get-tuple-element.83), channel_id=1, source_target_pairs={{0,8},{8,1},{1,9},{9,2},{2,10},{10,3},{3,11},{11,4},{4,12},{12,5},... | collective-permute-start | bytes 49160 | tf_op jit(solution)/shard_map/ppermute | solution.py:503
  38.6 1.9 collective-permute-start.6
  40.5 3.1 %collective-permute-done.6.high = f32[16,256]{1,0:T(8,128)S(1)} collective-permute-done((f32[16,256]{1,0:T(8,128)S(1)}, f32[16,256]{1,0:T(8,128)S(1)}, u32[]{:S(2)}, u32[]{:S(2)}) %collective-permute-start.6) | collective-permute-done | bytes 16416 | tf_op jit(solution)/shard_map/ppermute | solution.py:503
  44.9 1.5 collective-permute-start.7
  46.4 1.6 collective-permute-start.8
  50.8 3.9 %collective-permute-start.10 = (f32[16,256]{1,0:T(8,128)S(1)}, f32[16,256]{1,0:T(8,128)S(1)}, u32[]{:S(2)}, u32[]{:S(2)}) collective-permute-start(f32[16,256]{1,0:T(8,128)S(1)} %get-tuple-element.88), channel_id=1, source_target_pairs={{0,8},{8,1},{1,9},{9,2},{2,10},{10,3},{3,11},{11,4},{4,12},{12,5},... | collective-permute-start | bytes 49160 | tf_op jit(solution)/shard_map/ppermute | solution.py:503
  54.8 1.9 collective-permute-start.11
  56.7 3.1 %collective-permute-done.11.high = f32[16,256]{1,0:T(8,128)S(1)} collective-permute-done((f32[16,256]{1,0:T(8,128)S(1)}, f32[16,256]{1,0:T(8,128)S(1)}, u32[]{:S(2)}, u32[]{:S(2)}) %collective-permute-start.11) | collective-permute-done | bytes 16416 | tf_op jit(solution)/shard_map/ppermute | solution.py:503
  68.3 21.0 %collective-permute-start.20 = (f32[16,512]{1,0:T(8,128)S(1)}, f32[16,512]{1,0:T(8,128)S(1)}, u32[]{:S(2)}, u32[]{:S(2)}) collective-permute-start(f32[16,512]{1,0:T(8,128)S(1)} %get-tuple-element.102), channel_id=1, source_target_pairs={{0,24},{8,17},{1,25},{9,18},{2,26},{10,19},{3,27},{11,20},{4,28},{... | collective-permute-start | bytes 98312 | tf_op jit(solution)/shard_map/ppermute | solution.py:503
  96.9 2.0 cut_late.1
  100.2 4.9 %collective-permute-start.43 = (f32[2,3,2,128,128]{4,3,2,1,0:T(8,128)S(1)}, f32[2,3,2,128,128]{4,3,2,1,0:T(8,128)S(1)}, u32[]{:S(2)}, u32[]{:S(2)}) collective-permute-start(f32[2,3,2,128,128]{4,3,2,1,0:T(8,128)S(1)} %get-tuple-element.128), channel_id=1, source_target_pairs={{1,8},{2,9},{3,10},{4,11},{5,12},{6,13},{7,14},{8,1},{9,2},{10,3},... | collective-permute-start | bytes 2359304 | tf_op jit(solution)/shard_map/ppermute | solution.py:526
  107.7 9.6 %collective-permute-start.31 = (f32[16,512]{1,0:T(8,128)S(1)}, f32[16,512]{1,0:T(8,128)S(1)}, u32[]{:S(2)}, u32[]{:S(2)}) collective-permute-start(f32[16,512]{1,0:T(8,128)S(1)} %get-tuple-element.114), channel_id=1, source_target_pairs={{0,24},{8,17},{1,25},{9,18},{2,26},{10,19},{3,27},{11,20},{4,28},{... | collective-permute-start | bytes 98312 | tf_op jit(solution)/shard_map/ppermute | solution.py:503
  117.3 1.6 collective-permute-start.32
  122.3 3.9 %collective-permute-start.34 = (f32[2,16,512]{2,1,0:T(8,128)S(1)}, f32[2,16,512]{2,1,0:T(8,128)S(1)}, u32[]{:S(2)}, u32[]{:S(2)}) collective-permute-start(f32[2,16,512]{2,1,0:T(8,128)S(1)} %slice.3), channel_id=1, source_target_pairs={{0,8},{8,1},{1,9},{9,2},{2,10},{10,3},{3,11},{11,4},{4,12},{12,5},... | collective-permute-start | bytes 196616 | tf_op jit(solution)/shard_map/ppermute | solution.py:503
  126.3 1.9 collective-permute-start.35
  128.2 10.7 %collective-permute-done.34.left = f32[2,16,512]{2,1,0:T(8,128)S(1)} collective-permute-done((f32[2,16,512]{2,1,0:T(8,128)S(1)}, f32[2,16,512]{2,1,0:T(8,128)S(1)}, u32[]{:S(2)}, u32[]{:S(2)}) %collective-permute-start.34) | collective-permute-done | bytes 65568 | tf_op jit(solution)/shard_map/ppermute | solution.py:503
  143.4 1.3 collective-permute-done.36.low
  144.7 5.4 %collective-permute-done.37.mid = f32[16,512]{1,0:T(8,128)S(1)} collective-permute-done((f32[16,512]{1,0:T(8,128)S(1)}, f32[16,512]{1,0:T(8,128)S(1)}, u32[]{:S(2)}, u32[]{:S(2)}) %collective-permute-start.37) | collective-permute-done | bytes 32800 | tf_op jit(solution)/shard_map/ppermute | solution.py:503
  150.1 3.8 %collective-permute-done.38.high = f32[16,512]{1,0:T(8,128)S(1)} collective-permute-done((f32[16,512]{1,0:T(8,128)S(1)}, f32[16,512]{1,0:T(8,128)S(1)}, u32[]{:S(2)}, u32[]{:S(2)}) %collective-permute-start.38) | collective-permute-done | bytes 32800 | tf_op jit(solution)/shard_map/ppermute | solution.py:503
  157.7 1.7 halo_late.1.packed.refs_0_
  168.7 22.7 %collective-permute-done.47.low = f32[16,512]{1,0:T(8,128)S(1)} collective-permute-done((f32[16,512]{1,0:T(8,128)S(1)}, f32[16,512]{1,0:T(8,128)S(1)}, u32[]{:S(2)}, u32[]{:S(2)}) %collective-permute-start.47) | collective-permute-done | bytes 32800 | tf_op jit(solution)/shard_map/ppermute | solution.py:503
  191.3 3.7 %collective-permute-done.49.high = f32[16,512]{1,0:T(8,128)S(1)} collective-permute-done((f32[16,512]{1,0:T(8,128)S(1)}, f32[16,512]{1,0:T(8,128)S(1)}, u32[]{:S(2)}, u32[]{:S(2)}) %collective-permute-start.49) | collective-permute-done | bytes 32800 | tf_op jit(solution)/shard_map/ppermute | solution.py:503
  205.5 9.5 %collective-permute-done.58.low = f32[16,512]{1,0:T(8,128)S(1)} collective-permute-done((f32[16,512]{1,0:T(8,128)S(1)}, f32[16,512]{1,0:T(8,128)S(1)}, u32[]{:S(2)}, u32[]{:S(2)}) %collective-permute-start.58) | collective-permute-done | bytes 32800 | tf_op jit(solution)/shard_map/ppermute | solution.py:503
  215.2 2.6 %collective-permute-done.60.high = f32[16,512]{1,0:T(8,128)S(1)} collective-permute-done((f32[16,512]{1,0:T(8,128)S(1)}, f32[16,512]{1,0:T(8,128)S(1)}, u32[]{:S(2)}, u32[]{:S(2)}) %collective-permute-start.60) | collective-permute-done | bytes 32800 | tf_op jit(solution)/shard_map/ppermute | solution.py:503
  217.8 3.0 %up_0.1 = (f32[16,512]{1,0:T(8,128)}, f32[4,16,512]{2,1,0:T(8,128)S(1)}) custom-call(s32[4]{0:T(128)S(1)} %pad_add_fusion.ids, f32[16,512]{1,0:T(8,128)S(1)} %collective-permute-done.58.low, f32[16,512]{1,0:T(8,128)S(1)} %collective-permute-done.59.mid, f32[16,512]{1,0:T(8,128)S(1)} %collective-permute-done.60.high, ...), custom_call_target="tpu_custom_call", output_to_operand_aliasing={{1}: (9, {})} | custom-call | flops 1 | bytes 1 | tf_op jit(solution)/shard_map/up_0/pallas_call | solution.py:391
  221.5 1.3 collective-permute-done.61.taken
  (141 shorter events, 68.9 us)
Async XLA Ops:
  2.4 19.3 %collective-permute-start = (f32[2,8,3,2,128,128]{5,4,3,2,1,0:T(8,128)}, f32[2,8,3,2,128,128]{5,4,3,2,1,0:T(8,128)S(1)}, u32[]{:S(2)}, u32[]{:S(2)}) collective-permute-start(f32[2,8,3,2,128,128]{5,4,3,2,1,0:T(8,128)} %other.5), channel_id=1, source_target_pairs={{0,8},{1,9},{2,10},{3,11},{4,12},{5,13},{6,14},{7,15},{8,0},{9,1},... | collective-permute-start | bytes 18874376 | tf_op jit(solution)/shard_map/ppermute | solution.py:534
  3.9 22.2 %collective-permute-start.1 = (f32[1,3,2,128,128]{4,3,2,1,0:T(8,128)S(1)}, f32[1,3,2,128,128]{4,3,2,1,0:T(8,128)S(1)}, u32[]{:S(2)}, u32[]{:S(2)}) collective-permute-start(f32[1,3,2,128,128]{4,3,2,1,0:T(8,128)S(1)} %get-tuple-element.75), channel_id=1, source_target_pairs={{0,1},{1,2},{2,3},{3,4},{4,5},{5,6},{6,7},{9,8},{10,9},{11,10},{12... | collective-permute-start | bytes 1179656 | tf_op jit(solution)/shard_map/ppermute | solution.py:525
  5.2 22.8 %collective-permute-start.2 = (f32[1,3,2,128,128]{4,3,2,1,0:T(8,128)S(1)}, f32[1,3,2,128,128]{4,3,2,1,0:T(8,128)S(1)}, u32[]{:S(2)}, u32[]{:S(2)}) collective-permute-start(f32[1,3,2,128,128]{4,3,2,1,0:T(8,128)S(1)} %get-tuple-element.79), channel_id=1, source_target_pairs={{1,8},{2,9},{3,10},{4,11},{5,12},{6,13},{7,14},{8,1},{9,2},{10,3},... | collective-permute-start | bytes 1179656 | tf_op jit(solution)/shard_map/ppermute | solution.py:526
  14.0 5.3 %collective-permute-start.3 = (f32[2,20,1024]{2,1,0:T(8,128)S(1)}, f32[2,20,1024]{2,1,0:T(8,128)S(1)}, u32[]{:S(2)}, u32[]{:S(2)}) collective-permute-start(f32[2,20,1024]{2,1,0:T(8,128)S(1)} %rows.1), channel_id=1, source_target_pairs={{0,8},{1,9},{2,10},{3,11},{4,12},{5,13},{6,14},{7,15},{8,0},{9,1},... | collective-permute-start | bytes 491528 | tf_op jit(solution)/shard_map/ppermute | solution.py:543
  19.8 8.2 %collective-permute-start.4 = (f32[4,20,512]{2,1,0:T(8,128)S(1)}, f32[4,20,512]{2,1,0:T(8,128)S(1)}, u32[]{:S(2)}, u32[]{:S(2)}) collective-permute-start(f32[4,20,512]{2,1,0:T(8,128)S(1)} %edge.1), channel_id=1, source_target_pairs={{0,1},{1,2},{2,3},{3,4},{4,5},{5,6},{6,7},{9,8},{10,9},{11,10},{12... | collective-permute-start | bytes 491528 | tf_op jit(solution)/shard_map/ppermute | solution.py:549
  28.6 31.8 %collective-permute-start.12 = (f32[4,3,2,128,128]{4,3,2,1,0:T(8,128)S(1)}, f32[4,3,2,128,128]{4,3,2,1,0:T(8,128)S(1)}, u32[]{:S(2)}, u32[]{:S(2)}) collective-permute-start(f32[4,3,2,128,128]{4,3,2,1,0:T(8,128)S(1)} %get-tuple-element.95), channel_id=1, source_target_pairs={{32,33},{33,34},{34,35},{35,36},{36,37},{37,38},{38,39},{48,49},{4... | collective-permute-start | bytes 4718600 | tf_op jit(solution)/shard_map/ppermute | solution.py:525
  29.4 31.1 %collective-permute-start.13 = (f32[4,3,2,128,128]{4,3,2,1,0:T(8,128)S(1)}, f32[4,3,2,128,128]{4,3,2,1,0:T(8,128)S(1)}, u32[]{:S(2)}, u32[]{:S(2)}) collective-permute-start(f32[4,3,2,128,128]{4,3,2,1,0:T(8,128)S(1)} %get-tuple-element.96), channel_id=1, source_target_pairs={{33,40},{34,41},{35,42},{36,43},{37,44},{38,45},{39,46},{49,56},{5... | collective-permute-start | bytes 4718600 | tf_op jit(solution)/shard_map/ppermute | solution.py:526
  32.6 7.9 %collective-permute-start.5 = (f32[16,256]{1,0:T(8,128)S(1)}, f32[16,256]{1,0:T(8,128)S(1)}, u32[]{:S(2)}, u32[]{:S(2)}) collective-permute-start(f32[16,256]{1,0:T(8,128)S(1)} %get-tuple-element.83), channel_id=1, source_target_pairs={{0,8},{8,1},{1,9},{9,2},{2,10},{10,3},{3,11},{11,4},{4,12},{12,5},... | collective-permute-start | bytes 49160 | tf_op jit(solution)/shard_map/ppermute | solution.py:503
  38.6 5.1 %collective-permute-start.6 = (f32[16,256]{1,0:T(8,128)S(1)}, f32[16,256]{1,0:T(8,128)S(1)}, u32[]{:S(2)}, u32[]{:S(2)}) collective-permute-start(f32[16,256]{1,0:T(8,128)S(1)} %get-tuple-element.84.mid), channel_id=1, source_target_pairs={{8,0},{1,8},{9,1},{2,9},{10,2},{3,10},{11,3},{4,11},{12,4},{5,12},... | collective-permute-start | bytes 49160 | tf_op jit(solution)/shard_map/ppermute | solution.py:503
  44.9 4.4 %collective-permute-start.7 = (f32[16,512]{1,0:T(8,128)S(1)}, f32[16,512]{1,0:T(8,128)S(1)}, u32[]{:S(2)}, u32[]{:S(2)}) collective-permute-start(f32[16,512]{1,0:T(8,128)S(1)} %get-tuple-element.86), channel_id=1, source_target_pairs={{0,24},{8,17},{1,25},{9,18},{2,26},{10,19},{3,27},{11,20},{4,28},{... | collective-permute-start | bytes 98312 | tf_op jit(solution)/shard_map/ppermute | solution.py:503
  50.8 5.9 %collective-permute-start.10 = (f32[16,256]{1,0:T(8,128)S(1)}, f32[16,256]{1,0:T(8,128)S(1)}, u32[]{:S(2)}, u32[]{:S(2)}) collective-permute-start(f32[16,256]{1,0:T(8,128)S(1)} %get-tuple-element.88), channel_id=1, source_target_pairs={{0,8},{8,1},{1,9},{9,2},{2,10},{10,3},{3,11},{11,4},{4,12},{12,5},... | collective-permute-start | bytes 49160 | tf_op jit(solution)/shard_map/ppermute | solution.py:503
  54.8 5.1 %collective-permute-start.11 = (f32[16,256]{1,0:T(8,128)S(1)}, f32[16,256]{1,0:T(8,128)S(1)}, u32[]{:S(2)}, u32[]{:S(2)}) collective-permute-start(f32[16,256]{1,0:T(8,128)S(1)} %get-tuple-element.89.mid), channel_id=1, source_target_pairs={{8,0},{1,8},{9,1},{2,9},{10,2},{3,10},{11,3},{4,11},{12,4},{5,12},... | collective-permute-start | bytes 49160 | tf_op jit(solution)/shard_map/ppermute | solution.py:503
  61.1 35.2 %collective-permute-start.26 = (f32[2,3,2,128,128]{4,3,2,1,0:T(8,128)S(1)}, f32[2,3,2,128,128]{4,3,2,1,0:T(8,128)S(1)}, u32[]{:S(2)}, u32[]{:S(2)}) collective-permute-start(f32[2,3,2,128,128]{4,3,2,1,0:T(8,128)S(1)} %get-tuple-element.109), channel_id=1, source_target_pairs={{80,81},{81,82},{82,83},{83,84},{84,85},{85,86},{86,87},{89,88},{9... | collective-permute-start | bytes 2359304 | tf_op jit(solution)/shard_map/ppermute | solution.py:525
  61.8 34.5 %collective-permute-start.27 = (f32[2,3,2,128,128]{4,3,2,1,0:T(8,128)S(1)}, f32[2,3,2,128,128]{4,3,2,1,0:T(8,128)S(1)}, u32[]{:S(2)}, u32[]{:S(2)}) collective-permute-start(f32[2,3,2,128,128]{4,3,2,1,0:T(8,128)S(1)} %get-tuple-element.110), channel_id=1, source_target_pairs={{81,88},{82,89},{83,90},{84,91},{85,92},{86,93},{87,94},{88,81},{8... | collective-permute-start | bytes 2359304 | tf_op jit(solution)/shard_map/ppermute | solution.py:526
  68.3 23.6 %collective-permute-start.20 = (f32[16,512]{1,0:T(8,128)S(1)}, f32[16,512]{1,0:T(8,128)S(1)}, u32[]{:S(2)}, u32[]{:S(2)}) collective-permute-start(f32[16,512]{1,0:T(8,128)S(1)} %get-tuple-element.102), channel_id=1, source_target_pairs={{0,24},{8,17},{1,25},{9,18},{2,26},{10,19},{3,27},{11,20},{4,28},{... | collective-permute-start | bytes 98312 | tf_op jit(solution)/shard_map/ppermute | solution.py:503
  98.9 58.8 %collective-permute-start.42 = (f32[2,3,2,128,128]{4,3,2,1,0:T(8,128)S(1)}, f32[2,3,2,128,128]{4,3,2,1,0:T(8,128)S(1)}, u32[]{:S(2)}, u32[]{:S(2)}) collective-permute-start(f32[2,3,2,128,128]{4,3,2,1,0:T(8,128)S(1)} %get-tuple-element.127), channel_id=1, source_target_pairs={{0,1},{1,2},{2,3},{3,4},{4,5},{5,6},{6,7},{9,8},{10,9},{11,10},{12... | collective-permute-start | bytes 2359304 | tf_op jit(solution)/shard_map/ppermute | solution.py:525
  100.2 57.5 %collective-permute-start.43 = (f32[2,3,2,128,128]{4,3,2,1,0:T(8,128)S(1)}, f32[2,3,2,128,128]{4,3,2,1,0:T(8,128)S(1)}, u32[]{:S(2)}, u32[]{:S(2)}) collective-permute-start(f32[2,3,2,128,128]{4,3,2,1,0:T(8,128)S(1)} %get-tuple-element.128), channel_id=1, source_target_pairs={{1,8},{2,9},{3,10},{4,11},{5,12},{6,13},{7,14},{8,1},{9,2},{10,3},... | collective-permute-start | bytes 2359304 | tf_op jit(solution)/shard_map/ppermute | solution.py:526
  107.7 12.5 %collective-permute-start.31 = (f32[16,512]{1,0:T(8,128)S(1)}, f32[16,512]{1,0:T(8,128)S(1)}, u32[]{:S(2)}, u32[]{:S(2)}) collective-permute-start(f32[16,512]{1,0:T(8,128)S(1)} %get-tuple-element.114), channel_id=1, source_target_pairs={{0,24},{8,17},{1,25},{9,18},{2,26},{10,19},{3,27},{11,20},{4,28},{... | collective-permute-start | bytes 98312 | tf_op jit(solution)/shard_map/ppermute | solution.py:503
  117.3 2.9 %collective-permute-start.32 = (f32[16,512]{1,0:T(8,128)S(1)}, f32[16,512]{1,0:T(8,128)S(1)}, u32[]{:S(2)}, u32[]{:S(2)}) collective-permute-start(f32[16,512]{1,0:T(8,128)S(1)} %get-tuple-element.114), channel_id=1, source_target_pairs={{0,16},{8,24},{1,17},{9,25},{2,18},{10,26},{3,19},{11,27},{4,20},{... | collective-permute-start | bytes 98312 | tf_op jit(solution)/shard_map/ppermute | solution.py:503
  122.3 16.6 %collective-permute-start.34 = (f32[2,16,512]{2,1,0:T(8,128)S(1)}, f32[2,16,512]{2,1,0:T(8,128)S(1)}, u32[]{:S(2)}, u32[]{:S(2)}) collective-permute-start(f32[2,16,512]{2,1,0:T(8,128)S(1)} %slice.3), channel_id=1, source_target_pairs={{0,8},{8,1},{1,9},{9,2},{2,10},{10,3},{3,11},{11,4},{4,12},{12,5},... | collective-permute-start | bytes 196616 | tf_op jit(solution)/shard_map/ppermute | solution.py:503
  126.3 12.7 %collective-permute-start.35 = (f32[2,16,512]{2,1,0:T(8,128)S(1)}, f32[2,16,512]{2,1,0:T(8,128)S(1)}, u32[]{:S(2)}, u32[]{:S(2)}) collective-permute-start(f32[2,16,512]{2,1,0:T(8,128)S(1)} %slice.3), channel_id=1, source_target_pairs={{8,0},{1,8},{9,1},{2,9},{10,2},{3,10},{11,3},{4,11},{12,4},{5,12},... | collective-permute-start | bytes 196616 | tf_op jit(solution)/shard_map/ppermute | solution.py:503
  139.5 5.2 %collective-permute-start.36 = (f32[16,512]{1,0:T(8,128)S(1)}, f32[16,512]{1,0:T(8,128)S(1)}, u32[]{:S(2)}, u32[]{:S(2)}) collective-permute-start(f32[16,512]{1,0:T(8,128)S(1)} %get-tuple-element.117), channel_id=1, source_target_pairs={{16,8},{24,1},{17,9},{25,2},{18,10},{26,3},{19,11},{27,4},{20,12},... | collective-permute-start | bytes 98312 | tf_op jit(solution)/shard_map/ppermute | solution.py:503
  140.8 9.3 %collective-permute-start.37 = (f32[16,512]{1,0:T(8,128)S(1)}, f32[16,512]{1,0:T(8,128)S(1)}, u32[]{:S(2)}, u32[]{:S(2)}) collective-permute-start(f32[16,512]{1,0:T(8,128)S(1)} %get-tuple-element.117), channel_id=1, source_target_pairs={{16,0},{24,8},{17,1},{25,9},{18,2},{26,10},{19,3},{27,11},{20,4},{... | collective-permute-start | bytes 98312 | tf_op jit(solution)/shard_map/ppermute | solution.py:503
  142.1 11.8 %collective-permute-start.38 = (f32[16,512]{1,0:T(8,128)S(1)}, f32[16,512]{1,0:T(8,128)S(1)}, u32[]{:S(2)}, u32[]{:S(2)}) collective-permute-start(f32[16,512]{1,0:T(8,128)S(1)} %get-tuple-element.117), channel_id=1, source_target_pairs={{24,0},{17,8},{25,1},{18,9},{26,2},{19,10},{27,3},{20,11},{28,4},{... | collective-permute-start | bytes 98312 | tf_op jit(solution)/shard_map/ppermute | solution.py:503
  162.8 35.4 %collective-permute-start.53 = (f32[1,3,2,128,128]{4,3,2,1,0:T(8,128)S(1)}, f32[1,3,2,128,128]{4,3,2,1,0:T(8,128)S(1)}, u32[]{:S(2)}, u32[]{:S(2)}) collective-permute-start(f32[1,3,2,128,128]{4,3,2,1,0:T(8,128)S(1)} %get-tuple-element.139), channel_id=1, source_target_pairs={{0,1},{1,2},{2,3},{3,4},{4,5},{5,6},{6,7},{16,17},{17,18},{18,19},... | collective-permute-start | bytes 1179656 | tf_op jit(solution)/shard_map/ppermute | solution.py:525
  163.5 34.7 %collective-permute-start.54 = (f32[1,3,2,128,128]{4,3,2,1,0:T(8,128)S(1)}, f32[1,3,2,128,128]{4,3,2,1,0:T(8,128)S(1)}, u32[]{:S(2)}, u32[]{:S(2)}) collective-permute-start(f32[1,3,2,128,128]{4,3,2,1,0:T(8,128)S(1)} %get-tuple-element.140), channel_id=1, source_target_pairs={{1,8},{2,9},{3,10},{4,11},{5,12},{6,13},{7,14},{17,24},{18,25},{19... | collective-permute-start | bytes 1179656 | tf_op jit(solution)/shard_map/ppermute | solution.py:526
  164.8 26.6 %collective-permute-start.47 = (f32[16,512]{1,0:T(8,128)S(1)}, f32[16,512]{1,0:T(8,128)S(1)}, u32[]{:S(2)}, u32[]{:S(2)}) collective-permute-start(f32[16,512]{1,0:T(8,128)S(1)} %get-tuple-element.132), channel_id=1, source_target_pairs={{16,8},{24,1},{17,9},{25,2},{18,10},{26,3},{19,11},{27,4},{20,12},... | collective-permute-start | bytes 98312 | tf_op jit(solution)/shard_map/ppermute | solution.py:503
  166.1 25.3 %collective-permute-start.48 = (f32[16,512]{1,0:T(8,128)S(1)}, f32[16,512]{1,0:T(8,128)S(1)}, u32[]{:S(2)}, u32[]{:S(2)}) collective-permute-start(f32[16,512]{1,0:T(8,128)S(1)} %get-tuple-element.132), channel_id=1, source_target_pairs={{16,0},{24,8},{17,1},{25,9},{18,2},{26,10},{19,3},{27,11},{20,4},{... | collective-permute-start | bytes 98312 | tf_op jit(solution)/shard_map/ppermute | solution.py:503
  167.4 27.6 %collective-permute-start.49 = (f32[16,512]{1,0:T(8,128)S(1)}, f32[16,512]{1,0:T(8,128)S(1)}, u32[]{:S(2)}, u32[]{:S(2)}) collective-permute-start(f32[16,512]{1,0:T(8,128)S(1)} %get-tuple-element.132), channel_id=1, source_target_pairs={{24,0},{17,8},{25,1},{18,9},{26,2},{19,10},{27,3},{20,11},{28,4},{... | collective-permute-start | bytes 98312 | tf_op jit(solution)/shard_map/ppermute | solution.py:503
  201.6 13.4 %collective-permute-start.58 = (f32[16,512]{1,0:T(8,128)S(1)}, f32[16,512]{1,0:T(8,128)S(1)}, u32[]{:S(2)}, u32[]{:S(2)}) collective-permute-start(f32[16,512]{1,0:T(8,128)S(1)} %get-tuple-element.144), channel_id=1, source_target_pairs={{16,8},{24,1},{17,9},{25,2},{18,10},{26,3},{19,11},{27,4},{20,12},... | collective-permute-start | bytes 98312 | tf_op jit(solution)/shard_map/ppermute | solution.py:503
  202.9 12.3 %collective-permute-start.59 = (f32[16,512]{1,0:T(8,128)S(1)}, f32[16,512]{1,0:T(8,128)S(1)}, u32[]{:S(2)}, u32[]{:S(2)}) collective-permute-start(f32[16,512]{1,0:T(8,128)S(1)} %get-tuple-element.144), channel_id=1, source_target_pairs={{16,0},{24,8},{17,1},{25,9},{18,2},{26,10},{19,3},{27,11},{20,4},{... | collective-permute-start | bytes 98312 | tf_op jit(solution)/shard_map/ppermute | solution.py:503
  204.2 13.6 %collective-permute-start.60 = (f32[16,512]{1,0:T(8,128)S(1)}, f32[16,512]{1,0:T(8,128)S(1)}, u32[]{:S(2)}, u32[]{:S(2)}) collective-permute-start(f32[16,512]{1,0:T(8,128)S(1)} %get-tuple-element.144), channel_id=1, source_target_pairs={{24,0},{17,8},{25,1},{18,9},{26,2},{19,10},{27,3},{20,11},{28,4},{... | collective-permute-start | bytes 98312 | tf_op jit(solution)/shard_map/ppermute | solution.py:503
  (34 other events, 49.3 us)

commit v5 on v4

--- a/solution.py
+++ b/solution.py
@@ -300,8 +300,12 @@
                 down_operand(parts, window, layer + 1, lanes(spot + 1, spot + 2), value)
 
 
-def down_body(ids, low, mid, high, window, packed, _, out, waves, parts, *, turn):
-    @pl.when(ids[0] == turn)
+def my_turn(turn):
+    return lax.axis_index("depth") // 2 == turn
+
+
+def down_body(low, mid, high, window, packed, _, out, waves, parts, *, turn):
+    @pl.when(my_turn(turn))
     def _():
         for index, source in enumerate((low, mid, high)):
             down_operand(parts, window, 0, lanes(4 * index, 4 * index + 4), source[...])
@@ -309,10 +313,10 @@
         out[...] = waves[GROUP - 1, :, lanes(HALO, HALO + OWN)]
 
 
-def pair_body(ids, low, mid, high, window, packed, _, *refs, turn, first):
+def pair_body(low, mid, high, window, packed, _, *refs, turn, first):
     outs, waves, parts = refs[:-2], refs[-2], refs[-1]
 
-    @pl.when(ids[0] == turn)
+    @pl.when(my_turn(turn))
     def _():
         if first:
             waves[1, :, lanes(1, 3)] = low[...]
@@ -330,8 +334,8 @@
             outs[1][...] = waves[1, :, lanes(HALO + 2, HALO + OWN)]
 
 
-def up_body(ids, low, mid, high, window, packed, waves, left, right, _, out, field, parts, *, turn):
-    @pl.when(ids[0] == turn)
+def up_body(low, mid, high, window, packed, waves, left, right, _, out, field, parts, *, turn):
+    @pl.when(my_turn(turn))
     def _():
         for index, source in enumerate((low, mid, high)):
             up_operand(parts, window, GROUP - 1, lanes(4 * index, 4 * index + 4), source[...])
@@ -354,54 +358,54 @@
 PARTS = pltpu.VMEM((2, 32, WINDOW), jnp.bfloat16)
 
 
-def down_step(ids, received, window, packed, waves, turn):
+def down_step(received, window, packed, waves, turn):
     return pl.pallas_call(
         functools.partial(down_body, turn=turn),
-        in_specs=[SMEM_SPEC] + [VMEM_SPEC] * 6,
+        in_specs=[VMEM_SPEC] * 6,
         out_specs=(VMEM_SPEC, VMEM_SPEC),
         out_shape=(
             jax.ShapeDtypeStruct((16, HALF), jnp.float32),
             jax.ShapeDtypeStruct((GROUP, 16, SPAN), jnp.float32),
         ),
         scratch_shapes=[PARTS],
-        input_output_aliases={6: 1},
+        input_output_aliases={5: 1},
         compiler_params=PARAMS,
         cost_estimate=BRIEF,
         name=f"down_{turn}",
-    )(ids, *received, window, packed, waves)
-
-
-def pair_step(ids, low, mid, high, window, packed, waves, turn, first):
+    )(*received, window, packed, waves)
+
+
+def pair_step(low, mid, high, window, packed, waves, turn, first):
     widths = (HALF,) if first else (2 * TILE, 2 * TILE)
     return pl.pallas_call(
         functools.partial(pair_body, turn=turn, first=first),
-        in_specs=[SMEM_SPEC] + [VMEM_SPEC] * 6,
+        in_specs=[VMEM_SPEC] * 6,
         out_specs=(VMEM_SPEC,) * (len(widths) + 1),
         out_shape=tuple(jax.ShapeDtypeStruct((16, width), jnp.float32) for width in widths)
         + (jax.ShapeDtypeStruct((GROUP, 16, SPAN), jnp.float32),),
         scratch_shapes=[PARTS],
-        input_output_aliases={6: len(widths)},
+        input_output_aliases={5: len(widths)},
         compiler_params=PARAMS,
         cost_estimate=BRIEF,
         name=f"pair_{turn}_{first}",
-    )(ids, low, mid, high, window, packed, waves)
-
-
-def up_step(ids, received, window, packed, waves, left, right, field, turn):
+    )(low, mid, high, window, packed, waves)
+
+
+def up_step(received, window, packed, waves, left, right, field, turn):
     return pl.pallas_call(
         functools.partial(up_body, turn=turn),
-        in_specs=[SMEM_SPEC] + [VMEM_SPEC] * 9,
+        in_specs=[VMEM_SPEC] * 9,
         out_specs=(VMEM_SPEC, VMEM_SPEC),
         out_shape=(
             jax.ShapeDtypeStruct((16, HALF), jnp.float32),
             jax.ShapeDtypeStruct((GROUP, 16, HALF), jnp.float32),
         ),
         scratch_shapes=[PARTS],
-        input_output_aliases={9: 1},
+        input_output_aliases={8: 1},
         compiler_params=PARAMS,
         cost_estimate=BRIEF,
         name=f"up_{turn}",
-    )(ids, *received, window, packed, waves, left, right, field)
+    )(*received, window, packed, waves, left, right, field)
 
 
 def give_body(ids, waves, field, give):
@@ -563,11 +567,11 @@
     for turn in everyone:
         if turn < PAIR_ROWS:
             left_edge, right_edge, waves = pair_step(
-                ids, *received, window, packed, waves, turn, 0
+                *received, window, packed, waves, turn, 0
             )
             pairs = range(PAIR_ROWS)
             low, high = hop(right_edge, pairs, 0, 1), hop(left_edge, pairs, 0, -1)
-            out, waves = pair_step(ids, low, left_edge, high, window, packed, waves, turn, 2)
+            out, waves = pair_step(low, left_edge, high, window, packed, waves, turn, 2)
             if turn + 1 == PAIR_ROWS:
                 down_rows = (PAIR_ROWS, chip_rows)
                 packed = pack_halo(
@@ -576,7 +580,7 @@
                 _, early_halo = send_halo(gated(ids, out, *halo), other, early_parts, "cut_early")
                 out, packed = lax.optimization_barrier((out, packed))
         else:
-            out, waves = down_step(ids, received, window, packed, waves, turn)
+            out, waves = down_step(received, window, packed, waves, turn)
             if turn == LATE_ROWS:
                 late_ids, last_rows = gated(ids, out), (LATE_ROWS + 1, chip_rows)
                 packed = pack_halo(late_ids, early_halo, packed, last_rows, EARLY_SLOTS, "halo_last")
@@ -590,7 +594,7 @@
     left, right = hop(deep, everyone, 0, 1), hop(deep, everyone, 0, -1)
     received = (zero_half,) * 3
     for turn in reversed(everyone):
-        out, field = up_step(ids, received, window, packed, waves, left, right, field, turn)
+        out, field = up_step(received, window, packed, waves, left, right, field, turn)
         if turn == LATE_ROWS + 1:
             row = (LATE_ROWS, LATE_ROWS + 1)
             packed = pack_halo(gated(ids, out), early_halo, packed, row, EARLY_SLOTS, "halo_early")

time: 225 us -> 219 us (0.973)
  Pallas kernels: 38.8 us -> 29.2 us
    pallas_call x14, Pallas kernels: 11.2 us -> 3.7 us  [the longest x8 2.81 us: up_step(): pl.pallas_call(functools.partial(up_body, turn=turn), in_specs=[VMEM_SPEC...]
  transfers between devices with their start and end apart: 62 -> 62, of which waited for: 16 -> 16; matrix products, arithmetic and copies ran while one was open for 0% -> 0% of each run, Pallas kernels for 11% -> 7%
where the time goes in v5:
time: 219 us; the launch traced here: 218 us
  starting transfers between devices  110 us (50%)
  waiting for transfers between devices  73.5 us (34%)
  Pallas kernels  29.2 us (13%)
  local copies, waits for them, and re-layouts  3.01 us (1%)
    ppermute x48, starting transfers between devices, hop(): return lax.ppermute(value, AXES, pairs)  89.5 us
    ppermute x48, waiting for transfers between devices, hop(): return lax.ppermute(value, AXES, pairs)  70.4 us
    ppermute x5, starting transfers between devices, send_halo(): lax.ppermute(cross, AXES, beside_pairs(rows, False, sides))  12.9 us
    pallas_call x2, Pallas kernels, pack_chip(): pl.pallas_call(functools.partial(chip_body, mine=mine), in_specs=[SMEM_SP...  9.58 us
    pallas_call x5, Pallas kernels, cut(): pl.pallas_call(functools.partial(cut_body, parts=parts), in_specs=[SMEM_S...  5.53 us
    pallas_call x6, Pallas kernels, pack_halo(): pl.pallas_call(functools.partial(halo_body, rows=rows, slots=slots, split...  5.36 us
    ppermute x5, starting transfers between devices, send_halo(): lax.ppermute(straight, AXES, beside_pairs(rows, True, sides))  4.73 us
  transfers between devices with their start and end apart: 62, of which 16 were waited for; matrix products, arithmetic and copies ran while one was open for 0% of the time, Pallas kernels for 7%

profile of v5, /device:TPU:1, one launch (start us, length us, event | category | flops | bytes accessed | tf_op | source)
XLA Modules:
  0.0 217.6 jit_solution(16419905117629507916)
XLA Ops:
  0.7 1.7 cut_first.1
  2.4 1.5 collective-permute-start
  5.2 5.2 %collective-permute-start.2 = (f32[1,3,2,128,128]{4,3,2,1,0:T(8,128)S(1)}, f32[1,3,2,128,128]{4,3,2,1,0:T(8,128)S(1)}, u32[]{:S(2)}, u32[]{:S(2)}) collective-permute-start(f32[1,3,2,128,128]{4,3,2,1,0:T(8,128)S(1)} %get-tuple-element.79), channel_id=1, source_target_pairs={{1,8},{2,9},{3,10},{4,11},{5,12},{6,13},{7,14},{8,1},{9,2},{10,3},... | collective-permute-start | bytes 1179656 | tf_op jit(solution)/shard_map/ppermute | solution.py:530
  14.1 5.2 %pack_mine.1.refs_0_ = bf16[4,10,384,512]{3,2,1,0:T(8,128)(2,1)S(1)} custom-call(s32[4]{0:T(128)S(1)} %pad_add_fusion.ids, f32[2,8,3,2,128,128]{5,4,3,2,1,0:T(8,128)} %other.5), custom_call_target="tpu_custom_call" | custom-call | flops 1 | bytes 1 | tf_op jit(solution)/shard_map/pack_mine/pallas_call | solution.py:126
  21.8 4.4 %pack_partner.1.refs_0_ = bf16[4,10,384,512]{3,2,1,0:T(8,128)(2,1)S(1)} custom-call(s32[4]{0:T(128)S(1)} %pad_add_fusion.ids, f32[2,8,3,2,128,128]{5,4,3,2,1,0:T(8,128)S(1)} %collective-permute-done.source.other, bf16[4,10,384,512]{3,2,1,0:T(8,128)(2,1)S(1)} %pack_mine.1.refs_0_), custom_call_target="tpu_custom_call", output_to_operand_aliasing={{}: (2, {})} | custom-call | flops 1 | bytes 1 | tf_op jit(solution)/shard_map/pack_partner/pallas_call | solution.py:126
  26.2 1.8 collective-permute-done.2.cross
  32.0 6.0 %collective-permute-start.5 = (f32[16,256]{1,0:T(8,128)S(1)}, f32[16,256]{1,0:T(8,128)S(1)}, u32[]{:S(2)}, u32[]{:S(2)}) collective-permute-start(f32[16,256]{1,0:T(8,128)S(1)} %get-tuple-element.83), channel_id=1, source_target_pairs={{0,8},{8,1},{1,9},{9,2},{2,10},{10,3},{3,11},{11,4},{4,12},{12,5},... | collective-permute-start | bytes 49160 | tf_op jit(solution)/shard_map/ppermute | solution.py:507
  38.1 1.9 collective-permute-start.6
  40.0 3.1 %collective-permute-done.6.high = f32[16,256]{1,0:T(8,128)S(1)} collective-permute-done((f32[16,256]{1,0:T(8,128)S(1)}, f32[16,256]{1,0:T(8,128)S(1)}, u32[]{:S(2)}, u32[]{:S(2)}) %collective-permute-start.6) | collective-permute-done | bytes 16416 | tf_op jit(solution)/shard_map/ppermute | solution.py:507
  43.8 1.5 collective-permute-start.7
  45.3 1.6 collective-permute-start.8
  49.2 3.9 %collective-permute-start.10 = (f32[16,256]{1,0:T(8,128)S(1)}, f32[16,256]{1,0:T(8,128)S(1)}, u32[]{:S(2)}, u32[]{:S(2)}) collective-permute-start(f32[16,256]{1,0:T(8,128)S(1)} %get-tuple-element.88), channel_id=1, source_target_pairs={{0,8},{8,1},{1,9},{9,2},{2,10},{10,3},{3,11},{11,4},{4,12},{12,5},... | collective-permute-start | bytes 49160 | tf_op jit(solution)/shard_map/ppermute | solution.py:507
  53.1 1.9 collective-permute-start.11
  55.1 3.1 %collective-permute-done.11.high = f32[16,256]{1,0:T(8,128)S(1)} collective-permute-done((f32[16,256]{1,0:T(8,128)S(1)}, f32[16,256]{1,0:T(8,128)S(1)}, u32[]{:S(2)}, u32[]{:S(2)}) %collective-permute-start.11) | collective-permute-done | bytes 16416 | tf_op jit(solution)/shard_map/ppermute | solution.py:507
  65.0 23.2 %collective-permute-start.20 = (f32[16,512]{1,0:T(8,128)S(1)}, f32[16,512]{1,0:T(8,128)S(1)}, u32[]{:S(2)}, u32[]{:S(2)}) collective-permute-start(f32[16,512]{1,0:T(8,128)S(1)} %get-tuple-element.102), channel_id=1, source_target_pairs={{0,24},{8,17},{1,25},{9,18},{2,26},{10,19},{3,27},{11,20},{4,28},{... | collective-permute-start | bytes 98312 | tf_op jit(solution)/shard_map/ppermute | solution.py:507
  94.7 2.0 cut_late.1
  98.0 4.9 %collective-permute-start.43 = (f32[2,3,2,128,128]{4,3,2,1,0:T(8,128)S(1)}, f32[2,3,2,128,128]{4,3,2,1,0:T(8,128)S(1)}, u32[]{:S(2)}, u32[]{:S(2)}) collective-permute-start(f32[2,3,2,128,128]{4,3,2,1,0:T(8,128)S(1)} %get-tuple-element.128), channel_id=1, source_target_pairs={{1,8},{2,9},{3,10},{4,11},{5,12},{6,13},{7,14},{8,1},{9,2},{10,3},... | collective-permute-start | bytes 2359304 | tf_op jit(solution)/shard_map/ppermute | solution.py:530
  105.0 9.4 %collective-permute-start.31 = (f32[16,512]{1,0:T(8,128)S(1)}, f32[16,512]{1,0:T(8,128)S(1)}, u32[]{:S(2)}, u32[]{:S(2)}) collective-permute-start(f32[16,512]{1,0:T(8,128)S(1)} %get-tuple-element.114), channel_id=1, source_target_pairs={{0,24},{8,17},{1,25},{9,18},{2,26},{10,19},{3,27},{11,20},{4,28},{... | collective-permute-start | bytes 98312 | tf_op jit(solution)/shard_map/ppermute | solution.py:507
  114.4 1.6 collective-permute-start.32
  118.9 3.9 %collective-permute-start.34 = (f32[2,16,512]{2,1,0:T(8,128)S(1)}, f32[2,16,512]{2,1,0:T(8,128)S(1)}, u32[]{:S(2)}, u32[]{:S(2)}) collective-permute-start(f32[2,16,512]{2,1,0:T(8,128)S(1)} %slice.3), channel_id=1, source_target_pairs={{0,8},{8,1},{1,9},{9,2},{2,10},{10,3},{3,11},{11,4},{4,12},{12,5},... | collective-permute-start | bytes 196616 | tf_op jit(solution)/shard_map/ppermute | solution.py:507
  122.8 1.9 collective-permute-start.35
  124.7 12.4 %collective-permute-done.34.left = f32[2,16,512]{2,1,0:T(8,128)S(1)} collective-permute-done((f32[2,16,512]{2,1,0:T(8,128)S(1)}, f32[2,16,512]{2,1,0:T(8,128)S(1)}, u32[]{:S(2)}, u32[]{:S(2)}) %collective-permute-start.34) | collective-permute-done | bytes 65568 | tf_op jit(solution)/shard_map/ppermute | solution.py:507
  141.0 1.3 collective-permute-done.36.low
  142.4 5.2 %collective-permute-done.37.mid = f32[16,512]{1,0:T(8,128)S(1)} collective-permute-done((f32[16,512]{1,0:T(8,128)S(1)}, f32[16,512]{1,0:T(8,128)S(1)}, u32[]{:S(2)}, u32[]{:S(2)}) %collective-permute-start.37) | collective-permute-done | bytes 32800 | tf_op jit(solution)/shard_map/ppermute | solution.py:507
  147.5 3.4 %collective-permute-done.38.high = f32[16,512]{1,0:T(8,128)S(1)} collective-permute-done((f32[16,512]{1,0:T(8,128)S(1)}, f32[16,512]{1,0:T(8,128)S(1)}, u32[]{:S(2)}, u32[]{:S(2)}) %collective-permute-start.38) | collective-permute-done | bytes 32800 | tf_op jit(solution)/shard_map/ppermute | solution.py:507
  153.7 1.7 halo_late.1.packed.refs_0_
  164.1 22.5 %collective-permute-done.47.low = f32[16,512]{1,0:T(8,128)S(1)} collective-permute-done((f32[16,512]{1,0:T(8,128)S(1)}, f32[16,512]{1,0:T(8,128)S(1)}, u32[]{:S(2)}, u32[]{:S(2)}) %collective-permute-start.47) | collective-permute-done | bytes 32800 | tf_op jit(solution)/shard_map/ppermute | solution.py:507
  186.7 3.5 %collective-permute-done.49.high = f32[16,512]{1,0:T(8,128)S(1)} collective-permute-done((f32[16,512]{1,0:T(8,128)S(1)}, f32[16,512]{1,0:T(8,128)S(1)}, u32[]{:S(2)}, u32[]{:S(2)}) %collective-permute-start.49) | collective-permute-done | bytes 32800 | tf_op jit(solution)/shard_map/ppermute | solution.py:507
  199.1 9.1 %collective-permute-done.58.low = f32[16,512]{1,0:T(8,128)S(1)} collective-permute-done((f32[16,512]{1,0:T(8,128)S(1)}, f32[16,512]{1,0:T(8,128)S(1)}, u32[]{:S(2)}, u32[]{:S(2)}) %collective-permute-start.58) | collective-permute-done | bytes 32800 | tf_op jit(solution)/shard_map/ppermute | solution.py:507
  209.1 2.8 %collective-permute-done.60.high = f32[16,512]{1,0:T(8,128)S(1)} collective-permute-done((f32[16,512]{1,0:T(8,128)S(1)}, f32[16,512]{1,0:T(8,128)S(1)}, u32[]{:S(2)}, u32[]{:S(2)}) %collective-permute-start.60) | collective-permute-done | bytes 32800 | tf_op jit(solution)/shard_map/ppermute | solution.py:507
  211.9 2.5 %up_0.1 = (f32[16,512]{1,0:T(8,128)}, f32[4,16,512]{2,1,0:T(8,128)S(1)}) custom-call(f32[16,512]{1,0:T(8,128)S(1)} %collective-permute-done.58.low, f32[16,512]{1,0:T(8,128)S(1)} %collective-permute-done.59.mid, f32[16,512]{1,0:T(8,128)S(1)} %collective-permute-done.60.high, f32[4,20,1536]{2,1,0:T(8,128)S(1)} %window.1, ...), custom_call_target="tpu_custom_call", output_to_operand_aliasing={{1}: (8, {})} | custom-call | flops 1 | bytes 1 | tf_op jit(solution)/shard_map/up_0/pallas_call | solution.py:395
  215.0 1.3 collective-permute-done.61.taken
  (141 shorter events, 60.5 us)
Async XLA Ops:
  2.4 19.3 %collective-permute-start = (f32[2,8,3,2,128,128]{5,4,3,2,1,0:T(8,128)}, f32[2,8,3,2,128,128]{5,4,3,2,1,0:T(8,128)S(1)}, u32[]{:S(2)}, u32[]{:S(2)}) collective-permute-start(f32[2,8,3,2,128,128]{5,4,3,2,1,0:T(8,128)} %other.5), channel_id=1, source_target_pairs={{0,8},{1,9},{2,10},{3,11},{4,12},{5,13},{6,14},{7,15},{8,0},{9,1},... | collective-permute-start | bytes 18874376 | tf_op jit(solution)/shard_map/ppermute | solution.py:538
  3.9 22.2 %collective-permute-start.1 = (f32[1,3,2,128,128]{4,3,2,1,0:T(8,128)S(1)}, f32[1,3,2,128,128]{4,3,2,1,0:T(8,128)S(1)}, u32[]{:S(2)}, u32[]{:S(2)}) collective-permute-start(f32[1,3,2,128,128]{4,3,2,1,0:T(8,128)S(1)} %get-tuple-element.75), channel_id=1, source_target_pairs={{0,1},{1,2},{2,3},{3,4},{4,5},{5,6},{6,7},{9,8},{10,9},{11,10},{12... | collective-permute-start | bytes 1179656 | tf_op jit(solution)/shard_map/ppermute | solution.py:529
  5.2 22.8 %collective-permute-start.2 = (f32[1,3,2,128,128]{4,3,2,1,0:T(8,128)S(1)}, f32[1,3,2,128,128]{4,3,2,1,0:T(8,128)S(1)}, u32[]{:S(2)}, u32[]{:S(2)}) collective-permute-start(f32[1,3,2,128,128]{4,3,2,1,0:T(8,128)S(1)} %get-tuple-element.79), channel_id=1, source_target_pairs={{1,8},{2,9},{3,10},{4,11},{5,12},{6,13},{7,14},{8,1},{9,2},{10,3},... | collective-permute-start | bytes 1179656 | tf_op jit(solution)/shard_map/ppermute | solution.py:530
  14.0 5.3 %collective-permute-start.3 = (f32[2,20,1024]{2,1,0:T(8,128)S(1)}, f32[2,20,1024]{2,1,0:T(8,128)S(1)}, u32[]{:S(2)}, u32[]{:S(2)}) collective-permute-start(f32[2,20,1024]{2,1,0:T(8,128)S(1)} %rows.1), channel_id=1, source_target_pairs={{0,8},{1,9},{2,10},{3,11},{4,12},{5,13},{6,14},{7,15},{8,0},{9,1},... | collective-permute-start | bytes 491528 | tf_op jit(solution)/shard_map/ppermute | solution.py:547
  19.8 8.2 %collective-permute-start.4 = (f32[4,20,512]{2,1,0:T(8,128)S(1)}, f32[4,20,512]{2,1,0:T(8,128)S(1)}, u32[]{:S(2)}, u32[]{:S(2)}) collective-permute-start(f32[4,20,512]{2,1,0:T(8,128)S(1)} %edge.1), channel_id=1, source_target_pairs={{0,1},{1,2},{2,3},{3,4},{4,5},{5,6},{6,7},{9,8},{10,9},{11,10},{12... | collective-permute-start | bytes 491528 | tf_op jit(solution)/shard_map/ppermute | solution.py:553
  28.6 29.6 %collective-permute-start.12 = (f32[4,3,2,128,128]{4,3,2,1,0:T(8,128)S(1)}, f32[4,3,2,128,128]{4,3,2,1,0:T(8,128)S(1)}, u32[]{:S(2)}, u32[]{:S(2)}) collective-permute-start(f32[4,3,2,128,128]{4,3,2,1,0:T(8,128)S(1)} %get-tuple-element.95), channel_id=1, source_target_pairs={{32,33},{33,34},{34,35},{35,36},{36,37},{37,38},{38,39},{48,49},{4... | collective-permute-start | bytes 4718600 | tf_op jit(solution)/shard_map/ppermute | solution.py:529
  29.4 28.8 %collective-permute-start.13 = (f32[4,3,2,128,128]{4,3,2,1,0:T(8,128)S(1)}, f32[4,3,2,128,128]{4,3,2,1,0:T(8,128)S(1)}, u32[]{:S(2)}, u32[]{:S(2)}) collective-permute-start(f32[4,3,2,128,128]{4,3,2,1,0:T(8,128)S(1)} %get-tuple-element.96), channel_id=1, source_target_pairs={{33,40},{34,41},{35,42},{36,43},{37,44},{38,45},{39,46},{49,56},{5... | collective-permute-start | bytes 4718600 | tf_op jit(solution)/shard_map/ppermute | solution.py:530
  32.0 7.9 %collective-permute-start.5 = (f32[16,256]{1,0:T(8,128)S(1)}, f32[16,256]{1,0:T(8,128)S(1)}, u32[]{:S(2)}, u32[]{:S(2)}) collective-permute-start(f32[16,256]{1,0:T(8,128)S(1)} %get-tuple-element.83), channel_id=1, source_target_pairs={{0,8},{8,1},{1,9},{9,2},{2,10},{10,3},{3,11},{11,4},{4,12},{12,5},... | collective-permute-start | bytes 49160 | tf_op jit(solution)/shard_map/ppermute | solution.py:507
  38.1 5.1 %collective-permute-start.6 = (f32[16,256]{1,0:T(8,128)S(1)}, f32[16,256]{1,0:T(8,128)S(1)}, u32[]{:S(2)}, u32[]{:S(2)}) collective-permute-start(f32[16,256]{1,0:T(8,128)S(1)} %get-tuple-element.84.mid), channel_id=1, source_target_pairs={{8,0},{1,8},{9,1},{2,9},{10,2},{3,10},{11,3},{4,11},{12,4},{5,12},... | collective-permute-start | bytes 49160 | tf_op jit(solution)/shard_map/ppermute | solution.py:507
  43.8 4.4 %collective-permute-start.7 = (f32[16,512]{1,0:T(8,128)S(1)}, f32[16,512]{1,0:T(8,128)S(1)}, u32[]{:S(2)}, u32[]{:S(2)}) collective-permute-start(f32[16,512]{1,0:T(8,128)S(1)} %get-tuple-element.86), channel_id=1, source_target_pairs={{0,24},{8,17},{1,25},{9,18},{2,26},{10,19},{3,27},{11,20},{4,28},{... | collective-permute-start | bytes 98312 | tf_op jit(solution)/shard_map/ppermute | solution.py:507
  49.2 5.9 %collective-permute-start.10 = (f32[16,256]{1,0:T(8,128)S(1)}, f32[16,256]{1,0:T(8,128)S(1)}, u32[]{:S(2)}, u32[]{:S(2)}) collective-permute-start(f32[16,256]{1,0:T(8,128)S(1)} %get-tuple-element.88), channel_id=1, source_target_pairs={{0,8},{8,1},{1,9},{9,2},{2,10},{10,3},{3,11},{11,4},{4,12},{12,5},... | collective-permute-start | bytes 49160 | tf_op jit(solution)/shard_map/ppermute | solution.py:507
  53.1 5.1 %collective-permute-start.11 = (f32[16,256]{1,0:T(8,128)S(1)}, f32[16,256]{1,0:T(8,128)S(1)}, u32[]{:S(2)}, u32[]{:S(2)}) collective-permute-start(f32[16,256]{1,0:T(8,128)S(1)} %get-tuple-element.89.mid), channel_id=1, source_target_pairs={{8,0},{1,8},{9,1},{2,9},{10,2},{3,10},{11,3},{4,11},{12,4},{5,12},... | collective-permute-start | bytes 49160 | tf_op jit(solution)/shard_map/ppermute | solution.py:507
  58.8 35.3 %collective-permute-start.26 = (f32[2,3,2,128,128]{4,3,2,1,0:T(8,128)S(1)}, f32[2,3,2,128,128]{4,3,2,1,0:T(8,128)S(1)}, u32[]{:S(2)}, u32[]{:S(2)}) collective-permute-start(f32[2,3,2,128,128]{4,3,2,1,0:T(8,128)S(1)} %get-tuple-element.109), channel_id=1, source_target_pairs={{80,81},{81,82},{82,83},{83,84},{84,85},{85,86},{86,87},{89,88},{9... | collective-permute-start | bytes 2359304 | tf_op jit(solution)/shard_map/ppermute | solution.py:529
  59.5 34.6 %collective-permute-start.27 = (f32[2,3,2,128,128]{4,3,2,1,0:T(8,128)S(1)}, f32[2,3,2,128,128]{4,3,2,1,0:T(8,128)S(1)}, u32[]{:S(2)}, u32[]{:S(2)}) collective-permute-start(f32[2,3,2,128,128]{4,3,2,1,0:T(8,128)S(1)} %get-tuple-element.110), channel_id=1, source_target_pairs={{81,88},{82,89},{83,90},{84,91},{85,92},{86,93},{87,94},{88,81},{8... | collective-permute-start | bytes 2359304 | tf_op jit(solution)/shard_map/ppermute | solution.py:530
  65.0 25.8 %collective-permute-start.20 = (f32[16,512]{1,0:T(8,128)S(1)}, f32[16,512]{1,0:T(8,128)S(1)}, u32[]{:S(2)}, u32[]{:S(2)}) collective-permute-start(f32[16,512]{1,0:T(8,128)S(1)} %get-tuple-element.102), channel_id=1, source_target_pairs={{0,24},{8,17},{1,25},{9,18},{2,26},{10,19},{3,27},{11,20},{4,28},{... | collective-permute-start | bytes 98312 | tf_op jit(solution)/shard_map/ppermute | solution.py:507
  96.7 57.0 %collective-permute-start.42 = (f32[2,3,2,128,128]{4,3,2,1,0:T(8,128)S(1)}, f32[2,3,2,128,128]{4,3,2,1,0:T(8,128)S(1)}, u32[]{:S(2)}, u32[]{:S(2)}) collective-permute-start(f32[2,3,2,128,128]{4,3,2,1,0:T(8,128)S(1)} %get-tuple-element.127), channel_id=1, source_target_pairs={{0,1},{1,2},{2,3},{3,4},{4,5},{5,6},{6,7},{9,8},{10,9},{11,10},{12... | collective-permute-start | bytes 2359304 | tf_op jit(solution)/shard_map/ppermute | solution.py:529
  98.0 55.7 %collective-permute-start.43 = (f32[2,3,2,128,128]{4,3,2,1,0:T(8,128)S(1)}, f32[2,3,2,128,128]{4,3,2,1,0:T(8,128)S(1)}, u32[]{:S(2)}, u32[]{:S(2)}) collective-permute-start(f32[2,3,2,128,128]{4,3,2,1,0:T(8,128)S(1)} %get-tuple-element.128), channel_id=1, source_target_pairs={{1,8},{2,9},{3,10},{4,11},{5,12},{6,13},{7,14},{8,1},{9,2},{10,3},... | collective-permute-start | bytes 2359304 | tf_op jit(solution)/shard_map/ppermute | solution.py:530
  105.0 12.3 %collective-permute-start.31 = (f32[16,512]{1,0:T(8,128)S(1)}, f32[16,512]{1,0:T(8,128)S(1)}, u32[]{:S(2)}, u32[]{:S(2)}) collective-permute-start(f32[16,512]{1,0:T(8,128)S(1)} %get-tuple-element.114), channel_id=1, source_target_pairs={{0,24},{8,17},{1,25},{9,18},{2,26},{10,19},{3,27},{11,20},{4,28},{... | collective-permute-start | bytes 98312 | tf_op jit(solution)/shard_map/ppermute | solution.py:507
  114.4 2.9 %collective-permute-start.32 = (f32[16,512]{1,0:T(8,128)S(1)}, f32[16,512]{1,0:T(8,128)S(1)}, u32[]{:S(2)}, u32[]{:S(2)}) collective-permute-start(f32[16,512]{1,0:T(8,128)S(1)} %get-tuple-element.114), channel_id=1, source_target_pairs={{0,16},{8,24},{1,17},{9,25},{2,18},{10,26},{3,19},{11,27},{4,20},{... | collective-permute-start | bytes 98312 | tf_op jit(solution)/shard_map/ppermute | solution.py:507
  118.9 18.2 %collective-permute-start.34 = (f32[2,16,512]{2,1,0:T(8,128)S(1)}, f32[2,16,512]{2,1,0:T(8,128)S(1)}, u32[]{:S(2)}, u32[]{:S(2)}) collective-permute-start(f32[2,16,512]{2,1,0:T(8,128)S(1)} %slice.3), channel_id=1, source_target_pairs={{0,8},{8,1},{1,9},{9,2},{2,10},{10,3},{3,11},{11,4},{4,12},{12,5},... | collective-permute-start | bytes 196616 | tf_op jit(solution)/shard_map/ppermute | solution.py:507
  122.8 14.3 %collective-permute-start.35 = (f32[2,16,512]{2,1,0:T(8,128)S(1)}, f32[2,16,512]{2,1,0:T(8,128)S(1)}, u32[]{:S(2)}, u32[]{:S(2)}) collective-permute-start(f32[2,16,512]{2,1,0:T(8,128)S(1)} %slice.3), channel_id=1, source_target_pairs={{8,0},{1,8},{9,1},{2,9},{10,2},{3,10},{11,3},{4,11},{12,4},{5,12},... | collective-permute-start | bytes 196616 | tf_op jit(solution)/shard_map/ppermute | solution.py:507
  137.1 5.2 %collective-permute-start.36 = (f32[16,512]{1,0:T(8,128)S(1)}, f32[16,512]{1,0:T(8,128)S(1)}, u32[]{:S(2)}, u32[]{:S(2)}) collective-permute-start(f32[16,512]{1,0:T(8,128)S(1)} %get-tuple-element.117), channel_id=1, source_target_pairs={{16,8},{24,1},{17,9},{25,2},{18,10},{26,3},{19,11},{27,4},{20,12},... | collective-permute-start | bytes 98312 | tf_op jit(solution)/shard_map/ppermute | solution.py:507
  138.4 9.1 %collective-permute-start.37 = (f32[16,512]{1,0:T(8,128)S(1)}, f32[16,512]{1,0:T(8,128)S(1)}, u32[]{:S(2)}, u32[]{:S(2)}) collective-permute-start(f32[16,512]{1,0:T(8,128)S(1)} %get-tuple-element.117), channel_id=1, source_target_pairs={{16,0},{24,8},{17,1},{25,9},{18,2},{26,10},{19,3},{27,11},{20,4},{... | collective-permute-start | bytes 98312 | tf_op jit(solution)/shard_map/ppermute | solution.py:507
  139.7 11.2 %collective-permute-start.38 = (f32[16,512]{1,0:T(8,128)S(1)}, f32[16,512]{1,0:T(8,128)S(1)}, u32[]{:S(2)}, u32[]{:S(2)}) collective-permute-start(f32[16,512]{1,0:T(8,128)S(1)} %get-tuple-element.117), channel_id=1, source_target_pairs={{24,0},{17,8},{25,1},{18,9},{26,2},{19,10},{27,3},{20,11},{28,4},{... | collective-permute-start | bytes 98312 | tf_op jit(solution)/shard_map/ppermute | solution.py:507
  158.2 34.0 %collective-permute-start.53 = (f32[1,3,2,128,128]{4,3,2,1,0:T(8,128)S(1)}, f32[1,3,2,128,128]{4,3,2,1,0:T(8,128)S(1)}, u32[]{:S(2)}, u32[]{:S(2)}) collective-permute-start(f32[1,3,2,128,128]{4,3,2,1,0:T(8,128)S(1)} %get-tuple-element.139), channel_id=1, source_target_pairs={{0,1},{1,2},{2,3},{3,4},{4,5},{5,6},{6,7},{16,17},{17,18},{18,19},... | collective-permute-start | bytes 1179656 | tf_op jit(solution)/shard_map/ppermute | solution.py:529
  158.9 33.3 %collective-permute-start.54 = (f32[1,3,2,128,128]{4,3,2,1,0:T(8,128)S(1)}, f32[1,3,2,128,128]{4,3,2,1,0:T(8,128)S(1)}, u32[]{:S(2)}, u32[]{:S(2)}) collective-permute-start(f32[1,3,2,128,128]{4,3,2,1,0:T(8,128)S(1)} %get-tuple-element.140), channel_id=1, source_target_pairs={{1,8},{2,9},{3,10},{4,11},{5,12},{6,13},{7,14},{17,24},{18,25},{19... | collective-permute-start | bytes 1179656 | tf_op jit(solution)/shard_map/ppermute | solution.py:530
  160.2 26.4 %collective-permute-start.47 = (f32[16,512]{1,0:T(8,128)S(1)}, f32[16,512]{1,0:T(8,128)S(1)}, u32[]{:S(2)}, u32[]{:S(2)}) collective-permute-start(f32[16,512]{1,0:T(8,128)S(1)} %get-tuple-element.132), channel_id=1, source_target_pairs={{16,8},{24,1},{17,9},{25,2},{18,10},{26,3},{19,11},{27,4},{20,12},... | collective-permute-start | bytes 98312 | tf_op jit(solution)/shard_map/ppermute | solution.py:507
  161.5 25.1 %collective-permute-start.48 = (f32[16,512]{1,0:T(8,128)S(1)}, f32[16,512]{1,0:T(8,128)S(1)}, u32[]{:S(2)}, u32[]{:S(2)}) collective-permute-start(f32[16,512]{1,0:T(8,128)S(1)} %get-tuple-element.132), channel_id=1, source_target_pairs={{16,0},{24,8},{17,1},{25,9},{18,2},{26,10},{19,3},{27,11},{20,4},{... | collective-permute-start | bytes 98312 | tf_op jit(solution)/shard_map/ppermute | solution.py:507
  162.8 27.3 %collective-permute-start.49 = (f32[16,512]{1,0:T(8,128)S(1)}, f32[16,512]{1,0:T(8,128)S(1)}, u32[]{:S(2)}, u32[]{:S(2)}) collective-permute-start(f32[16,512]{1,0:T(8,128)S(1)} %get-tuple-element.132), channel_id=1, source_target_pairs={{24,0},{17,8},{25,1},{18,9},{26,2},{19,10},{27,3},{20,11},{28,4},{... | collective-permute-start | bytes 98312 | tf_op jit(solution)/shard_map/ppermute | solution.py:507
  195.2 13.0 %collective-permute-start.58 = (f32[16,512]{1,0:T(8,128)S(1)}, f32[16,512]{1,0:T(8,128)S(1)}, u32[]{:S(2)}, u32[]{:S(2)}) collective-permute-start(f32[16,512]{1,0:T(8,128)S(1)} %get-tuple-element.144), channel_id=1, source_target_pairs={{16,8},{24,1},{17,9},{25,2},{18,10},{26,3},{19,11},{27,4},{20,12},... | collective-permute-start | bytes 98312 | tf_op jit(solution)/shard_map/ppermute | solution.py:507
  196.5 12.6 %collective-permute-start.59 = (f32[16,512]{1,0:T(8,128)S(1)}, f32[16,512]{1,0:T(8,128)S(1)}, u32[]{:S(2)}, u32[]{:S(2)}) collective-permute-start(f32[16,512]{1,0:T(8,128)S(1)} %get-tuple-element.144), channel_id=1, source_target_pairs={{16,0},{24,8},{17,1},{25,9},{18,2},{26,10},{19,3},{27,11},{20,4},{... | collective-permute-start | bytes 98312 | tf_op jit(solution)/shard_map/ppermute | solution.py:507
  197.8 14.1 %collective-permute-start.60 = (f32[16,512]{1,0:T(8,128)S(1)}, f32[16,512]{1,0:T(8,128)S(1)}, u32[]{:S(2)}, u32[]{:S(2)}) collective-permute-start(f32[16,512]{1,0:T(8,128)S(1)} %get-tuple-element.144), channel_id=1, source_target_pairs={{24,0},{17,8},{25,1},{18,9},{26,2},{19,10},{27,3},{20,11},{28,4},{... | collective-permute-start | bytes 98312 | tf_op jit(solution)/shard_map/ppermute | solution.py:507
  (34 other events, 49.3 us)

commit v6 on v5

--- a/solution.py
+++ b/solution.py
@@ -25,6 +25,14 @@
 AXES = ("depth", "lat")
 
 
+def chip_row():
+    return lax.axis_index("depth") // 2
+
+
+def chip_core():
+    return lax.rem(lax.axis_index("depth"), 2)
+
+
 def split_store(buffer, slot_ref):
     for offset in range(3):
         for part in range(2):
@@ -63,7 +71,7 @@
 
 def chip_body(ids, source, *refs, mine):
     packed, buffers, sems = refs[-3:]
-    core = ids[1]
+    core = chip_core()
     first = 2 * core if mine else 2 * (1 - core)
     count = OWN + HALO
 
@@ -86,7 +94,7 @@
 
 def halo_body(ids, straight, cross, *refs, rows, slots, split):
     packed, buffers, sems = refs[-3:]
-    row, core = ids[0], ids[1]
+    row, core = chip_row(), chip_core()
     units = len(slots[0])
     first = units // 2
 
@@ -125,7 +133,7 @@
     extra = () if packed is None else (packed,)
     return pl.pallas_call(
         functools.partial(chip_body, mine=mine),
-        in_specs=[SMEM_SPEC, ANY_SPEC] + [VMEM_SPEC] * len(extra),
+        in_specs=[ANY_SPEC, ANY_SPEC] + [VMEM_SPEC] * len(extra),
         out_specs=VMEM_SPEC,
         out_shape=jax.ShapeDtypeStruct(PACKED, jnp.bfloat16),
         scratch_shapes=PACK_SCRATCH,
@@ -139,7 +147,7 @@
 def pack_halo(ids, sources, packed, rows, slots, name, split=True):
     return pl.pallas_call(
         functools.partial(halo_body, rows=rows, slots=slots, split=split),
-        in_specs=[SMEM_SPEC, ANY_SPEC, ANY_SPEC, VMEM_SPEC],
+        in_specs=[ANY_SPEC, ANY_SPEC, ANY_SPEC, VMEM_SPEC],
         out_specs=VMEM_SPEC,
         out_shape=jax.ShapeDtypeStruct(PACKED, jnp.bfloat16),
         scratch_shapes=PACK_SCRATCH,
@@ -151,11 +159,11 @@
 
 
 def cut_body(ids, mine, other, straight, cross, sems, *, parts):
-    row = ids[0]
+    row = chip_row()
     for begin_row, end_row, runs in parts:
         for side in range(2):
 
-            @pl.when((row >= begin_row) & (row < end_row) & (ids[1] == side))
+            @pl.when((row >= begin_row) & (row < end_row) & (chip_core() == side))
             def _():
                 copies = []
                 for out, entries in zip((straight, cross), runs[side]):
@@ -179,7 +187,7 @@
     count = sum(end - begin for _, begin, end in parts[0][2][0][0])
     return pl.pallas_call(
         functools.partial(cut_body, parts=parts),
-        in_specs=[SMEM_SPEC, ANY_SPEC, ANY_SPEC],
+        in_specs=[ANY_SPEC, ANY_SPEC, ANY_SPEC],
         out_specs=[ANY_SPEC] * 2,
         out_shape=[pltpu.VMEM((count, 3, 2, TILE, TILE), jnp.float32)] * 2,
         scratch_shapes=[pltpu.SemaphoreType.DMA((6,))],
@@ -195,7 +203,7 @@
 def rows_body(ids, cells, layers, rhs, couple, rows):
     strip = rhs.shape[-1]
     shot = lax.broadcasted_iota(jnp.int32, (8, strip), 0)
-    position = lax.broadcasted_iota(jnp.int32, (8, strip), 1) + ids[2] * strip
+    position = lax.broadcasted_iota(jnp.int32, (8, strip), 1) + lax.axis_index("lat") * strip
     target = jnp.full((8, strip), -1, jnp.int32)
     depth = jnp.full((8, strip), -1, jnp.int32)
     for index in range(8):
@@ -203,7 +211,7 @@
         depth = jnp.where(shot == index, layers[index], depth)
     here = target == position
     for layer in range(2):
-        hit = here & (depth == ids[3] * 2 + layer)
+        hit = here & (depth == lax.axis_index("depth") * 2 + layer)
         rows[layer, 0:8] = rhs[0, layer] + jnp.where(hit, 4.0, 0.0)
         rows[layer, 8:16] = rhs[1, layer]
         for way in range(2):
@@ -215,7 +223,7 @@
 def edge_body(ids, rows, other, edge):
     for side in range(2):
 
-        @pl.when(ids[1] == side)
+        @pl.when(chip_core() == side)
         def _():
             mine, partner = slice(2 * side, 2 * side + 2), slice(2 - 2 * side, 4 - 2 * side)
             where = slice(HALF, 2 * HALF) if side == 0 else slice(0, HALF)
@@ -226,7 +234,7 @@
 def window_body(ids, rows, other, beside, window):
     for side in range(2):
 
-        @pl.when(ids[1] == side)
+        @pl.when(chip_core() == side)
         def _():
             mine, partner = slice(2 * side, 2 * side + 2), slice(2 - 2 * side, 4 - 2 * side)
             chip = slice(HALF, WINDOW) if side == 0 else slice(0, 2 * HALF)
@@ -239,7 +247,7 @@
 def small_call(body, smem, arrays, shape, name):
     return pl.pallas_call(
         body,
-        in_specs=[SMEM_SPEC] * len(smem) + [VMEM_SPEC] * len(arrays),
+        in_specs=[ANY_SPEC] + [SMEM_SPEC] * (len(smem) - 1) + [VMEM_SPEC] * len(arrays),
         out_specs=VMEM_SPEC,
         out_shape=jax.ShapeDtypeStruct(shape, jnp.float32),
         compiler_params=PARAMS,
@@ -301,7 +309,7 @@
 
 
 def my_turn(turn):
-    return lax.axis_index("depth") // 2 == turn
+    return chip_row() == turn
 
 
 def down_body(low, mid, high, window, packed, _, out, waves, parts, *, turn):
@@ -412,7 +420,7 @@
     own = slice(HALO * TILE, (HALO + OWN) * TILE)
     for side in range(2):
 
-        @pl.when(ids[1] == side)
+        @pl.when(chip_core() == side)
         def _():
             partner = slice(2 - 2 * side, 4 - 2 * side)
             give[0] = waves[partner, :, own]
@@ -422,7 +430,7 @@
 def join_body(ids, waves, field, taken, out_waves, out_field):
     for side in range(2):
 
-        @pl.when(ids[1] == side)
+        @pl.when(chip_core() == side)
         def _():
             mine = slice(HALF * side, HALF * (side + 1))
             partner = slice(HALF * (1 - side), HALF * (2 - side))
@@ -439,7 +447,7 @@
 def join(ids, waves, field, taken, shape):
     return pl.pallas_call(
         join_body,
-        in_specs=[SMEM_SPEC] + [VMEM_SPEC] * 3,
+        in_specs=[ANY_SPEC] + [VMEM_SPEC] * 3,
         out_specs=(VMEM_SPEC,) * 2,
         out_shape=(jax.ShapeDtypeStruct(shape, jnp.float32),) * 2,
         compiler_params=PARAMS,

time: 219 us -> 213 us (0.973)
  Pallas kernels: 29.2 us -> 20.1 us
  waiting for transfers between devices: 73.5 us -> 76.8 us
    pallas_call x12, Pallas kernels: 18.7 us -> 12.7 us  [the longest x2 8.52 us: pack_chip(): pl.pallas_call(functools.partial(chip_body, mine=mine), in_specs=[ANY_SPE...]
    pallas_call x6, Pallas kernels: 5.36 us -> 2.18 us  [pack_halo(): pl.pallas_call(functools.partial(halo_body, rows=rows, slots=slots, split...]
    ppermute x5, waiting for transfers between devices: 1.81 us -> 4.02 us  [send_halo(): lax.ppermute(cross, AXES, beside_pairs(rows, False, sides))]
  transfers between devices with their start and end apart: 62 -> 62, of which waited for: 16 -> 16; matrix products, arithmetic and copies ran while one was open for 0% -> 0% of each run, Pallas kernels for 7% -> 6%
where the time goes in v6:
time: 213 us; the launch traced here: 212 us
  starting transfers between devices  110 us (52%)
  waiting for transfers between devices  76.8 us (36%)
  Pallas kernels  20.1 us (9%)
  local copies, waits for them, and re-layouts  3.01 us (1%)
    ppermute x48, starting transfers between devices, hop(): return lax.ppermute(value, AXES, pairs)  89.7 us
    ppermute x48, waiting for transfers between devices, hop(): return lax.ppermute(value, AXES, pairs)  71.4 us
    ppermute x5, starting transfers between devices, send_halo(): lax.ppermute(cross, AXES, beside_pairs(rows, False, sides))  12.6 us
    pallas_call x2, Pallas kernels, pack_chip(): pl.pallas_call(functools.partial(chip_body, mine=mine), in_specs=[ANY_SPE...  8.52 us
    ppermute x5, starting transfers between devices, send_halo(): lax.ppermute(straight, AXES, beside_pairs(rows, True, sides))  4.73 us
  transfers between devices with their start and end apart: 62, of which 16 were waited for; matrix products, arithmetic and copies ran while one was open for 0% of the time, Pallas kernels for 6%

profile of v6, /device:TPU:1, one launch (start us, length us, event | category | flops | bytes accessed | tf_op | source)
XLA Modules:
  0.0 211.7 jit_solution(18039744357520831658)
XLA Ops:
  1.9 1.5 collective-permute-start
  4.7 5.2 %collective-permute-start.2 = (f32[1,3,2,128,128]{4,3,2,1,0:T(8,128)S(1)}, f32[1,3,2,128,128]{4,3,2,1,0:T(8,128)S(1)}, u32[]{:S(2)}, u32[]{:S(2)}) collective-permute-start(f32[1,3,2,128,128]{4,3,2,1,0:T(8,128)S(1)} %get-tuple-element.79), channel_id=1, source_target_pairs={{1,8},{2,9},{3,10},{4,11},{5,12},{6,13},{7,14},{8,1},{9,2},{10,3},... | collective-permute-start | bytes 1179656 | tf_op jit(solution)/shard_map/ppermute | solution.py:538
  13.5 4.6 %pack_mine.1.refs_0_ = bf16[4,10,384,512]{3,2,1,0:T(8,128)(2,1)S(1)} custom-call(s32[4]{0:T(128)S(1)} %pad_add_fusion.ids, f32[2,8,3,2,128,128]{5,4,3,2,1,0:T(8,128)} %other.5), custom_call_target="tpu_custom_call" | custom-call | flops 1 | bytes 1 | tf_op jit(solution)/shard_map/pack_mine/pallas_call | solution.py:134
  18.2 1.3 collective-permute-start.4
  19.6 3.9 %pack_partner.1.refs_0_ = bf16[4,10,384,512]{3,2,1,0:T(8,128)(2,1)S(1)} custom-call(s32[4]{0:T(128)S(1)} %pad_add_fusion.ids, f32[2,8,3,2,128,128]{5,4,3,2,1,0:T(8,128)S(1)} %collective-permute-done.source.other, bf16[4,10,384,512]{3,2,1,0:T(8,128)(2,1)S(1)} %pack_mine.1.refs_0_), custom_call_target="tpu_custom_call", output_to_operand_aliasing={{}: (2, {})} | custom-call | flops 1 | bytes 1 | tf_op jit(solution)/shard_map/pack_partner/pallas_call | solution.py:134
  23.5 4.0 %collective-permute-done.2.cross = f32[1,3,2,128,128]{4,3,2,1,0:T(8,128)S(1)} collective-permute-done((f32[1,3,2,128,128]{4,3,2,1,0:T(8,128)S(1)}, f32[1,3,2,128,128]{4,3,2,1,0:T(8,128)S(1)}, u32[]{:S(2)}, u32[]{:S(2)}) %collective-permute-start.2) | collective-permute-done | bytes 393248 | tf_op jit(solution)/shard_map/ppermute | solution.py:538
  30.5 5.9 %collective-permute-start.5 = (f32[16,256]{1,0:T(8,128)S(1)}, f32[16,256]{1,0:T(8,128)S(1)}, u32[]{:S(2)}, u32[]{:S(2)}) collective-permute-start(f32[16,256]{1,0:T(8,128)S(1)} %get-tuple-element.83), channel_id=1, source_target_pairs={{0,8},{8,1},{1,9},{9,2},{2,10},{10,3},{3,11},{11,4},{4,12},{12,5},... | collective-permute-start | bytes 49160 | tf_op jit(solution)/shard_map/ppermute | solution.py:515
  36.4 1.9 collective-permute-start.6
  38.4 3.1 %collective-permute-done.6.high = f32[16,256]{1,0:T(8,128)S(1)} collective-permute-done((f32[16,256]{1,0:T(8,128)S(1)}, f32[16,256]{1,0:T(8,128)S(1)}, u32[]{:S(2)}, u32[]{:S(2)}) %collective-permute-start.6) | collective-permute-done | bytes 16416 | tf_op jit(solution)/shard_map/ppermute | solution.py:515
  42.2 1.5 collective-permute-start.7
  43.7 1.6 collective-permute-start.8
  47.6 3.9 %collective-permute-start.10 = (f32[16,256]{1,0:T(8,128)S(1)}, f32[16,256]{1,0:T(8,128)S(1)}, u32[]{:S(2)}, u32[]{:S(2)}) collective-permute-start(f32[16,256]{1,0:T(8,128)S(1)} %get-tuple-element.88), channel_id=1, source_target_pairs={{0,8},{8,1},{1,9},{9,2},{2,10},{10,3},{3,11},{11,4},{4,12},{12,5},... | collective-permute-start | bytes 49160 | tf_op jit(solution)/shard_map/ppermute | solution.py:515
  51.5 1.9 collective-permute-start.11
  53.5 3.1 %collective-permute-done.11.high = f32[16,256]{1,0:T(8,128)S(1)} collective-permute-done((f32[16,256]{1,0:T(8,128)S(1)}, f32[16,256]{1,0:T(8,128)S(1)}, u32[]{:S(2)}, u32[]{:S(2)}) %collective-permute-start.11) | collective-permute-done | bytes 16416 | tf_op jit(solution)/shard_map/ppermute | solution.py:515
  62.3 23.7 %collective-permute-start.20 = (f32[16,512]{1,0:T(8,128)S(1)}, f32[16,512]{1,0:T(8,128)S(1)}, u32[]{:S(2)}, u32[]{:S(2)}) collective-permute-start(f32[16,512]{1,0:T(8,128)S(1)} %get-tuple-element.102), channel_id=1, source_target_pairs={{0,24},{8,17},{1,25},{9,18},{2,26},{10,19},{3,27},{11,20},{4,28},{... | collective-permute-start | bytes 98312 | tf_op jit(solution)/shard_map/ppermute | solution.py:515
  92.0 1.4 cut_late.1
  94.8 4.7 %collective-permute-start.43 = (f32[2,3,2,128,128]{4,3,2,1,0:T(8,128)S(1)}, f32[2,3,2,128,128]{4,3,2,1,0:T(8,128)S(1)}, u32[]{:S(2)}, u32[]{:S(2)}) collective-permute-start(f32[2,3,2,128,128]{4,3,2,1,0:T(8,128)S(1)} %get-tuple-element.128), channel_id=1, source_target_pairs={{1,8},{2,9},{3,10},{4,11},{5,12},{6,13},{7,14},{8,1},{9,2},{10,3},... | collective-permute-start | bytes 2359304 | tf_op jit(solution)/shard_map/ppermute | solution.py:538
  101.5 9.2 %collective-permute-start.31 = (f32[16,512]{1,0:T(8,128)S(1)}, f32[16,512]{1,0:T(8,128)S(1)}, u32[]{:S(2)}, u32[]{:S(2)}) collective-permute-start(f32[16,512]{1,0:T(8,128)S(1)} %get-tuple-element.114), channel_id=1, source_target_pairs={{0,24},{8,17},{1,25},{9,18},{2,26},{10,19},{3,27},{11,20},{4,28},{... | collective-permute-start | bytes 98312 | tf_op jit(solution)/shard_map/ppermute | solution.py:515
  110.7 1.6 collective-permute-start.32
  115.2 3.9 %collective-permute-start.34 = (f32[2,16,512]{2,1,0:T(8,128)S(1)}, f32[2,16,512]{2,1,0:T(8,128)S(1)}, u32[]{:S(2)}, u32[]{:S(2)}) collective-permute-start(f32[2,16,512]{2,1,0:T(8,128)S(1)} %slice.3), channel_id=1, source_target_pairs={{0,8},{8,1},{1,9},{9,2},{2,10},{10,3},{3,11},{11,4},{4,12},{12,5},... | collective-permute-start | bytes 196616 | tf_op jit(solution)/shard_map/ppermute | solution.py:515
  119.1 1.9 collective-permute-start.35
  121.0 13.2 %collective-permute-done.34.left = f32[2,16,512]{2,1,0:T(8,128)S(1)} collective-permute-done((f32[2,16,512]{2,1,0:T(8,128)S(1)}, f32[2,16,512]{2,1,0:T(8,128)S(1)}, u32[]{:S(2)}, u32[]{:S(2)}) %collective-permute-start.34) | collective-permute-done | bytes 65568 | tf_op jit(solution)/shard_map/ppermute | solution.py:515
  138.2 1.3 collective-permute-done.36.low
  139.5 4.0 %collective-permute-done.37.mid = f32[16,512]{1,0:T(8,128)S(1)} collective-permute-done((f32[16,512]{1,0:T(8,128)S(1)}, f32[16,512]{1,0:T(8,128)S(1)}, u32[]{:S(2)}, u32[]{:S(2)}) %collective-permute-start.37) | collective-permute-done | bytes 32800 | tf_op jit(solution)/shard_map/ppermute | solution.py:515
  143.6 3.8 %collective-permute-done.38.high = f32[16,512]{1,0:T(8,128)S(1)} collective-permute-done((f32[16,512]{1,0:T(8,128)S(1)}, f32[16,512]{1,0:T(8,128)S(1)}, u32[]{:S(2)}, u32[]{:S(2)}) %collective-permute-start.38) | collective-permute-done | bytes 32800 | tf_op jit(solution)/shard_map/ppermute | solution.py:515
  158.9 22.0 %collective-permute-done.47.low = f32[16,512]{1,0:T(8,128)S(1)} collective-permute-done((f32[16,512]{1,0:T(8,128)S(1)}, f32[16,512]{1,0:T(8,128)S(1)}, u32[]{:S(2)}, u32[]{:S(2)}) %collective-permute-start.47) | collective-permute-done | bytes 32800 | tf_op jit(solution)/shard_map/ppermute | solution.py:515
  180.9 3.7 %collective-permute-done.49.high = f32[16,512]{1,0:T(8,128)S(1)} collective-permute-done((f32[16,512]{1,0:T(8,128)S(1)}, f32[16,512]{1,0:T(8,128)S(1)}, u32[]{:S(2)}, u32[]{:S(2)}) %collective-permute-start.49) | collective-permute-done | bytes 32800 | tf_op jit(solution)/shard_map/ppermute | solution.py:515
  193.0 9.4 %collective-permute-done.58.low = f32[16,512]{1,0:T(8,128)S(1)} collective-permute-done((f32[16,512]{1,0:T(8,128)S(1)}, f32[16,512]{1,0:T(8,128)S(1)}, u32[]{:S(2)}, u32[]{:S(2)}) %collective-permute-start.58) | collective-permute-done | bytes 32800 | tf_op jit(solution)/shard_map/ppermute | solution.py:515
  202.4 1.7 collective-permute-done.59.mid
  204.1 3.0 %collective-permute-done.60.high = f32[16,512]{1,0:T(8,128)S(1)} collective-permute-done((f32[16,512]{1,0:T(8,128)S(1)}, f32[16,512]{1,0:T(8,128)S(1)}, u32[]{:S(2)}, u32[]{:S(2)}) %collective-permute-start.60) | collective-permute-done | bytes 32800 | tf_op jit(solution)/shard_map/ppermute | solution.py:515
  207.1 2.5 %up_0.1 = (f32[16,512]{1,0:T(8,128)}, f32[4,16,512]{2,1,0:T(8,128)S(1)}) custom-call(f32[16,512]{1,0:T(8,128)S(1)} %collective-permute-done.58.low, f32[16,512]{1,0:T(8,128)S(1)} %collective-permute-done.59.mid, f32[16,512]{1,0:T(8,128)S(1)} %collective-permute-done.60.high, f32[4,20,1536]{2,1,0:T(8,128)S(1)} %window.1, ...), custom_call_target="tpu_custom_call", output_to_operand_aliasing={{1}: (8, {})} | custom-call | flops 1 | bytes 1 | tf_op jit(solution)/shard_map/up_0/pallas_call | solution.py:403
  209.7 1.3 collective-permute-done.61.taken
  (141 shorter events, 54.1 us)
Async XLA Ops:
  1.9 17.7 %collective-permute-start = (f32[2,8,3,2,128,128]{5,4,3,2,1,0:T(8,128)}, f32[2,8,3,2,128,128]{5,4,3,2,1,0:T(8,128)S(1)}, u32[]{:S(2)}, u32[]{:S(2)}) collective-permute-start(f32[2,8,3,2,128,128]{5,4,3,2,1,0:T(8,128)} %other.5), channel_id=1, source_target_pairs={{0,8},{1,9},{2,10},{3,11},{4,12},{5,13},{6,14},{7,15},{8,0},{9,1},... | collective-permute-start | bytes 18874376 | tf_op jit(solution)/shard_map/ppermute | solution.py:546
  3.4 20.1 %collective-permute-start.1 = (f32[1,3,2,128,128]{4,3,2,1,0:T(8,128)S(1)}, f32[1,3,2,128,128]{4,3,2,1,0:T(8,128)S(1)}, u32[]{:S(2)}, u32[]{:S(2)}) collective-permute-start(f32[1,3,2,128,128]{4,3,2,1,0:T(8,128)S(1)} %get-tuple-element.75), channel_id=1, source_target_pairs={{0,1},{1,2},{2,3},{3,4},{4,5},{5,6},{6,7},{9,8},{10,9},{11,10},{12... | collective-permute-start | bytes 1179656 | tf_op jit(solution)/shard_map/ppermute | solution.py:537
  4.7 22.8 %collective-permute-start.2 = (f32[1,3,2,128,128]{4,3,2,1,0:T(8,128)S(1)}, f32[1,3,2,128,128]{4,3,2,1,0:T(8,128)S(1)}, u32[]{:S(2)}, u32[]{:S(2)}) collective-permute-start(f32[1,3,2,128,128]{4,3,2,1,0:T(8,128)S(1)} %get-tuple-element.79), channel_id=1, source_target_pairs={{1,8},{2,9},{3,10},{4,11},{5,12},{6,13},{7,14},{8,1},{9,2},{10,3},... | collective-permute-start | bytes 1179656 | tf_op jit(solution)/shard_map/ppermute | solution.py:538
  13.4 4.7 %collective-permute-start.3 = (f32[2,20,1024]{2,1,0:T(8,128)S(1)}, f32[2,20,1024]{2,1,0:T(8,128)S(1)}, u32[]{:S(2)}, u32[]{:S(2)}) collective-permute-start(f32[2,20,1024]{2,1,0:T(8,128)S(1)} %rows.1), channel_id=1, source_target_pairs={{0,8},{1,9},{2,10},{3,11},{4,12},{5,13},{6,14},{7,15},{8,0},{9,1},... | collective-permute-start | bytes 491528 | tf_op jit(solution)/shard_map/ppermute | solution.py:555
  18.2 9.3 %collective-permute-start.4 = (f32[4,20,512]{2,1,0:T(8,128)S(1)}, f32[4,20,512]{2,1,0:T(8,128)S(1)}, u32[]{:S(2)}, u32[]{:S(2)}) collective-permute-start(f32[4,20,512]{2,1,0:T(8,128)S(1)} %edge.1), channel_id=1, source_target_pairs={{0,1},{1,2},{2,3},{3,4},{4,5},{5,6},{6,7},{9,8},{10,9},{11,10},{12... | collective-permute-start | bytes 491528 | tf_op jit(solution)/shard_map/ppermute | solution.py:561
  27.6 29.0 %collective-permute-start.12 = (f32[4,3,2,128,128]{4,3,2,1,0:T(8,128)S(1)}, f32[4,3,2,128,128]{4,3,2,1,0:T(8,128)S(1)}, u32[]{:S(2)}, u32[]{:S(2)}) collective-permute-start(f32[4,3,2,128,128]{4,3,2,1,0:T(8,128)S(1)} %get-tuple-element.95), channel_id=1, source_target_pairs={{32,33},{33,34},{34,35},{35,36},{36,37},{37,38},{38,39},{48,49},{4... | collective-permute-start | bytes 4718600 | tf_op jit(solution)/shard_map/ppermute | solution.py:537
  28.4 28.2 %collective-permute-start.13 = (f32[4,3,2,128,128]{4,3,2,1,0:T(8,128)S(1)}, f32[4,3,2,128,128]{4,3,2,1,0:T(8,128)S(1)}, u32[]{:S(2)}, u32[]{:S(2)}) collective-permute-start(f32[4,3,2,128,128]{4,3,2,1,0:T(8,128)S(1)} %get-tuple-element.96), channel_id=1, source_target_pairs={{33,40},{34,41},{35,42},{36,43},{37,44},{38,45},{39,46},{49,56},{5... | collective-permute-start | bytes 4718600 | tf_op jit(solution)/shard_map/ppermute | solution.py:538
  30.5 7.9 %collective-permute-start.5 = (f32[16,256]{1,0:T(8,128)S(1)}, f32[16,256]{1,0:T(8,128)S(1)}, u32[]{:S(2)}, u32[]{:S(2)}) collective-permute-start(f32[16,256]{1,0:T(8,128)S(1)} %get-tuple-element.83), channel_id=1, source_target_pairs={{0,8},{8,1},{1,9},{9,2},{2,10},{10,3},{3,11},{11,4},{4,12},{12,5},... | collective-permute-start | bytes 49160 | tf_op jit(solution)/shard_map/ppermute | solution.py:515
  36.4 5.1 %collective-permute-start.6 = (f32[16,256]{1,0:T(8,128)S(1)}, f32[16,256]{1,0:T(8,128)S(1)}, u32[]{:S(2)}, u32[]{:S(2)}) collective-permute-start(f32[16,256]{1,0:T(8,128)S(1)} %get-tuple-element.84.mid), channel_id=1, source_target_pairs={{8,0},{1,8},{9,1},{2,9},{10,2},{3,10},{11,3},{4,11},{12,4},{5,12},... | collective-permute-start | bytes 49160 | tf_op jit(solution)/shard_map/ppermute | solution.py:515
  42.2 4.4 %collective-permute-start.7 = (f32[16,512]{1,0:T(8,128)S(1)}, f32[16,512]{1,0:T(8,128)S(1)}, u32[]{:S(2)}, u32[]{:S(2)}) collective-permute-start(f32[16,512]{1,0:T(8,128)S(1)} %get-tuple-element.86), channel_id=1, source_target_pairs={{0,24},{8,17},{1,25},{9,18},{2,26},{10,19},{3,27},{11,20},{4,28},{... | collective-permute-start | bytes 98312 | tf_op jit(solution)/shard_map/ppermute | solution.py:515
  47.6 5.9 %collective-permute-start.10 = (f32[16,256]{1,0:T(8,128)S(1)}, f32[16,256]{1,0:T(8,128)S(1)}, u32[]{:S(2)}, u32[]{:S(2)}) collective-permute-start(f32[16,256]{1,0:T(8,128)S(1)} %get-tuple-element.88), channel_id=1, source_target_pairs={{0,8},{8,1},{1,9},{9,2},{2,10},{10,3},{3,11},{11,4},{4,12},{12,5},... | collective-permute-start | bytes 49160 | tf_op jit(solution)/shard_map/ppermute | solution.py:515
  51.5 5.1 %collective-permute-start.11 = (f32[16,256]{1,0:T(8,128)S(1)}, f32[16,256]{1,0:T(8,128)S(1)}, u32[]{:S(2)}, u32[]{:S(2)}) collective-permute-start(f32[16,256]{1,0:T(8,128)S(1)} %get-tuple-element.89.mid), channel_id=1, source_target_pairs={{8,0},{1,8},{9,1},{2,9},{10,2},{3,10},{11,3},{4,11},{12,4},{5,12},... | collective-permute-start | bytes 49160 | tf_op jit(solution)/shard_map/ppermute | solution.py:515
  56.7 35.2 %collective-permute-start.26 = (f32[2,3,2,128,128]{4,3,2,1,0:T(8,128)S(1)}, f32[2,3,2,128,128]{4,3,2,1,0:T(8,128)S(1)}, u32[]{:S(2)}, u32[]{:S(2)}) collective-permute-start(f32[2,3,2,128,128]{4,3,2,1,0:T(8,128)S(1)} %get-tuple-element.109), channel_id=1, source_target_pairs={{80,81},{81,82},{82,83},{83,84},{84,85},{85,86},{86,87},{89,88},{9... | collective-permute-start | bytes 2359304 | tf_op jit(solution)/shard_map/ppermute | solution.py:537
  57.4 34.5 %collective-permute-start.27 = (f32[2,3,2,128,128]{4,3,2,1,0:T(8,128)S(1)}, f32[2,3,2,128,128]{4,3,2,1,0:T(8,128)S(1)}, u32[]{:S(2)}, u32[]{:S(2)}) collective-permute-start(f32[2,3,2,128,128]{4,3,2,1,0:T(8,128)S(1)} %get-tuple-element.110), channel_id=1, source_target_pairs={{81,88},{82,89},{83,90},{84,91},{85,92},{86,93},{87,94},{88,81},{8... | collective-permute-start | bytes 2359304 | tf_op jit(solution)/shard_map/ppermute | solution.py:538
  62.3 26.3 %collective-permute-start.20 = (f32[16,512]{1,0:T(8,128)S(1)}, f32[16,512]{1,0:T(8,128)S(1)}, u32[]{:S(2)}, u32[]{:S(2)}) collective-permute-start(f32[16,512]{1,0:T(8,128)S(1)} %get-tuple-element.102), channel_id=1, source_target_pairs={{0,24},{8,17},{1,25},{9,18},{2,26},{10,19},{3,27},{11,20},{4,28},{... | collective-permute-start | bytes 98312 | tf_op jit(solution)/shard_map/ppermute | solution.py:515
  93.5 56.0 %collective-permute-start.42 = (f32[2,3,2,128,128]{4,3,2,1,0:T(8,128)S(1)}, f32[2,3,2,128,128]{4,3,2,1,0:T(8,128)S(1)}, u32[]{:S(2)}, u32[]{:S(2)}) collective-permute-start(f32[2,3,2,128,128]{4,3,2,1,0:T(8,128)S(1)} %get-tuple-element.127), channel_id=1, source_target_pairs={{0,1},{1,2},{2,3},{3,4},{4,5},{5,6},{6,7},{9,8},{10,9},{11,10},{12... | collective-permute-start | bytes 2359304 | tf_op jit(solution)/shard_map/ppermute | solution.py:537
  94.8 54.8 %collective-permute-start.43 = (f32[2,3,2,128,128]{4,3,2,1,0:T(8,128)S(1)}, f32[2,3,2,128,128]{4,3,2,1,0:T(8,128)S(1)}, u32[]{:S(2)}, u32[]{:S(2)}) collective-permute-start(f32[2,3,2,128,128]{4,3,2,1,0:T(8,128)S(1)} %get-tuple-element.128), channel_id=1, source_target_pairs={{1,8},{2,9},{3,10},{4,11},{5,12},{6,13},{7,14},{8,1},{9,2},{10,3},... | collective-permute-start | bytes 2359304 | tf_op jit(solution)/shard_map/ppermute | solution.py:538
  101.5 12.0 %collective-permute-start.31 = (f32[16,512]{1,0:T(8,128)S(1)}, f32[16,512]{1,0:T(8,128)S(1)}, u32[]{:S(2)}, u32[]{:S(2)}) collective-permute-start(f32[16,512]{1,0:T(8,128)S(1)} %get-tuple-element.114), channel_id=1, source_target_pairs={{0,24},{8,17},{1,25},{9,18},{2,26},{10,19},{3,27},{11,20},{4,28},{... | collective-permute-start | bytes 98312 | tf_op jit(solution)/shard_map/ppermute | solution.py:515
  110.7 2.9 %collective-permute-start.32 = (f32[16,512]{1,0:T(8,128)S(1)}, f32[16,512]{1,0:T(8,128)S(1)}, u32[]{:S(2)}, u32[]{:S(2)}) collective-permute-start(f32[16,512]{1,0:T(8,128)S(1)} %get-tuple-element.114), channel_id=1, source_target_pairs={{0,16},{8,24},{1,17},{9,25},{2,18},{10,26},{3,19},{11,27},{4,20},{... | collective-permute-start | bytes 98312 | tf_op jit(solution)/shard_map/ppermute | solution.py:515
  115.2 19.1 %collective-permute-start.34 = (f32[2,16,512]{2,1,0:T(8,128)S(1)}, f32[2,16,512]{2,1,0:T(8,128)S(1)}, u32[]{:S(2)}, u32[]{:S(2)}) collective-permute-start(f32[2,16,512]{2,1,0:T(8,128)S(1)} %slice.3), channel_id=1, source_target_pairs={{0,8},{8,1},{1,9},{9,2},{2,10},{10,3},{3,11},{11,4},{4,12},{12,5},... | collective-permute-start | bytes 196616 | tf_op jit(solution)/shard_map/ppermute | solution.py:515
  119.1 15.2 %collective-permute-start.35 = (f32[2,16,512]{2,1,0:T(8,128)S(1)}, f32[2,16,512]{2,1,0:T(8,128)S(1)}, u32[]{:S(2)}, u32[]{:S(2)}) collective-permute-start(f32[2,16,512]{2,1,0:T(8,128)S(1)} %slice.3), channel_id=1, source_target_pairs={{8,0},{1,8},{9,1},{2,9},{10,2},{3,10},{11,3},{4,11},{12,4},{5,12},... | collective-permute-start | bytes 196616 | tf_op jit(solution)/shard_map/ppermute | solution.py:515
  134.3 5.2 %collective-permute-start.36 = (f32[16,512]{1,0:T(8,128)S(1)}, f32[16,512]{1,0:T(8,128)S(1)}, u32[]{:S(2)}, u32[]{:S(2)}) collective-permute-start(f32[16,512]{1,0:T(8,128)S(1)} %get-tuple-element.117), channel_id=1, source_target_pairs={{16,8},{24,1},{17,9},{25,2},{18,10},{26,3},{19,11},{27,4},{20,12},... | collective-permute-start | bytes 98312 | tf_op jit(solution)/shard_map/ppermute | solution.py:515
  135.6 8.0 %collective-permute-start.37 = (f32[16,512]{1,0:T(8,128)S(1)}, f32[16,512]{1,0:T(8,128)S(1)}, u32[]{:S(2)}, u32[]{:S(2)}) collective-permute-start(f32[16,512]{1,0:T(8,128)S(1)} %get-tuple-element.117), channel_id=1, source_target_pairs={{16,0},{24,8},{17,1},{25,9},{18,2},{26,10},{19,3},{27,11},{20,4},{... | collective-permute-start | bytes 98312 | tf_op jit(solution)/shard_map/ppermute | solution.py:515
  136.9 10.5 %collective-permute-start.38 = (f32[16,512]{1,0:T(8,128)S(1)}, f32[16,512]{1,0:T(8,128)S(1)}, u32[]{:S(2)}, u32[]{:S(2)}) collective-permute-start(f32[16,512]{1,0:T(8,128)S(1)} %get-tuple-element.117), channel_id=1, source_target_pairs={{24,0},{17,8},{25,1},{18,9},{26,2},{19,10},{27,3},{20,11},{28,4},{... | collective-permute-start | bytes 98312 | tf_op jit(solution)/shard_map/ppermute | solution.py:515
  153.0 33.7 %collective-permute-start.53 = (f32[1,3,2,128,128]{4,3,2,1,0:T(8,128)S(1)}, f32[1,3,2,128,128]{4,3,2,1,0:T(8,128)S(1)}, u32[]{:S(2)}, u32[]{:S(2)}) collective-permute-start(f32[1,3,2,128,128]{4,3,2,1,0:T(8,128)S(1)} %get-tuple-element.139), channel_id=1, source_target_pairs={{0,1},{1,2},{2,3},{3,4},{4,5},{5,6},{6,7},{16,17},{17,18},{18,19},... | collective-permute-start | bytes 1179656 | tf_op jit(solution)/shard_map/ppermute | solution.py:537
  153.7 33.0 %collective-permute-start.54 = (f32[1,3,2,128,128]{4,3,2,1,0:T(8,128)S(1)}, f32[1,3,2,128,128]{4,3,2,1,0:T(8,128)S(1)}, u32[]{:S(2)}, u32[]{:S(2)}) collective-permute-start(f32[1,3,2,128,128]{4,3,2,1,0:T(8,128)S(1)} %get-tuple-element.140), channel_id=1, source_target_pairs={{1,8},{2,9},{3,10},{4,11},{5,12},{6,13},{7,14},{17,24},{18,25},{19... | collective-permute-start | bytes 1179656 | tf_op jit(solution)/shard_map/ppermute | solution.py:538
  155.0 25.9 %collective-permute-start.47 = (f32[16,512]{1,0:T(8,128)S(1)}, f32[16,512]{1,0:T(8,128)S(1)}, u32[]{:S(2)}, u32[]{:S(2)}) collective-permute-start(f32[16,512]{1,0:T(8,128)S(1)} %get-tuple-element.132), channel_id=1, source_target_pairs={{16,8},{24,1},{17,9},{25,2},{18,10},{26,3},{19,11},{27,4},{20,12},... | collective-permute-start | bytes 98312 | tf_op jit(solution)/shard_map/ppermute | solution.py:515
  156.3 24.6 %collective-permute-start.48 = (f32[16,512]{1,0:T(8,128)S(1)}, f32[16,512]{1,0:T(8,128)S(1)}, u32[]{:S(2)}, u32[]{:S(2)}) collective-permute-start(f32[16,512]{1,0:T(8,128)S(1)} %get-tuple-element.132), channel_id=1, source_target_pairs={{16,0},{24,8},{17,1},{25,9},{18,2},{26,10},{19,3},{27,11},{20,4},{... | collective-permute-start | bytes 98312 | tf_op jit(solution)/shard_map/ppermute | solution.py:515
  157.6 27.0 %collective-permute-start.49 = (f32[16,512]{1,0:T(8,128)S(1)}, f32[16,512]{1,0:T(8,128)S(1)}, u32[]{:S(2)}, u32[]{:S(2)}) collective-permute-start(f32[16,512]{1,0:T(8,128)S(1)} %get-tuple-element.132), channel_id=1, source_target_pairs={{24,0},{17,8},{25,1},{18,9},{26,2},{19,10},{27,3},{20,11},{28,4},{... | collective-permute-start | bytes 98312 | tf_op jit(solution)/shard_map/ppermute | solution.py:515
  189.1 13.3 %collective-permute-start.58 = (f32[16,512]{1,0:T(8,128)S(1)}, f32[16,512]{1,0:T(8,128)S(1)}, u32[]{:S(2)}, u32[]{:S(2)}) collective-permute-start(f32[16,512]{1,0:T(8,128)S(1)} %get-tuple-element.144), channel_id=1, source_target_pairs={{16,8},{24,1},{17,9},{25,2},{18,10},{26,3},{19,11},{27,4},{20,12},... | collective-permute-start | bytes 98312 | tf_op jit(solution)/shard_map/ppermute | solution.py:515
  190.4 13.7 %collective-permute-start.59 = (f32[16,512]{1,0:T(8,128)S(1)}, f32[16,512]{1,0:T(8,128)S(1)}, u32[]{:S(2)}, u32[]{:S(2)}) collective-permute-start(f32[16,512]{1,0:T(8,128)S(1)} %get-tuple-element.144), channel_id=1, source_target_pairs={{16,0},{24,8},{17,1},{25,9},{18,2},{26,10},{19,3},{27,11},{20,4},{... | collective-permute-start | bytes 98312 | tf_op jit(solution)/shard_map/ppermute | solution.py:515
  191.7 15.4 %collective-permute-start.60 = (f32[16,512]{1,0:T(8,128)S(1)}, f32[16,512]{1,0:T(8,128)S(1)}, u32[]{:S(2)}, u32[]{:S(2)}) collective-permute-start(f32[16,512]{1,0:T(8,128)S(1)} %get-tuple-element.144), channel_id=1, source_target_pairs={{24,0},{17,8},{25,1},{18,9},{26,2},{19,10},{27,3},{20,11},{28,4},{... | collective-permute-start | bytes 98312 | tf_op jit(solution)/shard_map/ppermute | solution.py:515
  (34 other events, 49.3 us)

commit v7 on v6

--- a/solution.py
+++ b/solution.py
@@ -456,7 +456,7 @@
     )(ids, waves, field, taken)
 
 
-PAIR_ROWS = 2
+PAIR_ROWS = 3
 LATE_ROWS = 5
 FIRST_RUNS = (
     (((0, 7, 8),), ((0, 0, 1),)),
@@ -611,7 +611,6 @@
             late_rows = (0, LATE_ROWS)
             packed = pack_halo(gated(ids, out), late_halo, packed, late_rows, EARLY_SLOTS, "halo_late")
             out, packed = lax.optimization_barrier((out, packed))
-        if turn == LATE_ROWS - 1:
             _, last_halo = send_halo(gated(ids, out), factor, last_parts, "cut_last", (0,))
         if turn == PAIR_ROWS:
             last_rows = (0, PAIR_ROWS)

time: 213 us -> 213 us (level)
  waiting for transfers between devices: 76.8 us -> 87.4 us
  starting transfers between devices: 110 us -> 99.7 us
    ppermute x48 -> x50, starting transfers between devices: 89.7 us -> 76.1 us  [hop(): return lax.ppermute(value, AXES, pairs)]
    ppermute x48 -> x50, waiting for transfers between devices: 71.4 us -> 82 us  [hop(): return lax.ppermute(value, AXES, pairs)]
    ppermute x5, starting transfers between devices: 12.6 us -> 15.9 us  [send_halo(): lax.ppermute(cross, AXES, beside_pairs(rows, False, sides))]
  transfers between devices with their start and end apart: 62 -> 64, of which waited for: 16 -> 18; matrix products, arithmetic and copies ran while one was open for 0% -> 0% of each run, Pallas kernels for 6% -> 6%
where the time goes in v7:
time: 213 us; the launch traced here: 212 us
  starting transfers between devices  99.7 us (47%)
  waiting for transfers between devices  87.4 us (41%)
  Pallas kernels  20.1 us (9%)
  local copies, waits for them, and re-layouts  3.01 us (1%)
    ppermute x50, waiting for transfers between devices, hop(): return lax.ppermute(value, AXES, pairs)  82 us
    ppermute x50, starting transfers between devices, hop(): return lax.ppermute(value, AXES, pairs)  76.1 us
    ppermute x5, starting transfers between devices, send_halo(): lax.ppermute(cross, AXES, beside_pairs(rows, False, sides))  15.9 us
    pallas_call x2, Pallas kernels, pack_chip(): pl.pallas_call(functools.partial(chip_body, mine=mine), in_specs=[ANY_SPE...  8.52 us
    ppermute x5, starting transfers between devices, send_halo(): lax.ppermute(straight, AXES, beside_pairs(rows, True, sides))  4.73 us
  transfers between devices with their start and end apart: 64, of which 18 were waited for; matrix products, arithmetic and copies ran while one was open for 0% of the time, Pallas kernels for 6%

profile of v7, /device:TPU:1, one launch (start us, length us, event | category | flops | bytes accessed | tf_op | source)
XLA Modules:
  0.0 212.0 jit_solution(1963969013493118972)
XLA Ops:
  1.9 1.5 collective-permute-start
  4.7 5.2 %collective-permute-start.2 = (f32[1,3,2,128,128]{4,3,2,1,0:T(8,128)S(1)}, f32[1,3,2,128,128]{4,3,2,1,0:T(8,128)S(1)}, u32[]{:S(2)}, u32[]{:S(2)}) collective-permute-start(f32[1,3,2,128,128]{4,3,2,1,0:T(8,128)S(1)} %get-tuple-element.82), channel_id=1, source_target_pairs={{1,8},{2,9},{3,10},{4,11},{5,12},{6,13},{7,14},{8,1},{9,2},{10,3},... | collective-permute-start | bytes 1179656 | tf_op jit(solution)/shard_map/ppermute | solution.py:538
  13.5 4.6 %pack_mine.1.refs_0_ = bf16[4,10,384,512]{3,2,1,0:T(8,128)(2,1)S(1)} custom-call(s32[4]{0:T(128)S(1)} %pad_add_fusion.ids, f32[2,8,3,2,128,128]{5,4,3,2,1,0:T(8,128)} %other.5), custom_call_target="tpu_custom_call" | custom-call | flops 1 | bytes 1 | tf_op jit(solution)/shard_map/pack_mine/pallas_call | solution.py:134
  19.6 3.9 %pack_partner.1.refs_0_ = bf16[4,10,384,512]{3,2,1,0:T(8,128)(2,1)S(1)} custom-call(s32[4]{0:T(128)S(1)} %pad_add_fusion.ids, f32[2,8,3,2,128,128]{5,4,3,2,1,0:T(8,128)S(1)} %collective-permute-done.source.other, bf16[4,10,384,512]{3,2,1,0:T(8,128)(2,1)S(1)} %pack_mine.1.refs_0_), custom_call_target="tpu_custom_call", output_to_operand_aliasing={{}: (2, {})} | custom-call | flops 1 | bytes 1 | tf_op jit(solution)/shard_map/pack_partner/pallas_call | solution.py:134
  23.5 4.0 %collective-permute-done.2.cross = f32[1,3,2,128,128]{4,3,2,1,0:T(8,128)S(1)} collective-permute-done((f32[1,3,2,128,128]{4,3,2,1,0:T(8,128)S(1)}, f32[1,3,2,128,128]{4,3,2,1,0:T(8,128)S(1)}, u32[]{:S(2)}, u32[]{:S(2)}) %collective-permute-start.2) | collective-permute-done | bytes 393248 | tf_op jit(solution)/shard_map/ppermute | solution.py:538
  30.5 5.9 %collective-permute-start.5 = (f32[16,256]{1,0:T(8,128)S(1)}, f32[16,256]{1,0:T(8,128)S(1)}, u32[]{:S(2)}, u32[]{:S(2)}) collective-permute-start(f32[16,256]{1,0:T(8,128)S(1)} %get-tuple-element.86), channel_id=1, source_target_pairs={{0,8},{8,1},{1,9},{9,2},{2,10},{10,3},{3,11},{11,4},{4,12},{12,5},... | collective-permute-start | bytes 49160 | tf_op jit(solution)/shard_map/ppermute | solution.py:515
  36.4 1.9 collective-permute-start.6
  38.4 3.1 %collective-permute-done.6.high = f32[16,256]{1,0:T(8,128)S(1)} collective-permute-done((f32[16,256]{1,0:T(8,128)S(1)}, f32[16,256]{1,0:T(8,128)S(1)}, u32[]{:S(2)}, u32[]{:S(2)}) %collective-permute-start.6) | collective-permute-done | bytes 16416 | tf_op jit(solution)/shard_map/ppermute | solution.py:515
  42.2 1.5 collective-permute-start.7
  43.7 1.6 collective-permute-start.8
  47.6 3.9 %collective-permute-start.10 = (f32[16,256]{1,0:T(8,128)S(1)}, f32[16,256]{1,0:T(8,128)S(1)}, u32[]{:S(2)}, u32[]{:S(2)}) collective-permute-start(f32[16,256]{1,0:T(8,128)S(1)} %get-tuple-element.91), channel_id=1, source_target_pairs={{0,8},{8,1},{1,9},{9,2},{2,10},{10,3},{3,11},{11,4},{4,12},{12,5},... | collective-permute-start | bytes 49160 | tf_op jit(solution)/shard_map/ppermute | solution.py:515
  51.5 1.9 collective-permute-start.11
  53.5 3.1 %collective-permute-done.11.high = f32[16,256]{1,0:T(8,128)S(1)} collective-permute-done((f32[16,256]{1,0:T(8,128)S(1)}, f32[16,256]{1,0:T(8,128)S(1)}, u32[]{:S(2)}, u32[]{:S(2)}) %collective-permute-start.11) | collective-permute-done | bytes 16416 | tf_op jit(solution)/shard_map/ppermute | solution.py:515
  58.6 1.9 collective-permute-start.15
  60.6 2.4 %collective-permute-start.16 = (f32[16,256]{1,0:T(8,128)S(1)}, f32[16,256]{1,0:T(8,128)S(1)}, u32[]{:S(2)}, u32[]{:S(2)}) collective-permute-start(f32[16,256]{1,0:T(8,128)S(1)} %get-tuple-element.97.mid), channel_id=1, source_target_pairs={{8,0},{1,8},{9,1},{2,9},{10,2},{3,10},{11,3},{4,11},{12,4},{5,12},... | collective-permute-start | bytes 49160 | tf_op jit(solution)/shard_map/ppermute | solution.py:515
  63.0 4.2 %collective-permute-done.16.high = f32[16,256]{1,0:T(8,128)S(1)} collective-permute-done((f32[16,256]{1,0:T(8,128)S(1)}, f32[16,256]{1,0:T(8,128)S(1)}, u32[]{:S(2)}, u32[]{:S(2)}) %collective-permute-start.16) | collective-permute-done | bytes 16416 | tf_op jit(solution)/shard_map/ppermute | solution.py:515
  70.8 7.1 %collective-permute-start.22 = (f32[16,512]{1,0:T(8,128)S(1)}, f32[16,512]{1,0:T(8,128)S(1)}, u32[]{:S(2)}, u32[]{:S(2)}) collective-permute-start(f32[16,512]{1,0:T(8,128)S(1)} %get-tuple-element.108), channel_id=1, source_target_pairs={{0,24},{8,17},{1,25},{9,18},{2,26},{10,19},{3,27},{11,20},{4,28},{... | collective-permute-start | bytes 98312 | tf_op jit(solution)/shard_map/ppermute | solution.py:515
  77.9 1.6 collective-permute-start.23
  86.9 8.0 %collective-permute-start.45 = (f32[2,3,2,128,128]{4,3,2,1,0:T(8,128)S(1)}, f32[2,3,2,128,128]{4,3,2,1,0:T(8,128)S(1)}, u32[]{:S(2)}, u32[]{:S(2)}) collective-permute-start(f32[2,3,2,128,128]{4,3,2,1,0:T(8,128)S(1)} %get-tuple-element.134), channel_id=1, source_target_pairs={{1,8},{2,9},{3,10},{4,11},{5,12},{6,13},{7,14},{8,1},{9,2},{10,3},... | collective-permute-start | bytes 2359304 | tf_op jit(solution)/shard_map/ppermute | solution.py:538
  97.0 7.6 %collective-permute-start.33 = (f32[16,512]{1,0:T(8,128)S(1)}, f32[16,512]{1,0:T(8,128)S(1)}, u32[]{:S(2)}, u32[]{:S(2)}) collective-permute-start(f32[16,512]{1,0:T(8,128)S(1)} %get-tuple-element.120), channel_id=1, source_target_pairs={{0,24},{8,17},{1,25},{9,18},{2,26},{10,19},{3,27},{11,20},{4,28},{... | collective-permute-start | bytes 98312 | tf_op jit(solution)/shard_map/ppermute | solution.py:515
  104.5 1.6 collective-permute-start.34
  109.0 3.9 %collective-permute-start.36 = (f32[2,16,512]{2,1,0:T(8,128)S(1)}, f32[2,16,512]{2,1,0:T(8,128)S(1)}, u32[]{:S(2)}, u32[]{:S(2)}) collective-permute-start(f32[2,16,512]{2,1,0:T(8,128)S(1)} %slice.3), channel_id=1, source_target_pairs={{0,8},{8,1},{1,9},{9,2},{2,10},{10,3},{3,11},{11,4},{4,12},{12,5},... | collective-permute-start | bytes 196616 | tf_op jit(solution)/shard_map/ppermute | solution.py:515
  113.0 1.9 collective-permute-start.37
  114.9 13.3 %collective-permute-done.36.left = f32[2,16,512]{2,1,0:T(8,128)S(1)} collective-permute-done((f32[2,16,512]{2,1,0:T(8,128)S(1)}, f32[2,16,512]{2,1,0:T(8,128)S(1)}, u32[]{:S(2)}, u32[]{:S(2)}) %collective-permute-start.36) | collective-permute-done | bytes 65568 | tf_op jit(solution)/shard_map/ppermute | solution.py:515
  133.5 4.6 %collective-permute-done.39.mid = f32[16,512]{1,0:T(8,128)S(1)} collective-permute-done((f32[16,512]{1,0:T(8,128)S(1)}, f32[16,512]{1,0:T(8,128)S(1)}, u32[]{:S(2)}, u32[]{:S(2)}) %collective-permute-start.39) | collective-permute-done | bytes 32800 | tf_op jit(solution)/shard_map/ppermute | solution.py:515
  138.0 3.5 %collective-permute-done.40.high = f32[16,512]{1,0:T(8,128)S(1)} collective-permute-done((f32[16,512]{1,0:T(8,128)S(1)}, f32[16,512]{1,0:T(8,128)S(1)}, u32[]{:S(2)}, u32[]{:S(2)}) %collective-permute-start.40) | collective-permute-done | bytes 32800 | tf_op jit(solution)/shard_map/ppermute | solution.py:515
  153.1 19.8 %collective-permute-done.49.low = f32[16,512]{1,0:T(8,128)S(1)} collective-permute-done((f32[16,512]{1,0:T(8,128)S(1)}, f32[16,512]{1,0:T(8,128)S(1)}, u32[]{:S(2)}, u32[]{:S(2)}) %collective-permute-start.49) | collective-permute-done | bytes 32800 | tf_op jit(solution)/shard_map/ppermute | solution.py:515
  172.9 4.9 %collective-permute-done.50.mid = f32[16,512]{1,0:T(8,128)S(1)} collective-permute-done((f32[16,512]{1,0:T(8,128)S(1)}, f32[16,512]{1,0:T(8,128)S(1)}, u32[]{:S(2)}, u32[]{:S(2)}) %collective-permute-start.50) | collective-permute-done | bytes 32800 | tf_op jit(solution)/shard_map/ppermute | solution.py:515
  187.2 15.4 %collective-permute-done.60.low = f32[16,512]{1,0:T(8,128)S(1)} collective-permute-done((f32[16,512]{1,0:T(8,128)S(1)}, f32[16,512]{1,0:T(8,128)S(1)}, u32[]{:S(2)}, u32[]{:S(2)}) %collective-permute-start.60) | collective-permute-done | bytes 32800 | tf_op jit(solution)/shard_map/ppermute | solution.py:515
  202.6 1.8 collective-permute-done.61.mid
  204.4 2.9 %collective-permute-done.62.high = f32[16,512]{1,0:T(8,128)S(1)} collective-permute-done((f32[16,512]{1,0:T(8,128)S(1)}, f32[16,512]{1,0:T(8,128)S(1)}, u32[]{:S(2)}, u32[]{:S(2)}) %collective-permute-start.62) | collective-permute-done | bytes 32800 | tf_op jit(solution)/shard_map/ppermute | solution.py:515
  207.4 2.5 %up_0.1 = (f32[16,512]{1,0:T(8,128)}, f32[4,16,512]{2,1,0:T(8,128)S(1)}) custom-call(f32[16,512]{1,0:T(8,128)S(1)} %collective-permute-done.60.low, f32[16,512]{1,0:T(8,128)S(1)} %collective-permute-done.61.mid, f32[16,512]{1,0:T(8,128)S(1)} %collective-permute-done.62.high, f32[4,20,1536]{2,1,0:T(8,128)S(1)} %window.1, ...), custom_call_target="tpu_custom_call", output_to_operand_aliasing={{1}: (8, {})} | custom-call | flops 1 | bytes 1 | tf_op jit(solution)/shard_map/up_0/pallas_call | solution.py:403
  (146 shorter events, 59.3 us)
Async XLA Ops:
  1.9 17.7 %collective-permute-start = (f32[2,8,3,2,128,128]{5,4,3,2,1,0:T(8,128)}, f32[2,8,3,2,128,128]{5,4,3,2,1,0:T(8,128)S(1)}, u32[]{:S(2)}, u32[]{:S(2)}) collective-permute-start(f32[2,8,3,2,128,128]{5,4,3,2,1,0:T(8,128)} %other.5), channel_id=1, source_target_pairs={{0,8},{1,9},{2,10},{3,11},{4,12},{5,13},{6,14},{7,15},{8,0},{9,1},... | collective-permute-start | bytes 18874376 | tf_op jit(solution)/shard_map/ppermute | solution.py:546
  3.4 20.1 %collective-permute-start.1 = (f32[1,3,2,128,128]{4,3,2,1,0:T(8,128)S(1)}, f32[1,3,2,128,128]{4,3,2,1,0:T(8,128)S(1)}, u32[]{:S(2)}, u32[]{:S(2)}) collective-permute-start(f32[1,3,2,128,128]{4,3,2,1,0:T(8,128)S(1)} %get-tuple-element.78), channel_id=1, source_target_pairs={{0,1},{1,2},{2,3},{3,4},{4,5},{5,6},{6,7},{9,8},{10,9},{11,10},{12... | collective-permute-start | bytes 1179656 | tf_op jit(solution)/shard_map/ppermute | solution.py:537
  4.7 22.8 %collective-permute-start.2 = (f32[1,3,2,128,128]{4,3,2,1,0:T(8,128)S(1)}, f32[1,3,2,128,128]{4,3,2,1,0:T(8,128)S(1)}, u32[]{:S(2)}, u32[]{:S(2)}) collective-permute-start(f32[1,3,2,128,128]{4,3,2,1,0:T(8,128)S(1)} %get-tuple-element.82), channel_id=1, source_target_pairs={{1,8},{2,9},{3,10},{4,11},{5,12},{6,13},{7,14},{8,1},{9,2},{10,3},... | collective-permute-start | bytes 1179656 | tf_op jit(solution)/shard_map/ppermute | solution.py:538
  13.4 4.7 %collective-permute-start.3 = (f32[2,20,1024]{2,1,0:T(8,128)S(1)}, f32[2,20,1024]{2,1,0:T(8,128)S(1)}, u32[]{:S(2)}, u32[]{:S(2)}) collective-permute-start(f32[2,20,1024]{2,1,0:T(8,128)S(1)} %rows.1), channel_id=1, source_target_pairs={{0,8},{1,9},{2,10},{3,11},{4,12},{5,13},{6,14},{7,15},{8,0},{9,1},... | collective-permute-start | bytes 491528 | tf_op jit(solution)/shard_map/ppermute | solution.py:555
  18.2 9.3 %collective-permute-start.4 = (f32[4,20,512]{2,1,0:T(8,128)S(1)}, f32[4,20,512]{2,1,0:T(8,128)S(1)}, u32[]{:S(2)}, u32[]{:S(2)}) collective-permute-start(f32[4,20,512]{2,1,0:T(8,128)S(1)} %edge.1), channel_id=1, source_target_pairs={{0,1},{1,2},{2,3},{3,4},{4,5},{5,6},{6,7},{9,8},{10,9},{11,10},{12... | collective-permute-start | bytes 491528 | tf_op jit(solution)/shard_map/ppermute | solution.py:561
  27.6 39.6 %collective-permute-start.17 = (f32[4,3,2,128,128]{4,3,2,1,0:T(8,128)S(1)}, f32[4,3,2,128,128]{4,3,2,1,0:T(8,128)S(1)}, u32[]{:S(2)}, u32[]{:S(2)}) collective-permute-start(f32[4,3,2,128,128]{4,3,2,1,0:T(8,128)S(1)} %get-tuple-element.103), channel_id=1, source_target_pairs={{48,49},{49,50},{50,51},{51,52},{52,53},{53,54},{54,55},{64,65},{6... | collective-permute-start | bytes 4718600 | tf_op jit(solution)/shard_map/ppermute | solution.py:537
  28.4 38.8 %collective-permute-start.18 = (f32[4,3,2,128,128]{4,3,2,1,0:T(8,128)S(1)}, f32[4,3,2,128,128]{4,3,2,1,0:T(8,128)S(1)}, u32[]{:S(2)}, u32[]{:S(2)}) collective-permute-start(f32[4,3,2,128,128]{4,3,2,1,0:T(8,128)S(1)} %get-tuple-element.104), channel_id=1, source_target_pairs={{49,56},{50,57},{51,58},{52,59},{53,60},{54,61},{55,62},{65,72},{6... | collective-permute-start | bytes 4718600 | tf_op jit(solution)/shard_map/ppermute | solution.py:538
  30.5 7.9 %collective-permute-start.5 = (f32[16,256]{1,0:T(8,128)S(1)}, f32[16,256]{1,0:T(8,128)S(1)}, u32[]{:S(2)}, u32[]{:S(2)}) collective-permute-start(f32[16,256]{1,0:T(8,128)S(1)} %get-tuple-element.86), channel_id=1, source_target_pairs={{0,8},{8,1},{1,9},{9,2},{2,10},{10,3},{3,11},{11,4},{4,12},{12,5},... | collective-permute-start | bytes 49160 | tf_op jit(solution)/shard_map/ppermute | solution.py:515
  36.4 5.1 %collective-permute-start.6 = (f32[16,256]{1,0:T(8,128)S(1)}, f32[16,256]{1,0:T(8,128)S(1)}, u32[]{:S(2)}, u32[]{:S(2)}) collective-permute-start(f32[16,256]{1,0:T(8,128)S(1)} %get-tuple-element.87.mid), channel_id=1, source_target_pairs={{8,0},{1,8},{9,1},{2,9},{10,2},{3,10},{11,3},{4,11},{12,4},{5,12},... | collective-permute-start | bytes 49160 | tf_op jit(solution)/shard_map/ppermute | solution.py:515
  42.2 4.4 %collective-permute-start.7 = (f32[16,512]{1,0:T(8,128)S(1)}, f32[16,512]{1,0:T(8,128)S(1)}, u32[]{:S(2)}, u32[]{:S(2)}) collective-permute-start(f32[16,512]{1,0:T(8,128)S(1)} %get-tuple-element.89), channel_id=1, source_target_pairs={{0,24},{8,17},{1,25},{9,18},{2,26},{10,19},{3,27},{11,20},{4,28},{... | collective-permute-start | bytes 98312 | tf_op jit(solution)/shard_map/ppermute | solution.py:515
  47.6 5.9 %collective-permute-start.10 = (f32[16,256]{1,0:T(8,128)S(1)}, f32[16,256]{1,0:T(8,128)S(1)}, u32[]{:S(2)}, u32[]{:S(2)}) collective-permute-start(f32[16,256]{1,0:T(8,128)S(1)} %get-tuple-element.91), channel_id=1, source_target_pairs={{0,8},{8,1},{1,9},{9,2},{2,10},{10,3},{3,11},{11,4},{4,12},{12,5},... | collective-permute-start | bytes 49160 | tf_op jit(solution)/shard_map/ppermute | solution.py:515
  51.5 5.1 %collective-permute-start.11 = (f32[16,256]{1,0:T(8,128)S(1)}, f32[16,256]{1,0:T(8,128)S(1)}, u32[]{:S(2)}, u32[]{:S(2)}) collective-permute-start(f32[16,256]{1,0:T(8,128)S(1)} %get-tuple-element.92.mid), channel_id=1, source_target_pairs={{8,0},{1,8},{9,1},{2,9},{10,2},{3,10},{11,3},{4,11},{12,4},{5,12},... | collective-permute-start | bytes 49160 | tf_op jit(solution)/shard_map/ppermute | solution.py:515
  60.6 6.6 %collective-permute-start.16 = (f32[16,256]{1,0:T(8,128)S(1)}, f32[16,256]{1,0:T(8,128)S(1)}, u32[]{:S(2)}, u32[]{:S(2)}) collective-permute-start(f32[16,256]{1,0:T(8,128)S(1)} %get-tuple-element.97.mid), channel_id=1, source_target_pairs={{8,0},{1,8},{9,1},{2,9},{10,2},{3,10},{11,3},{4,11},{12,4},{5,12},... | collective-permute-start | bytes 49160 | tf_op jit(solution)/shard_map/ppermute | solution.py:515
  67.3 16.8 %collective-permute-start.28 = (f32[2,3,2,128,128]{4,3,2,1,0:T(8,128)S(1)}, f32[2,3,2,128,128]{4,3,2,1,0:T(8,128)S(1)}, u32[]{:S(2)}, u32[]{:S(2)}) collective-permute-start(f32[2,3,2,128,128]{4,3,2,1,0:T(8,128)S(1)} %get-tuple-element.115), channel_id=1, source_target_pairs={{80,81},{81,82},{82,83},{83,84},{84,85},{85,86},{86,87},{89,88},{9... | collective-permute-start | bytes 2359304 | tf_op jit(solution)/shard_map/ppermute | solution.py:537
  68.0 16.1 %collective-permute-start.29 = (f32[2,3,2,128,128]{4,3,2,1,0:T(8,128)S(1)}, f32[2,3,2,128,128]{4,3,2,1,0:T(8,128)S(1)}, u32[]{:S(2)}, u32[]{:S(2)}) collective-permute-start(f32[2,3,2,128,128]{4,3,2,1,0:T(8,128)S(1)} %get-tuple-element.116), channel_id=1, source_target_pairs={{81,88},{82,89},{83,90},{84,91},{85,92},{86,93},{87,94},{88,81},{8... | collective-permute-start | bytes 2359304 | tf_op jit(solution)/shard_map/ppermute | solution.py:538
  70.8 10.0 %collective-permute-start.22 = (f32[16,512]{1,0:T(8,128)S(1)}, f32[16,512]{1,0:T(8,128)S(1)}, u32[]{:S(2)}, u32[]{:S(2)}) collective-permute-start(f32[16,512]{1,0:T(8,128)S(1)} %get-tuple-element.108), channel_id=1, source_target_pairs={{0,24},{8,17},{1,25},{9,18},{2,26},{10,19},{3,27},{11,20},{4,28},{... | collective-permute-start | bytes 98312 | tf_op jit(solution)/shard_map/ppermute | solution.py:515
  85.6 58.1 %collective-permute-start.44 = (f32[2,3,2,128,128]{4,3,2,1,0:T(8,128)S(1)}, f32[2,3,2,128,128]{4,3,2,1,0:T(8,128)S(1)}, u32[]{:S(2)}, u32[]{:S(2)}) collective-permute-start(f32[2,3,2,128,128]{4,3,2,1,0:T(8,128)S(1)} %get-tuple-element.133), channel_id=1, source_target_pairs={{0,1},{1,2},{2,3},{3,4},{4,5},{5,6},{6,7},{9,8},{10,9},{11,10},{12... | collective-permute-start | bytes 2359304 | tf_op jit(solution)/shard_map/ppermute | solution.py:537
  86.9 56.8 %collective-permute-start.45 = (f32[2,3,2,128,128]{4,3,2,1,0:T(8,128)S(1)}, f32[2,3,2,128,128]{4,3,2,1,0:T(8,128)S(1)}, u32[]{:S(2)}, u32[]{:S(2)}) collective-permute-start(f32[2,3,2,128,128]{4,3,2,1,0:T(8,128)S(1)} %get-tuple-element.134), channel_id=1, source_target_pairs={{1,8},{2,9},{3,10},{4,11},{5,12},{6,13},{7,14},{8,1},{9,2},{10,3},... | collective-permute-start | bytes 2359304 | tf_op jit(solution)/shard_map/ppermute | solution.py:538
  97.0 10.5 %collective-permute-start.33 = (f32[16,512]{1,0:T(8,128)S(1)}, f32[16,512]{1,0:T(8,128)S(1)}, u32[]{:S(2)}, u32[]{:S(2)}) collective-permute-start(f32[16,512]{1,0:T(8,128)S(1)} %get-tuple-element.120), channel_id=1, source_target_pairs={{0,24},{8,17},{1,25},{9,18},{2,26},{10,19},{3,27},{11,20},{4,28},{... | collective-permute-start | bytes 98312 | tf_op jit(solution)/shard_map/ppermute | solution.py:515
  109.0 19.1 %collective-permute-start.36 = (f32[2,16,512]{2,1,0:T(8,128)S(1)}, f32[2,16,512]{2,1,0:T(8,128)S(1)}, u32[]{:S(2)}, u32[]{:S(2)}) collective-permute-start(f32[2,16,512]{2,1,0:T(8,128)S(1)} %slice.3), channel_id=1, source_target_pairs={{0,8},{8,1},{1,9},{9,2},{2,10},{10,3},{3,11},{11,4},{4,12},{12,5},... | collective-permute-start | bytes 196616 | tf_op jit(solution)/shard_map/ppermute | solution.py:515
  113.0 15.2 %collective-permute-start.37 = (f32[2,16,512]{2,1,0:T(8,128)S(1)}, f32[2,16,512]{2,1,0:T(8,128)S(1)}, u32[]{:S(2)}, u32[]{:S(2)}) collective-permute-start(f32[2,16,512]{2,1,0:T(8,128)S(1)} %slice.3), channel_id=1, source_target_pairs={{8,0},{1,8},{9,1},{2,9},{10,2},{3,10},{11,3},{4,11},{12,4},{5,12},... | collective-permute-start | bytes 196616 | tf_op jit(solution)/shard_map/ppermute | solution.py:515
  128.2 5.2 %collective-permute-start.38 = (f32[16,512]{1,0:T(8,128)S(1)}, f32[16,512]{1,0:T(8,128)S(1)}, u32[]{:S(2)}, u32[]{:S(2)}) collective-permute-start(f32[16,512]{1,0:T(8,128)S(1)} %get-tuple-element.123), channel_id=1, source_target_pairs={{16,8},{24,1},{17,9},{25,2},{18,10},{26,3},{19,11},{27,4},{20,12},... | collective-permute-start | bytes 98312 | tf_op jit(solution)/shard_map/ppermute | solution.py:515
  129.5 8.5 %collective-permute-start.39 = (f32[16,512]{1,0:T(8,128)S(1)}, f32[16,512]{1,0:T(8,128)S(1)}, u32[]{:S(2)}, u32[]{:S(2)}) collective-permute-start(f32[16,512]{1,0:T(8,128)S(1)} %get-tuple-element.123), channel_id=1, source_target_pairs={{16,0},{24,8},{17,1},{25,9},{18,2},{26,10},{19,3},{27,11},{20,4},{... | collective-permute-start | bytes 98312 | tf_op jit(solution)/shard_map/ppermute | solution.py:515
  130.8 10.7 %collective-permute-start.40 = (f32[16,512]{1,0:T(8,128)S(1)}, f32[16,512]{1,0:T(8,128)S(1)}, u32[]{:S(2)}, u32[]{:S(2)}) collective-permute-start(f32[16,512]{1,0:T(8,128)S(1)} %get-tuple-element.123), channel_id=1, source_target_pairs={{24,0},{17,8},{25,1},{18,9},{26,2},{19,10},{27,3},{20,11},{28,4},{... | collective-permute-start | bytes 98312 | tf_op jit(solution)/shard_map/ppermute | solution.py:515
  144.9 33.9 %collective-permute-start.52 = (f32[1,3,2,128,128]{4,3,2,1,0:T(8,128)S(1)}, f32[1,3,2,128,128]{4,3,2,1,0:T(8,128)S(1)}, u32[]{:S(2)}, u32[]{:S(2)}) collective-permute-start(f32[1,3,2,128,128]{4,3,2,1,0:T(8,128)S(1)} %get-tuple-element.143), channel_id=1, source_target_pairs={{0,1},{1,2},{2,3},{3,4},{4,5},{5,6},{6,7},{16,17},{17,18},{18,19},... | collective-permute-start | bytes 1179656 | tf_op jit(solution)/shard_map/ppermute | solution.py:537
  145.6 33.2 %collective-permute-start.53 = (f32[1,3,2,128,128]{4,3,2,1,0:T(8,128)S(1)}, f32[1,3,2,128,128]{4,3,2,1,0:T(8,128)S(1)}, u32[]{:S(2)}, u32[]{:S(2)}) collective-permute-start(f32[1,3,2,128,128]{4,3,2,1,0:T(8,128)S(1)} %get-tuple-element.144), channel_id=1, source_target_pairs={{1,8},{2,9},{3,10},{4,11},{5,12},{6,13},{7,14},{17,24},{18,25},{19... | collective-permute-start | bytes 1179656 | tf_op jit(solution)/shard_map/ppermute | solution.py:538
  149.2 23.7 %collective-permute-start.49 = (f32[16,512]{1,0:T(8,128)S(1)}, f32[16,512]{1,0:T(8,128)S(1)}, u32[]{:S(2)}, u32[]{:S(2)}) collective-permute-start(f32[16,512]{1,0:T(8,128)S(1)} %get-tuple-element.138), channel_id=1, source_target_pairs={{16,8},{24,1},{17,9},{25,2},{18,10},{26,3},{19,11},{27,4},{20,12},... | collective-permute-start | bytes 98312 | tf_op jit(solution)/shard_map/ppermute | solution.py:515
  150.5 27.3 %collective-permute-start.50 = (f32[16,512]{1,0:T(8,128)S(1)}, f32[16,512]{1,0:T(8,128)S(1)}, u32[]{:S(2)}, u32[]{:S(2)}) collective-permute-start(f32[16,512]{1,0:T(8,128)S(1)} %get-tuple-element.138), channel_id=1, source_target_pairs={{16,0},{24,8},{17,1},{25,9},{18,2},{26,10},{19,3},{27,11},{20,4},{... | collective-permute-start | bytes 98312 | tf_op jit(solution)/shard_map/ppermute | solution.py:515
  151.8 27.0 %collective-permute-start.51 = (f32[16,512]{1,0:T(8,128)S(1)}, f32[16,512]{1,0:T(8,128)S(1)}, u32[]{:S(2)}, u32[]{:S(2)}) collective-permute-start(f32[16,512]{1,0:T(8,128)S(1)} %get-tuple-element.138), channel_id=1, source_target_pairs={{24,0},{17,8},{25,1},{18,9},{26,2},{19,10},{27,3},{20,11},{28,4},{... | collective-permute-start | bytes 98312 | tf_op jit(solution)/shard_map/ppermute | solution.py:515
  183.3 19.3 %collective-permute-start.60 = (f32[16,512]{1,0:T(8,128)S(1)}, f32[16,512]{1,0:T(8,128)S(1)}, u32[]{:S(2)}, u32[]{:S(2)}) collective-permute-start(f32[16,512]{1,0:T(8,128)S(1)} %get-tuple-element.150), channel_id=1, source_target_pairs={{16,8},{24,1},{17,9},{25,2},{18,10},{26,3},{19,11},{27,4},{20,12},... | collective-permute-start | bytes 98312 | tf_op jit(solution)/shard_map/ppermute | solution.py:515
  184.6 19.9 %collective-permute-start.61 = (f32[16,512]{1,0:T(8,128)S(1)}, f32[16,512]{1,0:T(8,128)S(1)}, u32[]{:S(2)}, u32[]{:S(2)}) collective-permute-start(f32[16,512]{1,0:T(8,128)S(1)} %get-tuple-element.150), channel_id=1, source_target_pairs={{16,0},{24,8},{17,1},{25,9},{18,2},{26,10},{19,3},{27,11},{20,4},{... | collective-permute-start | bytes 98312 | tf_op jit(solution)/shard_map/ppermute | solution.py:515
  185.9 21.5 %collective-permute-start.62 = (f32[16,512]{1,0:T(8,128)S(1)}, f32[16,512]{1,0:T(8,128)S(1)}, u32[]{:S(2)}, u32[]{:S(2)}) collective-permute-start(f32[16,512]{1,0:T(8,128)S(1)} %get-tuple-element.150), channel_id=1, source_target_pairs={{24,0},{17,8},{25,1},{18,9},{26,2},{19,10},{27,3},{20,11},{28,4},{... | collective-permute-start | bytes 98312 | tf_op jit(solution)/shard_map/ppermute | solution.py:515
  (36 other events, 56.8 us)
